TPU v7x, 32 devices: a whole 2x2x4 slice. The times are simulated.
32 devices in a mesh: tp: 4 (over y, x), ep: 8 (over z, core).
Axes of the slice: x: 2, y: 2, z: 4, core: 2. Of those that a mesh axis runs over, the one named last changes fastest.
Arguments:
- tokens: bfloat16 [16, 1024, 1024], P('ep', 'tp'), may hold values from -6 to 6
- cotangent: bfloat16 [16, 1024, 1024], P('ep', 'tp'), may hold values from -6 to 6
- norm_gains: float32 [2, 1024], replicated, may hold values from 0.5 to 1.5
- query_key_value_weight: bfloat16 [1024, 8, 256], P('ep', 'tp'), may hold values from -0.625 to 0.625
- output_weight: bfloat16 [8, 128, 1024], P('tp', None, 'ep'), may hold values from -3 to 3
- w_router: bfloat16 [1024, 32], replicated, may hold values from -0.09375 to 0.09375
- w_gate_up: bfloat16 [32, 1024, 1024], P('ep', 'tp'), may hold values from -0.1875 to 0.1875
- w_down: bfloat16 [32, 512, 1024], P('ep', None, 'tp'), may hold values from -3 to 3
- segment_ids: int32 [16, 1024], P('ep'), may hold values from 0 to 3, never falling along the last dimension, each value on 1 to 512 neighbouring positions
- routes: int32 [16, 4, 256, 8], P('ep', 'tp'), may hold values from 0 to 31, all different within a row; in each aligned block of 256 rows (0 to 255, 256 to 511, ..., all dimensions but the last counted through in order) at most 96 rows name the same one
Outputs:
- output: bfloat16 [16, 1024, 1024], P('ep', 'tp')
- input_grad: float32 [16, 1024, 1024], P('ep', 'tp')
- grad_gains: float32 [2, 1024], P(None, ('tp', 'ep'))
- grad_qkv: float32 [1024, 8, 256], P('ep', 'tp')
- grad_out: float32 [8, 128, 1024], P('tp', None, 'ep')
- grad_router: float32 [1024, 32], P(('tp', 'ep'))
- grad_gate_up: float32 [32, 1024, 1024], P('ep', 'tp')
- grad_down: float32 [32, 512, 1024], P('ep', None, 'tp')
Inputs may be any that keep to these rules, and one draw needn't show every extreme that they name: `routes`: each row names 8 different experts; in each aligned block of 256 rows (one device's tokens of one micro-batch) no expert is named more than 96 times. `segment_ids`: document numbers never fall along a sequence; every one of the 4 documents has 1 to 512 positions, one exactly that many.
All inputs are finite; a program needn't handle non-finite values.
Results may differ from a plain program's by a relative error of at most 0.023.
Values may be sent and summed in bfloat16 or wider, within the bound.
No kernel may reach another device: no remote copies, remote signals or barrier semaphores. Data moves between devices by JAX's collectives and lax.ppermute only.
A program may use at most 136 MiB of HBM per device.

v0:
```python
import jax
import jax.numpy as jnp
from jax import lax
from jax.sharding import PartitionSpec as P

MODEL_WIDTH = 1024
QUERY_HEADS = 16
KEY_HEADS = 8
HEAD_SIZE = 64
FF = 512
EXPERTS = 32
TOP = 8
DOCS = 4
CAP = 96


epsilon = 1e-06
score_scale = 0.015625
residual_scale = 0.22
rope_base = 10000.0
masked_score = -1000000000.0


def positions_of(segment_row):
    onehot = (segment_row[:, None] == jnp.arange(DOCS, dtype=jnp.int32)[None, :]).astype(jnp.int32)
    doc_len = jnp.sum(onehot, axis=0)
    starts = jnp.cumsum(doc_len) - doc_len
    return jnp.arange(segment_row.shape[0], dtype=jnp.int32) - jnp.sum(
        onehot * starts[None, :], axis=1
    )


def rope_tables(positions):
    halves = HEAD_SIZE // 2
    freqs = rope_base ** (-(jnp.arange(halves, dtype=jnp.float32) * 2.0) / HEAD_SIZE)
    angles = positions.astype(jnp.float32)[:, None] * freqs[None, :]
    return (jnp.cos(angles), jnp.sin(angles))


def rotate_pairs(values, cosine_table, sine_table):
    halves = values.shape[-1] // 2
    first = values[..., :halves]
    second = values[..., halves:]
    return jnp.concatenate(
        [first * cosine_table - second * sine_table, second * cosine_table + first * sine_table],
        axis=-1,
    )


def unrotate(grads, cosine_table, sine_table):
    halves = grads.shape[-1] // 2
    first = grads[..., :halves]
    second = grads[..., halves:]
    return jnp.concatenate(
        [first * cosine_table + second * sine_table, second * cosine_table - first * sine_table],
        axis=-1,
    )


def norm_forward(values, gain):
    scale = lax.rsqrt(jnp.mean(values * values, axis=-1, keepdims=True) + epsilon)
    return (scale, (values * scale * gain).astype(jnp.bfloat16))


def norm_backward(values, scale, gain, grad_normed):
    weighted = grad_normed * gain
    inner = jnp.mean(weighted * values, axis=-1, keepdims=True)
    grad_values = scale * weighted - values * scale * scale * scale * inner
    grad_gain = jnp.sum(grad_normed * values * scale, axis=0)
    return (grad_values, grad_gain)


def split_heads(projected, head_group, query_cos, query_sin, key_cos, key_sin):
    sequence_length = projected.shape[0]
    heads = projected.shape[1]
    query_rows = rotate_pairs(
        projected[:, :, : head_group * HEAD_SIZE].reshape(
            sequence_length, heads, head_group, HEAD_SIZE
        ),
        query_cos,
        query_sin,
    ).astype(jnp.bfloat16)
    keys = rotate_pairs(
        projected[:, :, head_group * HEAD_SIZE : (head_group + 1) * HEAD_SIZE], key_cos, key_sin
    ).astype(jnp.bfloat16)
    values = projected[:, :, (head_group + 1) * HEAD_SIZE :].astype(jnp.bfloat16)
    return (query_rows, keys, values)


def masked_scores(query_block, keys, segment_row, start, block):
    scores = (
        jnp.einsum("qhgd,khd->hgqk", query_block, keys, preferred_element_type=jnp.float32)
        * score_scale
    )
    query_index = start + jnp.arange(block, dtype=jnp.int32)
    key_index = jnp.arange(keys.shape[0], dtype=jnp.int32)
    query_segment = lax.dynamic_slice_in_dim(segment_row, start, block)
    allowed = (key_index[None, :] <= query_index[:, None]) & (
        segment_row[None, :] == query_segment[:, None]
    )
    return jnp.where(allowed[None, None], scores, masked_score)


def attention_forward(query_rows, keys, values, segment_row):
    sequence_length = query_rows.shape[0]
    block = min(512, sequence_length)
    count = sequence_length // block

    def one_block(start):
        query_block = lax.dynamic_slice_in_dim(query_rows, start, block, 0)
        scores = masked_scores(query_block, keys, segment_row, start, block)
        highest_precision = jnp.max(scores, axis=-1, keepdims=True)
        expo = jnp.exp(scores - highest_precision)
        totals = jnp.sum(expo, axis=-1, keepdims=True)
        probs = (expo / totals).astype(jnp.bfloat16)
        context = jnp.einsum("hgqk,khd->qhgd", probs, values, preferred_element_type=jnp.float32)
        return (context.astype(jnp.bfloat16), (highest_precision + jnp.log(totals))[..., 0])

    starts = jnp.arange(count, dtype=jnp.int32) * block
    context, lse_blocks = lax.map(one_block, starts)
    context = context.reshape(query_rows.shape)
    log_totals = jnp.moveaxis(lse_blocks, 0, 2).reshape(
        lse_blocks.shape[1], lse_blocks.shape[2], sequence_length
    )
    return (context, log_totals)


def attention_backward(query_rows, keys, values, segment_row, log_totals, grad_context):
    sequence_length = query_rows.shape[0]
    block = min(512, sequence_length)
    count = sequence_length // block

    def one_block(carry, start):
        grad_keys, grad_values = carry
        query_block = lax.dynamic_slice_in_dim(query_rows, start, block, 0)
        grad_block = lax.dynamic_slice_in_dim(grad_context, start, block, 0)
        totals = lax.dynamic_slice_in_dim(log_totals, start, block, 2)
        scores = masked_scores(query_block, keys, segment_row, start, block)
        probs = jnp.exp(scores - totals[..., None])
        grad_probs = jnp.einsum(
            "qhgd,khd->hgqk", grad_block, values, preferred_element_type=jnp.float32
        )
        delta = jnp.sum(probs * grad_probs, axis=-1, keepdims=True)
        grad_scores = (probs * (grad_probs - delta)).astype(jnp.bfloat16)
        grad_query = (
            jnp.einsum("hgqk,khd->qhgd", grad_scores, keys, preferred_element_type=jnp.float32)
            * score_scale
        )
        grad_keys = (
            grad_keys
            + jnp.einsum(
                "hgqk,qhgd->khd", grad_scores, query_block, preferred_element_type=jnp.float32
            )
            * score_scale
        )
        grad_values = grad_values + jnp.einsum(
            "hgqk,qhgd->khd",
            probs.astype(jnp.bfloat16),
            grad_block,
            preferred_element_type=jnp.float32,
        )
        return ((grad_keys, grad_values), grad_query)

    zero_heads = jnp.zeros(keys.shape, jnp.float32)
    starts = jnp.arange(count, dtype=jnp.int32) * block
    (grad_keys, grad_values), grad_queries = lax.scan(one_block, (zero_heads, zero_heads), starts)
    return (grad_queries.reshape(query_rows.shape), grad_keys, grad_values)


def routing_slots(route_rows):
    flat = route_rows.reshape(-1)
    onehot = (flat[:, None] == jnp.arange(EXPERTS, dtype=jnp.int32)[None, :]).astype(jnp.int32)
    running = jnp.cumsum(onehot, axis=0)
    return flat * CAP + jnp.sum(onehot * running, axis=1) - 1


def shards(
    tokens,
    cotangent,
    norm_gains,
    query_key_value_weight,
    output_weight,
    w_router,
    w_gate_up,
    w_down,
    segment_ids,
    routes,
):
    micro = tokens.shape[0]
    rows = tokens.shape[1]
    local_heads = query_key_value_weight.shape[1]
    local_experts = w_gate_up.shape[0]
    head_group = QUERY_HEADS // KEY_HEADS
    ep_size = lax.axis_size("ep")
    expert_ids = jnp.arange(EXPERTS, dtype=jnp.int32)
    acc_qkv = jnp.zeros((MODEL_WIDTH, local_heads, query_key_value_weight.shape[2]), jnp.float32)
    acc_out = jnp.zeros((local_heads, output_weight.shape[1], MODEL_WIDTH), jnp.float32)
    acc_router = jnp.zeros((MODEL_WIDTH, EXPERTS), jnp.float32)
    acc_gains = jnp.zeros((2, MODEL_WIDTH), jnp.float32)
    acc_gate_up = jnp.zeros((local_experts, MODEL_WIDTH, 2 * FF), jnp.float32)
    acc_down = jnp.zeros((local_experts, FF, MODEL_WIDTH), jnp.float32)
    outputs = []
    input_grads = []
    for micro_index in range(micro):
        qkv_full, out_full = (
            lax.all_gather(query_key_value_weight, "ep", axis=0, tiled=True),
            lax.all_gather(output_weight, "ep", axis=2, tiled=True),
        )
        gate_up_full, down_full = (
            lax.all_gather(w_gate_up, "tp", axis=1, tiled=True),
            lax.all_gather(w_down, "tp", axis=2, tiled=True),
        )
        inputs = tokens[micro_index].astype(jnp.float32)
        scale_one, normed_rows = norm_forward(inputs, norm_gains[0])
        segment_row = segment_ids[micro_index]
        cosine_table, sine_table = rope_tables(positions_of(segment_row))
        query_cos = cosine_table[:, None, None, :]
        query_sin = sine_table[:, None, None, :]
        key_cos = cosine_table[:, None, :]
        key_sin = sine_table[:, None, :]
        normed_full = lax.all_gather(normed_rows, "tp", axis=0, tiled=True)
        sequence_length = normed_full.shape[0]
        projected = jnp.dot(
            normed_full, qkv_full.reshape(MODEL_WIDTH, -1), preferred_element_type=jnp.float32
        )
        projected = projected.reshape(sequence_length, local_heads, -1)
        query_rows, keys, values = split_heads(
            projected, head_group, query_cos, query_sin, key_cos, key_sin
        )
        context, log_totals = attention_forward(query_rows, keys, values, segment_row)
        context_flat = context.reshape(sequence_length, local_heads, head_group * HEAD_SIZE)
        partial_value = jnp.einsum(
            "lhc,hcm->lm", context_flat, out_full, preferred_element_type=jnp.float32
        )
        branch = lax.psum_scatter(partial_value, "tp", scatter_dimension=0, tiled=True)
        hidden = inputs + residual_scale * branch
        scale_two, normed_two = norm_forward(hidden, norm_gains[1])
        logits = jnp.dot(normed_two, w_router, preferred_element_type=jnp.float32)
        route_rows = routes[micro_index, 0]
        route_onehot = (route_rows[:, :, None] == expert_ids[None, None, :]).astype(jnp.float32)
        chosen = jnp.sum(route_onehot * logits[:, None, :], axis=-1)
        gates = jax.nn.softmax(chosen, axis=-1)
        slots = routing_slots(route_rows)
        outgoing = (
            jnp.zeros((EXPERTS * CAP, MODEL_WIDTH), jnp.bfloat16)
            .at[slots]
            .set(jnp.repeat(normed_two, TOP, axis=0))
        )
        received = lax.all_to_all(
            outgoing.reshape(ep_size, local_experts, CAP, MODEL_WIDTH),
            "ep",
            split_axis=0,
            concat_axis=0,
            tiled=True,
        )
        expert_hidden = jnp.einsum(
            "secd,edf->secf", received, gate_up_full, preferred_element_type=jnp.float32
        )
        gate_part = expert_hidden[..., :FF]
        up_part = expert_hidden[..., FF:]
        sigmoid = jax.nn.sigmoid(gate_part)
        active = (gate_part * sigmoid * up_part).astype(jnp.bfloat16)
        expert_out = jnp.einsum(
            "secf,efd->secd", active, down_full, preferred_element_type=jnp.float32
        ).astype(jnp.bfloat16)
        returned = lax.all_to_all(expert_out, "ep", split_axis=0, concat_axis=0, tiled=True)
        picked = returned.reshape(EXPERTS * CAP, MODEL_WIDTH)[slots].reshape(rows, TOP, MODEL_WIDTH)
        mixture = jnp.sum(gates[:, :, None] * picked, axis=1)
        outputs.append((hidden + residual_scale * mixture).astype(jnp.bfloat16))
        grad_top = cotangent[micro_index].astype(jnp.float32)
        grad_mix = residual_scale * grad_top
        grad_gates = jnp.sum(picked * grad_mix[:, None, :], axis=-1)
        grad_picked = (gates[:, :, None] * grad_mix[:, None, :]).astype(jnp.bfloat16)
        grad_outgoing = (
            jnp.zeros((EXPERTS * CAP, MODEL_WIDTH), jnp.bfloat16)
            .at[slots]
            .set(grad_picked.reshape(rows * TOP, MODEL_WIDTH))
        )
        grad_expert_out = lax.all_to_all(
            grad_outgoing.reshape(ep_size, local_experts, CAP, MODEL_WIDTH),
            "ep",
            split_axis=0,
            concat_axis=0,
            tiled=True,
        )
        grad_active = jnp.einsum(
            "secd,efd->secf", grad_expert_out, down_full, preferred_element_type=jnp.float32
        )
        acc_down = acc_down + jnp.einsum(
            "secf,secd->efd", active, grad_expert_out, preferred_element_type=jnp.float32
        )
        grad_gate = grad_active * up_part * sigmoid * (1.0 + gate_part * (1.0 - sigmoid))
        grad_up = grad_active * gate_part * sigmoid
        grad_expert_hidden = jnp.concatenate([grad_gate, grad_up], axis=-1).astype(jnp.bfloat16)
        acc_gate_up = acc_gate_up + jnp.einsum(
            "secd,secf->edf", received, grad_expert_hidden, preferred_element_type=jnp.float32
        )
        grad_received = jnp.einsum(
            "secf,edf->secd", grad_expert_hidden, gate_up_full, preferred_element_type=jnp.float32
        ).astype(jnp.bfloat16)
        grad_sent = lax.all_to_all(grad_received, "ep", split_axis=0, concat_axis=0, tiled=True)
        grad_dispatched = grad_sent.reshape(EXPERTS * CAP, MODEL_WIDTH)[slots].reshape(
            rows, TOP, MODEL_WIDTH
        )
        grad_chosen = gates * (grad_gates - jnp.sum(gates * grad_gates, axis=-1, keepdims=True))
        grad_logits = jnp.sum(route_onehot * grad_chosen[:, :, None], axis=1).astype(jnp.bfloat16)
        acc_router = acc_router + jnp.dot(
            normed_two.T, grad_logits, preferred_element_type=jnp.float32
        )
        grad_normed_two = jnp.einsum("rkd->rd", grad_dispatched, preferred_element_type=jnp.float32)
        grad_normed_two = grad_normed_two + jnp.dot(
            grad_logits, w_router.T, preferred_element_type=jnp.float32
        )
        grad_from_two, gain_two = norm_backward(hidden, scale_two, norm_gains[1], grad_normed_two)
        grad_hidden = grad_top + grad_from_two
        grad_branch = (residual_scale * grad_hidden).astype(jnp.bfloat16)
        grad_branch_full = lax.all_gather(grad_branch, "tp", axis=0, tiled=True)
        acc_out = acc_out + jnp.einsum(
            "lhc,lm->hcm", context_flat, grad_branch_full, preferred_element_type=jnp.float32
        )
        grad_context = jnp.einsum(
            "lm,hcm->lhc", grad_branch_full, out_full, preferred_element_type=jnp.float32
        )
        grad_context = grad_context.astype(jnp.bfloat16).reshape(
            sequence_length, local_heads, head_group, HEAD_SIZE
        )
        grad_queries, grad_keys, grad_values = attention_backward(
            query_rows, keys, values, segment_row, log_totals, grad_context
        )
        grad_queries = unrotate(grad_queries, query_cos, query_sin)
        grad_keys = unrotate(grad_keys, key_cos, key_sin)
        grad_projected = jnp.concatenate(
            [
                grad_queries.reshape(sequence_length, local_heads, head_group * HEAD_SIZE),
                grad_keys,
                grad_values,
            ],
            axis=-1,
        )
        grad_projected = grad_projected.astype(jnp.bfloat16)
        acc_qkv = acc_qkv + jnp.einsum(
            "ld,lhc->dhc", normed_full, grad_projected, preferred_element_type=jnp.float32
        )
        partial_grad = jnp.einsum(
            "lhc,dhc->ld", grad_projected, qkv_full, preferred_element_type=jnp.float32
        )
        grad_normed = lax.psum_scatter(
            partial_grad.astype(jnp.bfloat16), "tp", scatter_dimension=0, tiled=True
        ).astype(jnp.float32)
        grad_from_one, gain_one = norm_backward(inputs, scale_one, norm_gains[0], grad_normed)
        input_grads.append(grad_hidden + grad_from_one)
        acc_gains = acc_gains + jnp.stack([gain_one, gain_two])
    grad_gate_up, grad_down, part_router, part_gains = (
        lax.psum_scatter(
            acc_gate_up.astype(jnp.bfloat16), "tp", scatter_dimension=1, tiled=True
        ).astype(jnp.float32),
        lax.psum_scatter(
            acc_down.astype(jnp.bfloat16), "tp", scatter_dimension=2, tiled=True
        ).astype(jnp.float32),
        lax.psum_scatter(
            acc_router.astype(jnp.bfloat16), "tp", scatter_dimension=0, tiled=True
        ).astype(jnp.float32),
        lax.psum_scatter(
            acc_gains.astype(jnp.bfloat16), "tp", scatter_dimension=1, tiled=True
        ).astype(jnp.float32),
    )
    grad_qkv, grad_out, grad_router, grad_gains = (
        lax.psum_scatter(
            acc_qkv.astype(jnp.bfloat16), "ep", scatter_dimension=0, tiled=True
        ).astype(jnp.float32),
        lax.psum_scatter(
            acc_out.astype(jnp.bfloat16), "ep", scatter_dimension=2, tiled=True
        ).astype(jnp.float32),
        lax.psum_scatter(
            part_router.astype(jnp.bfloat16), "ep", scatter_dimension=0, tiled=True
        ).astype(jnp.float32),
        lax.psum_scatter(
            part_gains.astype(jnp.bfloat16), "ep", scatter_dimension=1, tiled=True
        ).astype(jnp.float32),
    )
    return (
        jnp.stack(outputs),
        jnp.stack(input_grads),
        grad_gains,
        grad_qkv,
        grad_out,
        grad_router,
        grad_gate_up,
        grad_down,
    )


def solution(mesh):
    placed = (
        P("ep", "tp", None),
        P("ep", "tp", None),
        P(),
        P("ep", "tp", None),
        P("tp", None, "ep"),
        P(),
        P("ep", "tp", None),
        P("ep", None, "tp"),
        P("ep", None),
        P("ep", "tp", None, None),
    )
    return jax.shard_map(
        shards,
        mesh=mesh,
        in_specs=placed,
        out_specs=(
            P("ep", "tp", None),
            P("ep", "tp", None),
            P(None, ("tp", "ep")),
            P("ep", "tp", None),
            P("tp", None, "ep"),
            P(("tp", "ep"), None),
            P("ep", "tp", None),
            P("ep", None, "tp"),
        ),
        check_vma=False,
    )
```

profile of v0, /device:TPU:0, one launch (start us, length us, event | category | flops | bytes accessed | tf_op | source)
XLA Modules:
  0.0 1997.2 jit_solution(1558384414448985356)
XLA Ops:
  17.8 20.4 %all_gather.30 = bf16[2,128,1024]{2,1,0:T(8,128)(2,1)S(1)} all-gather(bf16[2,128,128]{2,1,0:T(8,128)(2,1)} %param.22), channel_id=1, replica_groups=mesh['tp'=4,'ep'=8] {'ep'}, dimensions={2}, use_global_device_ids=true | all-gather | bytes 589824 | tf_op jit(solution)/shard_map/all_gather | solution.py:207
  40.9 34.4 %all-gather.16.cloned.1.call-done = bf16[1024,1024]{1,0:T(8,128)(2,1)} async-done(((bf16[256,1024]{1,0:T(8,128)(2,1)}), bf16[1024,1024]{1,0:T(8,128)(2,1)}) %all-gather.16.cloned.1.call-update) | async-done | bytes 2097168 | tf_op jit(solution)/shard_map/all_gather | solution.py:221
  78.7 23.5 %while.55 = (s32[]{:T(128)}, bf16[2,512,2,2,64]{1,4,3,2,0:T(8,128)(2,1)S(1)}, f32[2,2,2,512]{3,2,1,0:T(2,128)S(1)}, s32[2]{0:T(128)}, s32[1,1024]{1,0:T(1,128)S(...) while((s32[]{:T(128)}, ...), condition=%wide.region_25.26_spmd, body=%wide.region_22.25_spmd.sunk | while | flops 563739136 | bytes 28391608 | solution.py:120
  116.6 23.7 %while.54 = (s32[]{:T(128)}, bf16[2,512,2,2,64]{1,4,3,2,0:T(8,128)(2,1)S(1)}, f32[2,2,2,512]{3,2,1,0:T(2,128)S(1)}, s32[2]{0:T(128)}, s32[1,1024]{1,0:T(1,128)S(...) while((s32[]{:T(128)}, ...), condition=%wide.region_7.8_spmd, body=%wide.region_4.7_spmd.sunk | while | flops 563739136 | bytes 28391608 | solution.py:120
  168.4 56.0 %reduce-scatter.21.cloned.1.call-done = f32[256,1024]{1,0:T(8,128)} async-done(((f32[1024,1024]{1,0:T(8,128)}), f32[256,1024]{1,0:T(8,128)}) %reduce-scatter.21.cloned.1.call-update) | async-done | bytes 1048592 | tf_op jit(solution)/shard_map/reduce_scatter | solution.py:235
  227.1 13.9 scatter_custom_fusion
  250.5 14.5 scatter_custom_fusion.2
  265.0 119.7 %all-to-all-done = bf16[8,4,96,1024]{3,2,1,0:T(8,128)(2,1)} async-done(((bf16[8,4,96,1024]{3,2,1,0:T(8,128)(2,1)}), bf16[8,4,96,1024]{3,2,1,0:T(8,128)(2,1)}, u32[]{:S(2)}, u32[]{:S(2)}) %all-to-all-start) | async-done | bytes 6291488 | tf_op jit(solution)/shard_map/all_to_all | solution.py:249
  404.1 40.9 %all-gather.14.cloned.1.call-done = bf16[4,512,1024]{2,1,0:T(8,128)(2,1)} async-done(((bf16[4,512,256]{2,1,0:T(8,128)(2,1)}), bf16[4,512,1024]{2,1,0:T(8,128)(2,1)}) %all-gather.14.cloned.1.call-update) | async-done | bytes 4194320 | tf_op jit(solution)/shard_map/all_gather | solution.py:211
  445.0 83.4 %all-to-all-done.4 = bf16[8,4,96,1024]{3,2,1,0:T(8,128)(2,1)} async-done(((bf16[8,4,96,1024]{3,2,1,0:T(8,128)(2,1)}), bf16[8,4,96,1024]{3,2,1,0:T(8,128)(2,1)}, u32[]{:S(2)}, u32[]{:S(2)}) %all-to-all-start.4) | async-done | bytes 6291488 | tf_op jit(solution)/shard_map/all_to_all | solution.py:279
  574.8 119.4 %all-to-all-done.1 = bf16[8,4,96,1024]{3,2,1,0:T(8,128)(2,1)} async-done(((bf16[8,4,96,1024]{3,2,1,0:T(8,128)(2,1)}), bf16[8,4,96,1024]{3,2,1,0:T(8,128)(2,1)}, u32[]{:S(2)}, u32[]{:S(2)}) %all-to-all-start.1) | async-done | bytes 6291488 | tf_op jit(solution)/shard_map/all_to_all | solution.py:266
  700.3 15.9 reduce-window.40
  721.9 14.6 gather_fusion
  742.8 95.3 %all-to-all-done.5 = bf16[8,4,96,1024]{3,2,1,0:T(8,128)(2,1)} async-done(((bf16[8,4,96,1024]{3,2,1,0:T(8,128)(2,1)}), bf16[8,4,96,1024]{3,2,1,0:T(8,128)(2,1)}, u32[]{:S(2)}, u32[]{:S(2)}) %all-to-all-start.5) | async-done | bytes 6291488 | tf_op jit(solution)/shard_map/all_to_all | solution.py:301
  838.1 14.5 gather_fusion.2
  860.4 14.3 scatter_custom_fusion.1
  881.0 14.3 scatter_custom_fusion.3
  895.3 123.0 %all-to-all-done.2 = bf16[8,4,96,1024]{3,2,1,0:T(8,128)(2,1)} async-done(((bf16[8,4,96,1024]{3,2,1,0:T(8,128)(2,1)}), bf16[8,4,96,1024]{3,2,1,0:T(8,128)(2,1)}, u32[]{:S(2)}, u32[]{:S(2)}) %all-to-all-start.2) | async-done | bytes 6291488 | tf_op jit(solution)/shard_map/all_to_all | solution.py:249
  1037.1 125.1 %all-to-all-done.6 = bf16[8,4,96,1024]{3,2,1,0:T(8,128)(2,1)} async-done(((bf16[8,4,96,1024]{3,2,1,0:T(8,128)(2,1)}), bf16[8,4,96,1024]{3,2,1,0:T(8,128)(2,1)}, u32[]{:S(2)}, u32[]{:S(2)}) %all-to-all-start.6) | async-done | bytes 6291488 | tf_op jit(solution)/shard_map/all_to_all | solution.py:279
  1208.6 119.4 %all-to-all-done.3 = bf16[8,4,96,1024]{3,2,1,0:T(8,128)(2,1)} async-done(((bf16[8,4,96,1024]{3,2,1,0:T(8,128)(2,1)}), bf16[8,4,96,1024]{3,2,1,0:T(8,128)(2,1)}, u32[]{:S(2)}, u32[]{:S(2)}) %all-to-all-start.3) | async-done | bytes 6291488 | tf_op jit(solution)/shard_map/all_to_all | solution.py:266
  1335.1 14.5 gather_fusion.1
  1357.9 113.8 %all-to-all-done.7 = bf16[8,4,96,1024]{3,2,1,0:T(8,128)(2,1)} async-done(((bf16[8,4,96,1024]{3,2,1,0:T(8,128)(2,1)}), bf16[8,4,96,1024]{3,2,1,0:T(8,128)(2,1)}, u32[]{:S(2)}, u32[]{:S(2)}) %all-to-all-start.7) | async-done | bytes 6291488 | tf_op jit(solution)/shard_map/all_to_all | solution.py:301
  1471.7 14.5 gather_fusion.3
  1533.0 70.4 %while.57 = (s32[]{:T(128)}, f32[1024,2,64]{0,2,1:T(8,128)S(1)}, f32[1024,2,64]{0,2,1:T(8,128)}, f32[2,512,2,2,64]{1,0,4,3,2:T(2,128)}, s32[2]{0:T(128)}, /*inde...) while((s32[]{:T(128)}, f32[1024,2,64]{0,2,1:T(8,128)S(1)}, ...), condition=%wide.region_55.56_spmd.clone, body=%wide.region_53.55_spmd.clone.sunk | while | flops 1375992320 | bytes 126163296 | solution.py:166
  1613.2 70.3 %while.56 = (s32[]{:T(128)}, f32[1024,2,64]{0,2,1:T(8,128)S(1)}, f32[1024,2,64]{0,2,1:T(8,128)}, f32[2,512,2,2,64]{1,0,4,3,2:T(2,128)}, s32[2]{0:T(128)}, /*inde...) while((s32[]{:T(128)}, f32[1024,2,64]{0,2,1:T(8,128)S(1)}, ...), condition=%wide.region_44.45_spmd.clone, body=%wide.region_42.44_spmd.clone.sunk | while | flops 1375992320 | bytes 126163296 | solution.py:166
  1708.2 13.9 fusion.123
  1722.1 15.1 fusion.96
  1766.2 85.9 %reduce-scatter.33.cloned.1.call-done = bf16[4,256,1024]{2,1,0:T(8,128)(2,1)} async-done(((bf16[4,1024,1024]{2,1,0:T(8,128)(2,1)}), bf16[4,256,1024]{2,1,0:T(8,128)(2,1)}) %reduce-scatter.33.cloned.1.call-update) | async-done | bytes 2097168 | tf_op jit(solution)/shard_map/reduce_scatter | solution.py:354
  1856.3 33.9 %reduce-scatter.27.cloned.1.call-done = bf16[256,1024]{1,0:T(8,128)(2,1)} async-done(((bf16[1024,1024]{1,0:T(8,128)(2,1)}), bf16[256,1024]{1,0:T(8,128)(2,1)}) %reduce-scatter.27.cloned.1.call-update) | async-done | bytes 524304 | tf_op jit(solution)/shard_map/reduce_scatter | solution.py:347
  1890.2 38.6 %reduce-scatter.25.cloned.1.call-done = bf16[256,1024]{1,0:T(8,128)(2,1)} async-done(((bf16[1024,1024]{1,0:T(8,128)(2,1)}), bf16[256,1024]{1,0:T(8,128)(2,1)}) %reduce-scatter.25.cloned.1.call-update) | async-done | bytes 524304 | tf_op jit(solution)/shard_map/reduce_scatter | solution.py:347
  1935.1 21.2 %reduce-scatter.37.cloned.1.call-done = bf16[256,2]{1,0:T(8,128)(2,1)} async-done(((bf16[1024,2]{1,0:T(8,128)(2,1)}), bf16[256,2]{1,0:T(8,128)(2,1)}) %reduce-scatter.37.cloned.1.call-update) | async-done | bytes 1040
  1959.5 29.7 %reduce-scatter.39.cloned.1.call-done = bf16[32,2]{1,0:T(8,128)(2,1)} async-done(((bf16[256,2]{1,0:T(8,128)(2,1)}), bf16[32,2]{1,0:T(8,128)(2,1)}) %reduce-scatter.39.cloned.1.call-update) | async-done | bytes 144
  (491 shorter events, 544.9 us)
Async XLA Ops:
  7.2 241.7 %copy-start = (bf16[1024,32]{0,1:T(8,128)(2,1)S(1)}, bf16[1024,32]{0,1:T(8,128)(2,1)}, u32[]{:S(2)}) copy-start(bf16[1024,32]{0,1:T(8,128)(2,1)} %param.23) | copy-start | bytes 196612
  7.2 32.1 %all-gather.10.cloned.1.call-start = ((), (), s32[]{:S(2)}) async-start(), calls=%async_computation.21 | async-start | bytes 1179648 | tf_op jit(solution)/shard_map/all_gather | solution.py:206
  8.8 66.4 %all-gather.16.cloned.1.call-start = ((), (), s32[]{:S(2)}) async-start(), calls=%async_computation.25 | async-start | bytes 2621440 | tf_op jit(solution)/shard_map/all_gather | solution.py:221
  14.9 98.0 %all-gather.8.cloned.1.call-start = ((), (), s32[]{:S(2)}) async-start(), calls=%async_computation.20 | async-start | bytes 2621440 | tf_op jit(solution)/shard_map/all_gather | solution.py:221
  15.6 152.8 %reduce-scatter.23.cloned.1.call-start = ((), (), s32[]{:S(2)}) async-start(), calls=%async_computation.26 | async-start | bytes 5242880 | tf_op jit(solution)/shard_map/reduce_scatter | solution.py:235
  107.0 117.4 %reduce-scatter.21.cloned.1.call-start = ((), (), s32[]{:S(2)}) async-start(), calls=%async_computation.22 | async-start | bytes 5242880 | tf_op jit(solution)/shard_map/reduce_scatter | solution.py:235
  241.1 143.7 %all-to-all-start = ((bf16[8,4,96,1024]{3,2,1,0:T(8,128)(2,1)}), bf16[8,4,96,1024]{3,2,1,0:T(8,128)(2,1)}, u32[]{:S(2)}, u32[]{:S(2)}) async-start(bf16[8,4,96,1024]{3,2,1,0:T(8,128)(2,1)} %bitcast.647), calls=%async_computation.1 | async-start | bytes 12582912 | tf_op jit(solution)/shard_map/all_to_all | solution.py:249
  245.8 144.5 %all-gather.12.cloned.1.call-start = ((), (), s32[]{:S(2)}) async-start(), calls=%async_computation.23 | async-start | bytes 10485760 | tf_op jit(solution)/shard_map/all_gather | solution.py:210
  384.8 143.7 %all-to-all-start.4 = ((bf16[8,4,96,1024]{3,2,1,0:T(8,128)(2,1)}), bf16[8,4,96,1024]{3,2,1,0:T(8,128)(2,1)}, u32[]{:S(2)}, u32[]{:S(2)}) async-start(bf16[8,4,96,1024]{3,2,1,0:T(8,128)(2,1)} %bitcast.648), calls=%async_computation.6 | async-start | bytes 12582912 | tf_op jit(solution)/shard_map/all_to_all | solution.py:279
  389.5 55.5 %all-gather.14.cloned.1.call-start = ((), (), s32[]{:S(2)}) async-start(), calls=%async_computation.24 | async-start | bytes 5242880 | tf_op jit(solution)/shard_map/all_gather | solution.py:211
  550.6 143.7 %all-to-all-start.1 = ((bf16[8,4,96,1024]{3,2,1,0:T(8,128)(2,1)}), bf16[8,4,96,1024]{3,2,1,0:T(8,128)(2,1)}, u32[]{:S(2)}, u32[]{:S(2)}) async-start(bf16[8,4,96,1024]{3,2,1,0:T(8,128)(2,1)} %copy.242), calls=%async_computation.2 | async-start | bytes 12582912 | tf_op jit(solution)/shard_map/all_to_all | solution.py:266
  694.2 143.9 %all-to-all-start.5 = ((bf16[8,4,96,1024]{3,2,1,0:T(8,128)(2,1)}), bf16[8,4,96,1024]{3,2,1,0:T(8,128)(2,1)}, u32[]{:S(2)}, u32[]{:S(2)}) async-start(bf16[8,4,96,1024]{3,2,1,0:T(8,128)(2,1)} %copy.255), calls=%async_computation.7 | async-start | bytes 12582912 | tf_op jit(solution)/shard_map/all_to_all | solution.py:301
  874.6 143.7 %all-to-all-start.2 = ((bf16[8,4,96,1024]{3,2,1,0:T(8,128)(2,1)}), bf16[8,4,96,1024]{3,2,1,0:T(8,128)(2,1)}, u32[]{:S(2)}, u32[]{:S(2)}) async-start(bf16[8,4,96,1024]{3,2,1,0:T(8,128)(2,1)} %bitcast.649), calls=%async_computation.4 | async-start | bytes 12582912 | tf_op jit(solution)/shard_map/all_to_all | solution.py:249
  1018.3 143.9 %all-to-all-start.6 = ((bf16[8,4,96,1024]{3,2,1,0:T(8,128)(2,1)}), bf16[8,4,96,1024]{3,2,1,0:T(8,128)(2,1)}, u32[]{:S(2)}, u32[]{:S(2)}) async-start(bf16[8,4,96,1024]{3,2,1,0:T(8,128)(2,1)} %bitcast.650), calls=%async_computation.9 | async-start | bytes 12582912 | tf_op jit(solution)/shard_map/all_to_all | solution.py:279
  1184.3 143.7 %all-to-all-start.3 = ((bf16[8,4,96,1024]{3,2,1,0:T(8,128)(2,1)}), bf16[8,4,96,1024]{3,2,1,0:T(8,128)(2,1)}, u32[]{:S(2)}, u32[]{:S(2)}) async-start(bf16[8,4,96,1024]{3,2,1,0:T(8,128)(2,1)} %copy.252), calls=%async_computation.5 | async-start | bytes 12582912 | tf_op jit(solution)/shard_map/all_to_all | solution.py:266
  1328.0 143.7 %all-to-all-start.7 = ((bf16[8,4,96,1024]{3,2,1,0:T(8,128)(2,1)}), bf16[8,4,96,1024]{3,2,1,0:T(8,128)(2,1)}, u32[]{:S(2)}, u32[]{:S(2)}) async-start(bf16[8,4,96,1024]{3,2,1,0:T(8,128)(2,1)} %copy.266), calls=%async_computation.10 | async-start | bytes 12582912 | tf_op jit(solution)/shard_map/all_to_all | solution.py:301
  1332.8 184.0 %reduce-scatter.31.cloned.1.call-start = ((), (), s32[]{:S(2)}) async-start(), calls=%async_computation.32 | async-start | bytes 81920 | tf_op jit(solution)/shard_map/reduce_scatter | solution.py:360
  1357.8 171.6 %all-gather.20.cloned.1.call-start = ((), (), s32[]{:S(2)}) async-start(), calls=%async_computation.29 | async-start | bytes 2621440 | tf_op jit(solution)/shard_map/all_gather | solution.py:317
  1496.2 113.4 %all-gather.18.cloned.1.call-start = ((), (), s32[]{:S(2)}) async-start(), calls=%async_computation.27 | async-start | bytes 2621440 | tf_op jit(solution)/shard_map/all_gather | solution.py:317
  1496.7 249.6 %reduce-scatter.35.cloned.1.call-start = ((), (), s32[]{:S(2)}) async-start(), calls=%async_computation.34 | async-start | bytes 5242880 | tf_op jit(solution)/shard_map/reduce_scatter | solution.py:357
  1516.6 234.9 %reduce-scatter.43.cloned.1.call-start = ((), (), s32[]{:S(2)}) async-start(), calls=%async_computation.38 | async-start | bytes 73728
  1518.4 234.6 %reduce-scatter.41.cloned.1.call-start = ((), (), s32[]{:S(2)}) async-start(), calls=%async_computation.37 | async-start | bytes 589824
  1700.1 64.4 %reduce-scatter.29.cloned.1.call-start = ((), (), s32[]{:S(2)}) async-start(), calls=%async_computation.31 | async-start | bytes 1179648 | tf_op jit(solution)/shard_map/reduce_scatter | solution.py:368
  1708.1 144.0 %reduce-scatter.33.cloned.1.call-start = ((), (), s32[]{:S(2)}) async-start(), calls=%async_computation.33 | async-start | bytes 10485760 | tf_op jit(solution)/shard_map/reduce_scatter | solution.py:354
  1737.2 153.0 %reduce-scatter.27.cloned.1.call-start = ((), (), s32[]{:S(2)}) async-start(), calls=%async_computation.30 | async-start | bytes 2621440 | tf_op jit(solution)/shard_map/reduce_scatter | solution.py:347
  1742.3 186.5 %reduce-scatter.25.cloned.1.call-start = ((), (), s32[]{:S(2)}) async-start(), calls=%async_computation.28 | async-start | bytes 2621440 | tf_op jit(solution)/shard_map/reduce_scatter | solution.py:347
  1746.2 182.6 %copy-start.11 = (bf16[2,256,1024]{2,1,0:T(8,128)(2,1)S(1)}, bf16[2,256,1024]{2,1,0:T(8,128)(2,1)}, u32[]{:S(2)}) copy-start(bf16[2,256,1024]{2,1,0:T(8,128)(2,1)} %param.18) | copy-start | bytes 3145732
  1746.2 182.6 %copy-start.58 = (f32[1,1024]{1,0:T(1,128)S(1)}, f32[1,1024]{1,0:T(1,128)}, u32[]{:S(2)}) copy-start(f32[1,1024]{1,0:T(1,128)} %copy-done.57) | copy-start | bytes 12292
  1746.2 210.1 %reduce-scatter.37.cloned.1.call-start = ((), (), s32[]{:S(2)}) async-start(), calls=%async_computation.35 | async-start | bytes 327680
  1749.1 182.8 %copy-start.31 = (f32[256,1024]{1,0:T(8,128)S(1)}, f32[256,1024]{1,0:T(8,128)}, u32[]{:S(2)}) copy-start(f32[256,1024]{1,0:T(8,128)} %get-tuple-element.469) | copy-start | bytes 3145732
  1749.1 182.8 %copy-start.32 = (f32[256,1024]{1,0:T(8,128)S(1)}, f32[256,1024]{1,0:T(8,128)}, u32[]{:S(2)}) copy-start(f32[256,1024]{1,0:T(8,128)} %get-tuple-element.505) | copy-start | bytes 3145732
  1931.8 57.4 %reduce-scatter.39.cloned.1.call-start = ((), (), s32[]{:S(2)}) async-start(), calls=%async_computation.36 | async-start | bytes 73728
  (81 other events, 2509.2 us)
Sparse Core Ops, SparseCore 0:
  10.2 28.0 all-gather.9
  40.7 34.5 all-gather.15
  77.7 35.1 all-gather.7
  115.7 52.6 reduce-scatter.22
  171.8 52.5 reduce-scatter.20
  248.2 87.8 all-gather.11
  392.2 52.8 all-gather.13
  1357.9 24.4 reduce-scatter.30
  1496.3 33.0 all-gather.19
  1531.7 35.1 all-gather.17
  1570.4 52.5 reduce-scatter.34
  1625.1 30.4 reduce-scatter.42
  1700.2 31.4 reduce-scatter.40
  1733.8 30.6 reduce-scatter.28
  1767.4 84.7 reduce-scatter.32
  1855.0 35.1 reduce-scatter.26
  1893.6 35.1 reduce-scatter.24
  1932.0 24.3 reduce-scatter.36
  1958.6 30.5 reduce-scatter.38
where the time goes:
time: 2010 us; the launch traced here: 2000 us
  waiting for transfers between devices  1280 us (64%)
  matrix products  264 us (13%)
  local copies, waits for them, and re-layouts  210 us (10%)
  other arithmetic  149 us (7%)
  starting transfers between devices  40 us (2%)
  blocking collectives  20.4 us (1%)
    all_to_all x2, waiting for transfers between devices, shards(): lax.all_to_all(outgoing.reshape(ep_size, local_experts, CAP, MODEL_WIDTH)...  243 us
    all_to_all x2, waiting for transfers between devices, shards(): lax.all_to_all(expert_out, 'ep', split_axis=0, concat_axis=0, tiled=True)  239 us
    all_to_all x2, waiting for transfers between devices, shards(): lax.all_to_all(grad_received, 'ep', split_axis=0, concat_axis=0, tiled=True)  209 us
    all_to_all x2, waiting for transfers between devices, shards(): lax.all_to_all(grad_outgoing.reshape(ep_size, local_experts, CAP, MODEL_W...  208 us
    reduce_scatter x1, waiting for transfers between devices, shards(): lax.psum_scatter(acc_gate_up.astype(jnp.bfloat16), 'tp', scatter_dimensio...  85.9 us
    reduce_scatter x2, waiting for transfers between devices, shards(): lax.psum_scatter(partial_grad.astype(jnp.bfloat16), 'tp', scatter_dimensi...  72.5 us
    reduce_scatter x2, waiting for transfers between devices, shards(): lax.psum_scatter(partial_value, 'tp', scatter_dimension=0, tiled=True)  68.5 us
    unnamed x23, waiting for transfers between devices  53.4 us
  transfers between devices with their start and end apart: 27, of which 20 were waited for; matrix products, arithmetic and copies ran while one was open for 25% of the time, Pallas kernels for 0%

commit v1 on v0

v1 whole, which is shorter than its diff:
```python
import functools

import jax
import jax.numpy as jnp
from jax import lax
from jax.experimental import pallas as pl
from jax.experimental.pallas import tpu as pltpu
from jax.sharding import PartitionSpec as P

MODEL_WIDTH = 1024
HEAD_SIZE = 64
FF = 512
EXPERTS = 32
DOCS = 4
CAP = 96
LANES = 128
ROW_BLOCK = 256
GROUP_COLS = 256

epsilon = 1e-06
score_scale = 0.015625
residual_scale = 0.22
rope_base = 10000.0
masked_score = -1000000000.0

f32 = jnp.float32
bf16 = jnp.bfloat16

params = pltpu.CompilerParams(vmem_limit_bytes=58 * 1024 * 1024)
row_params = pltpu.CompilerParams(
    vmem_limit_bytes=58 * 1024 * 1024, dimension_semantics=("arbitrary",)
)


def dot(a, b):
    return jnp.dot(a, b, preferred_element_type=f32)


def dot_nt(a, b):
    return lax.dot_general(a, b, (((1,), (1,)), ((), ())), preferred_element_type=f32)


def dot_tn(a, b):
    return lax.dot_general(a, b, (((0,), (0,)), ((), ())), preferred_element_type=f32)


def lane_masks(rows):
    lane = lax.broadcasted_iota(jnp.int32, (rows, LANES), 1)
    return lane < HEAD_SIZE, (lane % HEAD_SIZE) < HEAD_SIZE // 2


def swap_halves(values, first):
    half = HEAD_SIZE // 2
    return jnp.where(first, pltpu.roll(values, LANES - half, 1), pltpu.roll(values, half, 1))


def for_blocks(count, body):
    if count <= 4:
        for index in range(count):
            body(index)
    else:

        def step(index, carry):
            body(index)
            return carry

        lax.fori_loop(0, count, step, 0)


def block_rows(index):
    if isinstance(index, int):
        return pl.ds(index * ROW_BLOCK, ROW_BLOCK)
    return pl.ds(pl.multiple_of(index * ROW_BLOCK, ROW_BLOCK), ROW_BLOCK)


def key_window(index, length):
    reach = -(-(length // 2) // ROW_BLOCK)
    if isinstance(index, int):
        start = max(0, index - reach) * ROW_BLOCK
        return start, (index + 1) * ROW_BLOCK - start
    start = jnp.maximum(index - reach, 0) * ROW_BLOCK
    return pl.multiple_of(start, ROW_BLOCK), (reach + 1) * ROW_BLOCK


def allowed_keys(index, start, width, seg_col_ref, seg_row_ref):
    query = lax.broadcasted_iota(jnp.int32, (ROW_BLOCK, width), 0) + index * ROW_BLOCK
    key = lax.broadcasted_iota(jnp.int32, (ROW_BLOCK, width), 1) + start
    same = seg_row_ref[:, pl.ds(start, width)] == seg_col_ref[block_rows(index), :]
    return (key <= query) & same


def place_rows(starts_ref, pieces, whole):
    for index, piece in enumerate(pieces):
        rows = piece.shape[0]
        begin = pl.multiple_of(starts_ref[index], ROW_BLOCK)
        whole[pl.ds(begin, rows), :] = piece[...]


def each_block(starts_ref, pieces):
    for index, piece in enumerate(pieces):
        for inner in range(0, piece.shape[0], ROW_BLOCK):
            begin = pl.multiple_of(starts_ref[index] + inner, ROW_BLOCK)
            yield pl.ds(begin, ROW_BLOCK), piece, slice(inner, inner + ROW_BLOCK)


def attention_forward_body(starts_ref, *refs, count):
    x_pieces = refs[:count]
    gain_ref, weights_ref, cos_ref, sin_ref, seg_col_ref, seg_row_ref = refs[count : count + 6]
    parts = refs[count + 6 : 2 * count + 6]
    qa_ref, qb_ref, kd_ref, vd_ref, ctx_ref, x_ref = refs[2 * count + 6 :]
    place_rows(starts_ref, x_pieces, x_ref)
    length = x_ref.shape[0]
    groups = weights_ref.shape[1] // (GROUP_COLS + LANES)
    low, first = lane_masks(ROW_BLOCK)

    def project(index):
        rows = block_rows(index)
        x = x_ref[rows, :].astype(f32)
        scale = lax.rsqrt(jnp.mean(x * x, axis=-1, keepdims=True) + epsilon)
        normed = (x * scale * gain_ref[...]).astype(bf16)
        projected = dot(normed, weights_ref[:, : groups * GROUP_COLS])
        cosine = cos_ref[rows, :]
        sine = sin_ref[rows, :]
        for group in range(groups):
            cols = slice(group * LANES, (group + 1) * LANES)
            query = projected[:, group * GROUP_COLS : group * GROUP_COLS + LANES]
            pair = projected[:, group * GROUP_COLS + LANES : (group + 1) * GROUP_COLS]
            query = (query * cosine + swap_halves(query, first) * sine) * score_scale
            qa_ref[rows, cols] = jnp.where(low, query, 0.0).astype(bf16)
            qb_ref[rows, cols] = jnp.where(low, 0.0, query).astype(bf16)
            turned = pair * cosine + swap_halves(pair, first) * sine
            kd_ref[rows, cols] = jnp.where(low, turned, pltpu.roll(turned, HEAD_SIZE, 1)).astype(
                bf16
            )
            vd_ref[rows, cols] = jnp.where(low, pltpu.roll(pair, HEAD_SIZE, 1), pair).astype(bf16)

    def attend(index):
        rows = block_rows(index)
        start, width = key_window(index, length)
        keys = pl.ds(start, width)
        allowed = allowed_keys(index, start, width, seg_col_ref, seg_row_ref)
        for group in range(groups):
            cols = slice(group * LANES, (group + 1) * LANES)
            heads = []
            for q_ref in (qa_ref, qb_ref):
                scores = dot_nt(q_ref[rows, cols], kd_ref[keys, cols])
                scores = jnp.where(allowed, scores, masked_score)
                expo = jnp.exp(scores - jnp.max(scores, axis=-1, keepdims=True))
                total = jnp.sum(expo, axis=-1, keepdims=True)
                probs = (expo * (1.0 / total)).astype(bf16)
                heads.append(dot(probs, vd_ref[keys, cols]))
            ctx_ref[rows, cols] = jnp.where(low, heads[0], heads[1]).astype(bf16)

    for_blocks(length // ROW_BLOCK, project)
    for_blocks(length // ROW_BLOCK, attend)
    for rows, part, inner in each_block(starts_ref, parts):
        part[inner, :] = dot_nt(ctx_ref[rows, :], weights_ref[:, groups * GROUP_COLS :]).astype(
            bf16
        )


def in_vmem(count):
    return [pl.BlockSpec(memory_space=pltpu.SMEM)] + [
        pl.BlockSpec(memory_space=pltpu.VMEM) for _ in range(count)
    ]


def attention_forward(starts, pieces, gain, weights, cosine, sine, seg_col, seg_row):
    length = cosine.shape[0]
    count = len(pieces)
    half = jax.ShapeDtypeStruct((length, weights.shape[1] // 3), bf16)
    results = pl.pallas_call(
        functools.partial(attention_forward_body, count=count),
        out_shape=tuple(jax.ShapeDtypeStruct(p.shape, bf16) for p in pieces) + (half,) * 5,
        in_specs=in_vmem(count + 6),
        scratch_shapes=[pltpu.VMEM((length, MODEL_WIDTH), bf16)],
        compiler_params=params,
        name="attn_fwd",
    )(starts, *pieces, gain, weights, cosine, sine, seg_col, seg_row)
    return results[:count], results[count:]


def attention_backward_body(starts_ref, *refs, count):
    x_pieces, refs = refs[:count], refs[count:]
    gain_ref, weights_ref, cos_ref, sin_ref, seg_col_ref, seg_row_ref = refs[:6]
    qa_ref, qb_ref, kd_ref, vd_ref, ctx_ref = refs[6:11]
    gb_pieces, parts, refs = refs[11 : 11 + count], refs[11 + count : 11 + 2 * count], refs[
        11 + 2 * count :
    ]
    grad_ref, gain_grad_ref, gb_ref, norm_sc, proj_sc, dk_sc, dv_sc = refs
    place_rows(starts_ref, gb_pieces, gb_ref)
    length = gb_ref.shape[0]
    groups = weights_ref.shape[1] // (GROUP_COLS + LANES)
    split = groups * GROUP_COLS
    low, first = lane_masks(ROW_BLOCK)
    dk_sc[...] = jnp.zeros_like(dk_sc)
    dv_sc[...] = jnp.zeros_like(dv_sc)

    def attend(index):
        rows = block_rows(index)
        start, width = key_window(index, length)
        keys = pl.ds(start, width)
        allowed = allowed_keys(index, start, width, seg_col_ref, seg_row_ref)
        grad_context = dot(gb_ref[rows, :], weights_ref[:, split:])
        cosine = cos_ref[rows, :]
        sine = sin_ref[rows, :]
        for group in range(groups):
            cols = slice(group * LANES, (group + 1) * LANES)
            grad_group = grad_context[:, cols]
            grad_queries = []
            for head, q_ref in enumerate((qa_ref, qb_ref)):
                if head == 0:
                    grad_head = jnp.where(low, grad_group, 0.0).astype(bf16)
                else:
                    grad_head = jnp.where(low, 0.0, grad_group).astype(bf16)
                query = q_ref[rows, cols]
                scores = dot_nt(query, kd_ref[keys, cols])
                scores = jnp.where(allowed, scores, masked_score)
                expo = jnp.exp(scores - jnp.max(scores, axis=-1, keepdims=True))
                probs = expo * (1.0 / jnp.sum(expo, axis=-1, keepdims=True))
                grad_probs = dot_nt(grad_head, vd_ref[keys, cols])
                delta = jnp.sum(probs * grad_probs, axis=-1, keepdims=True)
                grad_scores = (probs * (grad_probs - delta)).astype(bf16)
                grad_queries.append(dot(grad_scores, kd_ref[keys, cols]))
                dk_sc[keys, cols] += dot_tn(grad_scores, query)
                dv_sc[keys, cols] += dot_tn(probs.astype(bf16), grad_head)
            grad_query = jnp.where(low, grad_queries[0], grad_queries[1]) * score_scale
            grad_query = grad_query * cosine - swap_halves(grad_query, first) * sine
            proj_sc[rows, group * GROUP_COLS : group * GROUP_COLS + LANES] = grad_query.astype(bf16)

    for_blocks(length // ROW_BLOCK, attend)
    gain_grad_ref[...] = jnp.zeros_like(gain_grad_ref)

    def finish(rows, part, inner, x_piece):
        cosine = cos_ref[rows, :]
        sine = sin_ref[rows, :]
        for group in range(groups):
            cols = slice(group * LANES, (group + 1) * LANES)
            grad_key = dk_sc[rows, cols]
            grad_key = grad_key + pltpu.roll(grad_key, HEAD_SIZE, 1)
            grad_key = grad_key * cosine - swap_halves(grad_key, first) * sine
            grad_value = dv_sc[rows, cols]
            grad_value = grad_value + pltpu.roll(grad_value, HEAD_SIZE, 1)
            proj_sc[rows, group * GROUP_COLS + LANES : (group + 1) * GROUP_COLS] = jnp.where(
                low, grad_key, grad_value
            ).astype(bf16)
        grad_normed = dot_nt(proj_sc[rows, :], weights_ref[:, :split])
        x = x_piece[inner, :].astype(f32)
        unit = x * lax.rsqrt(jnp.mean(x * x, axis=-1, keepdims=True) + epsilon)
        norm_sc[rows, :] = (unit * gain_ref[...]).astype(bf16)
        gain_grad_ref[...] += jnp.sum(grad_normed * unit, axis=0, keepdims=True)
        part[inner, :] = grad_normed.astype(bf16)

    if count > 1:
        for (rows, part, inner), x_piece in zip(each_block(starts_ref, parts), x_pieces):
            finish(rows, part, inner, x_piece)
    else:

        def whole_step(index):
            finish(block_rows(index), parts[0], block_rows(index), x_pieces[0])

        for_blocks(length // ROW_BLOCK, whole_step)
    grad_ref[:, :split] = dot_tn(norm_sc[...], proj_sc[...]).astype(bf16)
    grad_ref[:, split:] = dot_tn(gb_ref[...], ctx_ref[...]).astype(bf16)


def attention_backward(
    starts, pieces, gain, weights, cosine, sine, seg_col, seg_row, kept, grad_pieces
):
    length = cosine.shape[0]
    count = len(pieces)
    heads = weights.shape[1] // 3
    results = pl.pallas_call(
        functools.partial(attention_backward_body, count=count),
        out_shape=tuple(jax.ShapeDtypeStruct(p.shape, bf16) for p in pieces)
        + (
            jax.ShapeDtypeStruct(weights.shape, bf16),
            jax.ShapeDtypeStruct((1, MODEL_WIDTH), f32),
        ),
        in_specs=in_vmem(2 * count + 11),
        scratch_shapes=[
            pltpu.VMEM((length, MODEL_WIDTH), bf16),
            pltpu.VMEM((length, MODEL_WIDTH), bf16),
            pltpu.VMEM((length, 2 * heads), bf16),
            pltpu.VMEM((length, heads), f32),
            pltpu.VMEM((length, heads), f32),
        ],
        compiler_params=params,
        name="attn_bwd",
    )(starts, *pieces, gain, weights, cosine, sine, seg_col, seg_row, *kept, *grad_pieces)
    return results[:count], results[count:]


def dispatch_body(order_ref, x_ref, router_ref, *refs, local):
    gm_pieces, (xd_ref, gd_ref, pt_ref, pgt_ref, gm_ref) = refs[:-5], refs[-5:]
    rows = x_ref.shape[0]
    for index, piece in enumerate(gm_pieces):

        @pl.when(pl.program_id(0) == index)
        def _(piece=piece):
            gm_ref[...] = piece[...]

    slots = local * CAP
    x = x_ref[...]
    mask = gm_ref[:, MODEL_WIDTH:]
    chosen = mask.astype(f32) > 0.0
    logits = jnp.where(chosen, dot(x, router_ref[...]), masked_score)
    expo = jnp.where(chosen, jnp.exp(logits - jnp.max(logits, axis=-1, keepdims=True)), 0.0)
    gates = (expo / jnp.sum(expo, axis=-1, keepdims=True)).astype(bf16)
    earlier = lax.broadcasted_iota(jnp.int32, (rows, rows), 1) < lax.broadcasted_iota(
        jnp.int32, (rows, rows), 0
    )
    place = dot(jnp.where(earlier, 1.0, 0.0).astype(bf16), mask)
    place = jnp.where(chosen, place, -1.0).astype(bf16)
    offset = order_ref[pl.num_programs(0)]

    def pick(shape, slot_axis):
        slot = lax.broadcasted_iota(jnp.int32, shape, slot_axis)
        expert = lax.broadcasted_iota(jnp.int32, shape, 1 - slot_axis)
        hit = jnp.zeros(shape, jnp.bool_)
        for own in range(local):
            hit = hit | (
                (slot >= own * CAP) & (slot < (own + 1) * CAP) & (expert == offset + own)
            )
        return jnp.where(hit, 1.0, 0.0).astype(bf16)

    def in_slot(shape, slot_axis):
        slot = lax.broadcasted_iota(jnp.int32, shape, slot_axis)
        for own in range(1, local):
            slot = jnp.where(slot >= CAP, slot - CAP, slot)
        return slot.astype(f32)

    spread = pick((slots, LANES), 0)
    hit = dot_nt(spread, place) == in_slot((slots, rows), 0)
    send = jnp.where(hit, 1.0, 0.0).astype(bf16)
    send_gated = jnp.where(hit, dot_nt(spread, gates), 0.0).astype(bf16)
    xd_ref[...] = dot(send, x).astype(bf16).reshape(xd_ref.shape)
    gd_ref[...] = (
        (dot(send_gated, gm_ref[:, :MODEL_WIDTH]) * residual_scale).astype(bf16)
    ).reshape(gd_ref.shape)
    spread = pick((LANES, slots), 1)
    hit = dot(place, spread) == in_slot((rows, slots), 1)
    pt_ref[...] = jnp.where(hit, 1.0, 0.0).astype(bf16)
    pgt_ref[...] = jnp.where(hit, dot(gates, spread), 0.0).astype(bf16)


def dispatch(order, x, gm_pieces, router, local):
    blocks = x.shape[0] // ROW_BLOCK
    slots = local * CAP
    slotted = jax.ShapeDtypeStruct((local, blocks, CAP, MODEL_WIDTH), bf16)
    slotted_spec = pl.BlockSpec((local, 1, CAP, MODEL_WIDTH), lambda s, o: (0, o[s], 0, 0))
    return pl.pallas_call(
        functools.partial(dispatch_body, local=local),
        grid_spec=pltpu.PrefetchScalarGridSpec(
            num_scalar_prefetch=1,
            grid=(blocks,),
            in_specs=[
                pl.BlockSpec((ROW_BLOCK, MODEL_WIDTH), lambda s, o: (o[s], 0)),
                pl.BlockSpec((MODEL_WIDTH, LANES), lambda s, o: (0, 0)),
            ]
            + [pl.BlockSpec((ROW_BLOCK, MODEL_WIDTH + LANES), lambda s, o: (0, 0))]
            * len(gm_pieces),
            out_specs=[
                slotted_spec,
                slotted_spec,
                pl.BlockSpec((ROW_BLOCK, slots), lambda s, o: (o[s], 0)),
                pl.BlockSpec((ROW_BLOCK, slots), lambda s, o: (o[s], 0)),
            ],
            scratch_shapes=[pltpu.VMEM((ROW_BLOCK, MODEL_WIDTH + LANES), bf16)],
        ),
        out_shape=(
            slotted,
            slotted,
            jax.ShapeDtypeStruct((x.shape[0], slots), bf16),
            jax.ShapeDtypeStruct((x.shape[0], slots), bf16),
        ),
        compiler_params=row_params,
        name="dispatch",
    )(order, x, router, *gm_pieces)


def experts_body(place_ref, *refs, count, carried):
    xd_ref, gd_ref, refs = refs[0], refs[1], refs[2:]
    tables = count + 1 if count > 1 else count
    gu_pieces, d_pieces, refs = refs[:tables], refs[tables : 2 * tables], refs[2 * tables :]
    old, refs = (refs[: 2 * count], refs[2 * count :]) if carried else ((), refs)
    out_ref, dx_ref, h_ref = refs[:3]
    dgu_refs, dd_refs = refs[3 : 3 + count], refs[3 + count : 3 + 2 * count]
    wgu_ref, wd_ref, act_sc, dh_sc = refs[3 + 2 * count :]
    expert = pl.program_id(0)
    half = pl.num_programs(0) // 2

    def starts(index, rows):
        return pl.multiple_of(place_ref[1 + index] * rows, LANES)

    def put(index, gu_piece, d_piece):
        rows = gu_piece.shape[1]
        begin = starts(index, rows)
        wgu_ref[pl.ds(begin, rows), :] = gu_piece[0]
        wd_ref[:, pl.ds(begin, rows)] = d_piece[0]

    for index in range(min(count, 3)):
        put(index, gu_pieces[index], d_pieces[index])
    if count > 1:

        @pl.when(expert < half)
        def _():
            put(3, gu_pieces[3], d_pieces[3])

        @pl.when(expert >= half)
        def _():
            put(3, gu_pieces[4], d_pieces[4])

    total = xd_ref.shape[1]
    chunk = ROW_BLOCK
    own = place_ref[0] + expert
    lane = lax.broadcasted_iota(jnp.int32, (chunk, LANES), 1)

    def chunk_step(index):
        rows = block_rows(index)
        hidden = dot(xd_ref[0, rows, :], wgu_ref[...])
        gate = hidden[:, :FF]
        up = hidden[:, FF:]
        sigmoid = jax.nn.sigmoid(gate)
        act = (gate * sigmoid * up).astype(bf16)
        act_sc[rows, :] = act
        out = dot(act, wd_ref[...]).astype(bf16)
        out_ref[0, rows, :] = out
        grad_out = gd_ref[0, rows, :]
        h = jnp.sum(grad_out.astype(f32) * out.astype(f32), axis=-1, keepdims=True)
        h_ref[0, rows, :] = jnp.where(lane == own, h, 0.0).astype(bf16)
        grad_act = dot_nt(grad_out, wd_ref[...])
        grad_gate = grad_act * up * sigmoid * (1.0 + gate * (1.0 - sigmoid))
        grad_up = grad_act * gate * sigmoid
        dh_sc[rows, :FF] = grad_gate.astype(bf16)
        dh_sc[rows, FF:] = grad_up.astype(bf16)
        dx_ref[0, rows, :] = dot_nt(dh_sc[rows, :], wgu_ref[...]).astype(bf16)

    for_blocks(total // chunk, chunk_step)
    for index in range(count):
        rows = dgu_refs[index].shape[1]
        begin = starts(index, rows)
        grad_down = dot_tn(act_sc[...], gd_ref[0, :, pl.ds(begin, rows)])
        grad_gate_up = dot_tn(xd_ref[0, :, pl.ds(begin, rows)], dh_sc[...])
        if carried:
            grad_gate_up = grad_gate_up + old[index][0].astype(f32)
            grad_down = grad_down + old[count + index][0].astype(f32)
        dgu_refs[index][0] = grad_gate_up.astype(bf16)
        dd_refs[index][0] = grad_down.astype(bf16)


def run_experts(place, xd, gd, gu_pieces, d_pieces, old):
    local, total = xd.shape[:2]
    count = place.shape[0] - 1
    rows = MODEL_WIDTH // count

    def spec(a, b):
        return pl.BlockSpec((1, a, b), lambda e, o: (e, 0, 0))

    def piece_specs(a, b):
        half = local // 2
        specs = [spec(a, b)] * min(count, 3)
        if count > 1:
            specs.append(pl.BlockSpec((1, a, b), lambda e, o: (jnp.minimum(e, half - 1), 0, 0)))
            specs.append(pl.BlockSpec((1, a, b), lambda e, o: (jnp.maximum(e - half, 0), 0, 0)))
        return specs

    row_spec = spec(total, MODEL_WIDTH)
    grad_specs = [spec(rows, 2 * FF)] * count + [spec(FF, rows)] * count
    results = pl.pallas_call(
        functools.partial(experts_body, count=count, carried=bool(old)),
        grid_spec=pltpu.PrefetchScalarGridSpec(
            num_scalar_prefetch=1,
            grid=(local,),
            in_specs=[row_spec, row_spec]
            + piece_specs(rows, 2 * FF)
            + piece_specs(FF, rows)
            + (grad_specs if old else []),
            out_specs=[row_spec, row_spec, spec(total, LANES)] + grad_specs,
            scratch_shapes=[
                pltpu.VMEM((MODEL_WIDTH, 2 * FF), bf16),
                pltpu.VMEM((FF, MODEL_WIDTH), bf16),
                pltpu.VMEM((total, FF), bf16),
                pltpu.VMEM((total, 2 * FF), bf16),
            ],
        ),
        out_shape=(
            jax.ShapeDtypeStruct((local, total, MODEL_WIDTH), bf16),
            jax.ShapeDtypeStruct((local, total, MODEL_WIDTH), bf16),
            jax.ShapeDtypeStruct((local, total, LANES), bf16),
        )
        + (jax.ShapeDtypeStruct((local, rows, 2 * FF), bf16),) * count
        + (jax.ShapeDtypeStruct((local, FF, rows), bf16),) * count,
        compiler_params=row_params,
        name="experts",
    )(place, xd, gd, *gu_pieces, *d_pieces, *old)
    return results[:3], results[3:]


def combine_body(out_ref, dx_ref, h_ref, pt_ref, pgt_ref, mix_ref, grad_ref):
    slots = pt_ref.shape[1]
    mix_ref[...] = dot(pgt_ref[...], out_ref[...].reshape(slots, MODEL_WIDTH)).astype(bf16)
    grad_ref[:, :MODEL_WIDTH] = dot(
        pt_ref[...], dx_ref[...].reshape(slots, MODEL_WIDTH)
    ).astype(bf16)
    grad_ref[:, MODEL_WIDTH:] = dot(pt_ref[...], h_ref[...].reshape(slots, LANES)).astype(bf16)


def combine(out, dx, h, pt, pgt):
    local = out.shape[0]
    blocks = pt.shape[0] // ROW_BLOCK
    slots = pt.shape[1]

    def slotted(array):
        return array.reshape(local, blocks, CAP, array.shape[-1])

    def spec(width):
        return pl.BlockSpec((local, 1, CAP, width), lambda s: (0, s, 0, 0))

    def row_spec(width):
        return pl.BlockSpec((ROW_BLOCK, width), lambda s: (s, 0))

    return pl.pallas_call(
        combine_body,
        grid=(blocks,),
        in_specs=[
            spec(MODEL_WIDTH), spec(MODEL_WIDTH), spec(LANES), row_spec(slots), row_spec(slots)
        ],
        out_specs=[row_spec(MODEL_WIDTH), row_spec(MODEL_WIDTH + LANES)],
        out_shape=(
            jax.ShapeDtypeStruct((pt.shape[0], MODEL_WIDTH), bf16),
            jax.ShapeDtypeStruct((pt.shape[0], MODEL_WIDTH + LANES), bf16),
        ),
        compiler_params=row_params,
        name="combine",
    )(slotted(out), slotted(dx), slotted(h), pt, pgt)


def flip(value, bits):
    return lax.ppermute(value, "tp", [(t, t ^ bits) for t in range(4)])


def square():
    return lax.axis_size("tp") == 4


def tp_places():
    me = lax.axis_index("tp").astype(jnp.int32)
    if square():
        return jnp.stack([me ^ bits for bits in range(4)])
    return jnp.zeros((1,), jnp.int32)


def gather_rows(value):
    if square():
        return [value] + [flip(value, bits) for bits in (1, 2, 3)]
    return [lax.all_gather(value, "tp", axis=0, tiled=True)]


def sum_rows(parts):
    if square():
        total = parts[0].astype(f32)
        for bits in (1, 2, 3):
            total = total + flip(parts[bits], bits).astype(f32)
        return total
    return lax.psum_scatter(parts[0], "tp", scatter_dimension=0, tiled=True).astype(f32)


def gather_weights(value, axis):
    if square():
        half = value.shape[0] // 2
        along_x = flip(value, 1)
        along_y = flip(value, 2)
        return [value, along_x, along_y, flip(along_y[:half], 1), flip(along_x[half:], 2)]
    return [lax.all_gather(value, "tp", axis=axis, tiled=True)]


def sum_weights(parts, axis):
    if square():
        half = parts[0].shape[0] // 2
        wide = [p.astype(f32) for p in parts]
        top = flip(parts[1][:half], 1) + wide[0][:half]
        top_far = flip(parts[3][:half], 1) + wide[2][:half]
        low = flip(parts[2][half:], 2) + wide[0][half:]
        low_far = flip(parts[3][half:], 2) + wide[1][half:]
        top = top + flip(top_far.astype(bf16), 2)
        low = low + flip(low_far.astype(bf16), 1)
        return jnp.concatenate([top, low])
    return lax.psum_scatter(parts[0], "tp", scatter_dimension=axis, tiled=True).astype(f32)


def ring_devices():
    size = lax.axis_size("ep")
    return [2 * r if 2 * r < size else 2 * (size - 1 - r) + 1 for r in range(size)]


def ring_order():
    size = lax.axis_size("ep")
    devices = ring_devices()
    table = []
    for me in range(size):
        at = devices.index(me)
        steps = [0]
        for step in range(1, size // 2 + 1):
            steps.append(-step)
            if step < size // 2:
                steps.append(step)
        table.append([devices[(at + step) % size] for step in steps])
    return jnp.asarray(table, jnp.int32)[lax.axis_index("ep")]


def ring_gather(value):
    size = lax.axis_size("ep")
    devices = ring_devices()
    ahead = [(devices[r], devices[(r + 1) % size]) for r in range(size)]
    back = [(b, a) for a, b in ahead]
    pieces = [value]
    left = right = value
    for step in range(1, size // 2 + 1):
        left = lax.ppermute(left, "ep", ahead)
        pieces.append(left)
        if step < size // 2:
            right = lax.ppermute(right, "ep", back)
            pieces.append(right)
    return pieces


def ag_ep(value, axis=0):
    return lax.all_gather(value, "ep", axis=axis, tiled=True)


def rs_ep(value, axis=0):
    return lax.psum_scatter(value, "ep", scatter_dimension=axis, tiled=True)


def rope_tables(segment_row):
    onehot = (segment_row[:, None] == jnp.arange(DOCS, dtype=jnp.int32)[None, :]).astype(jnp.int32)
    doc_len = jnp.sum(onehot, axis=0)
    starts = [jnp.sum(doc_len[:doc]) for doc in range(DOCS)]
    begin = jnp.zeros_like(segment_row)
    for doc in range(1, DOCS):
        begin = jnp.where(segment_row == doc, starts[doc], begin)
    positions = jnp.arange(segment_row.shape[0], dtype=jnp.int32) - begin
    lane = jnp.arange(LANES, dtype=jnp.int32)
    halves = HEAD_SIZE // 2
    freqs = rope_base ** (-((lane % halves).astype(f32) * 2.0) / HEAD_SIZE)
    angles = positions.astype(f32)[:, None] * freqs[None, :]
    sign = jnp.where((lane % HEAD_SIZE) < halves, -1.0, 1.0).astype(f32)
    return jnp.cos(angles), jnp.sin(angles) * sign[None, :]


def shards(
    tokens,
    cotangent,
    norm_gains,
    query_key_value_weight,
    output_weight,
    w_router,
    w_gate_up,
    w_down,
    segment_ids,
    routes,
):
    micro, rows = tokens.shape[:2]
    local_heads = query_key_value_weight.shape[1]
    local = w_gate_up.shape[0]
    ep_size = lax.axis_size("ep")
    offset = (lax.axis_index("ep") * local).astype(jnp.int32).reshape(1)
    places = tp_places()
    starts = places * ROW_BLOCK
    place = jnp.concatenate([offset, places])
    gain_one = norm_gains[0:1]
    gain_two = norm_gains[1:2]
    router = jnp.pad(w_router, ((0, 0), (0, LANES - EXPERTS)))

    order = jnp.concatenate([ring_order(), offset])

    weights = ag_ep(
        jnp.concatenate(
            [
                query_key_value_weight.reshape(query_key_value_weight.shape[0], -1),
                output_weight.reshape(-1, output_weight.shape[2]).T,
            ],
            axis=1,
        )
    )
    token_full = [gather_rows(tokens[m]) for m in range(micro)]
    lanes = jnp.arange(LANES, dtype=jnp.int32)
    masks = jnp.any(
        routes.reshape(micro, rows, -1)[..., None] == lanes, axis=2
    ).astype(bf16)
    gm_full = [ring_gather(jnp.concatenate([cotangent[m], masks[m]], axis=-1)) for m in range(micro)]
    gu_pieces = gather_weights(w_gate_up, 1)
    d_pieces = gather_weights(w_down, 2)

    tables = [rope_tables(segment_ids[m]) for m in range(micro)]
    fixed = []
    for m in range(micro):
        fixed.append(
            (
                starts, token_full[m], gain_one, weights, tables[m][0], tables[m][1],
                segment_ids[m][:, None], segment_ids[m][None, :],
            )
        )

    kept = []
    hiddens = []
    normed_twos = []
    scales = []
    gate_rows = []
    for m in range(micro):
        parts, saved = attention_forward(*fixed[m])
        kept.append(saved)
        branch = sum_rows(parts)
        hidden = tokens[m].astype(f32) + residual_scale * branch
        scale_two = lax.rsqrt(jnp.mean(hidden * hidden, axis=-1, keepdims=True) + epsilon)
        normed_two = (hidden * scale_two * gain_two).astype(bf16)
        logits = jnp.where(masks[m] > 0, dot(normed_two, router), masked_score)
        expo = jnp.where(
            masks[m] > 0, jnp.exp(logits - jnp.max(logits, axis=-1, keepdims=True)), 0.0
        )
        gate_rows.append(expo / jnp.sum(expo, axis=-1, keepdims=True))
        hiddens.append(hidden)
        normed_twos.append(normed_two)
        scales.append(scale_two)

    old = ()
    mixes = []
    outputs = []
    input_grads = []
    acc_router = 0.0
    acc_gain_one = 0.0
    acc_gain_two = 0.0
    acc_weights = 0.0
    for m in range(micro):
        x_full = ag_ep(normed_twos[m])
        xd, gd, pt, pgt = dispatch(order, x_full, gm_full[m], router, local)
        merged = (local, ep_size * CAP, MODEL_WIDTH)
        (out, dx, h), old = run_experts(
            place, xd.reshape(merged), gd.reshape(merged), gu_pieces, d_pieces, old
        )
        mix, grad = combine(out, dx, h, pt, pgt)
        grad = rs_ep(grad).astype(f32)
        mixes.append(mix)

        h_rows = grad[:, MODEL_WIDTH:]
        grad_logits = (
            h_rows - gate_rows[m] * jnp.sum(h_rows, axis=-1, keepdims=True)
        ).astype(bf16)
        acc_router = acc_router + dot_tn(normed_twos[m], grad_logits)
        grad_normed = grad[:, :MODEL_WIDTH] + dot_nt(grad_logits, router)
        scale = scales[m]
        weighted = grad_normed * gain_two
        inner = jnp.mean(weighted * hiddens[m], axis=-1, keepdims=True)
        grad_hidden = (
            cotangent[m].astype(f32)
            + scale * weighted
            - hiddens[m] * scale * scale * scale * inner
        )
        acc_gain_two = acc_gain_two + jnp.sum(grad_normed * hiddens[m] * scale, axis=0)
        grad_branch = gather_rows((residual_scale * grad_hidden).astype(bf16))
        parts, (gweights, ggain) = attention_backward(*fixed[m], kept[m], grad_branch)
        acc_weights = acc_weights + gweights.astype(f32)
        acc_gain_one = acc_gain_one + ggain[0]
        grad_normed = sum_rows(parts)
        inputs = tokens[m].astype(f32)
        scale = lax.rsqrt(jnp.mean(inputs * inputs, axis=-1, keepdims=True) + epsilon)
        weighted = grad_normed * gain_one
        inner = jnp.mean(weighted * inputs, axis=-1, keepdims=True)
        input_grads.append(
            grad_hidden + scale * weighted - inputs * scale * scale * scale * inner
        )

    for m in range(micro):
        mix, _ = lax.optimization_barrier((mixes[m], grad))
        mix = rs_ep(mix).astype(f32)
        outputs.append((hiddens[m] + residual_scale * mix).astype(bf16))

    count = places.shape[0]
    grad_gate_up = sum_weights(old[:count], 1)
    grad_down = sum_weights(old[count:], 2)

    small = jnp.concatenate(
        [
            acc_router[:, :EXPERTS],
            acc_gain_one[:, None],
            acc_gain_two[:, None],
            jnp.zeros((MODEL_WIDTH, LANES - EXPERTS - 2), f32),
        ],
        axis=-1,
    ).astype(bf16)
    rows = MODEL_WIDTH // lax.axis_size("tp")
    if square():
        small = sum_rows(
            [lax.dynamic_slice_in_dim(small, places[k] * rows, rows) for k in range(4)]
        ).astype(bf16)
    else:
        small = lax.psum_scatter(small, "tp", scatter_dimension=0, tiled=True)
    columns = acc_weights.shape[1]
    own_rows = MODEL_WIDTH // ep_size
    small_rows = rows // ep_size
    small = small.reshape(ep_size, small_rows * LANES)
    extra = -(-small.shape[1] // (8 * columns)) * 8
    small = jnp.pad(small, ((0, 0), (0, extra * columns - small.shape[1])))
    packed = jnp.concatenate(
        [
            acc_weights.astype(bf16).reshape(ep_size, own_rows, columns),
            small.reshape(ep_size, extra, columns),
        ],
        axis=1,
    )
    summed = rs_ep(packed.reshape(-1, columns)).astype(f32)
    split = local_heads * GROUP_COLS
    grad_qkv = summed[:own_rows, :split].reshape(own_rows, local_heads, GROUP_COLS)
    grad_out = summed[:own_rows, split:].T.reshape(local_heads, LANES, own_rows)
    small = summed[own_rows:].reshape(-1)[: small_rows * LANES].reshape(small_rows, LANES)
    grad_router = small[:, :EXPERTS]
    grad_gains = small[:, EXPERTS : EXPERTS + 2].T
    return (
        jnp.stack(outputs),
        jnp.stack(input_grads),
        grad_gains,
        grad_qkv,
        grad_out,
        grad_router,
        grad_gate_up,
        grad_down,
    )


def solution(mesh):
    placed = (
        P("ep", "tp", None),
        P("ep", "tp", None),
        P(),
        P("ep", "tp", None),
        P("tp", None, "ep"),
        P(),
        P("ep", "tp", None),
        P("ep", None, "tp"),
        P("ep", None),
        P("ep", "tp", None, None),
    )
    return jax.shard_map(
        shards,
        mesh=mesh,
        in_specs=placed,
        out_specs=(
            P("ep", "tp", None),
            P("ep", "tp", None),
            P(None, ("tp", "ep")),
            P("ep", "tp", None),
            P("tp", None, "ep"),
            P(("tp", "ep"), None),
            P("ep", "tp", None),
            P("ep", None, "tp"),
        ),
        check_vma=False,
    )
```

time: 2010 us -> 835 us (0.42)
  waiting for transfers between devices: 1280 us -> 402 us
  matrix products: 264 us -> 4.22 us
  Pallas kernels: 0 us -> 217 us
  local copies, waits for them, and re-layouts: 210 us -> 32.1 us
  other arithmetic: 149 us -> 57.9 us
  starting transfers between devices: 40 us -> 94.2 us
  blocking collectives: 20.4 us -> 0 us
    all_to_all x8 -> x0, waiting for transfers between devices: 899 us -> none  [the longest x2 243 us: shards(): lax.all_to_all(outgoing.reshape(ep_size, local_experts, CAP, MODEL_WIDTH)...]
    dot_general x58 -> x6, matrix products: 264 us -> 4.22 us  [the longest x2 1.91 us: dot(): return jnp.dot(a, b, preferred_element_type=f32)]
    ppermute x0 -> x61, waiting for transfers between devices: none -> 230 us  [the longest x47 125 us: flip(): return lax.ppermute(value, 'tp', [(t, t ^ bits) for t in range(4)])]
    pallas_call x0 -> x10, Pallas kernels: none -> 217 us  [the longest x2 84.9 us: run_experts(): pl.pallas_call(functools.partial(experts_body, count=count, carried=bool(...]
    ppermute x0 -> x61, starting transfers between devices: none -> 93.7 us  [the longest x47 58.5 us: flip(): return lax.ppermute(value, 'tp', [(t, t ^ bits) for t in range(4)])]
    all_gather x7 -> x3, waiting for transfers between devices: 92.2 us -> 0.04 us  [ag_ep(): return lax.all_gather(value, 'ep', axis=axis, tiled=True)]
    reduce_scatter x8 -> x5, waiting for transfers between devices: 237 us -> 170 us  [rs_ep(): return lax.psum_scatter(value, 'ep', scatter_dimension=axis, tiled=True)]
    gather x4 -> x0, local copies, waits for them, and re-layouts: 58.1 us -> none  [the longest x2 29.1 us: shards(): returned.reshape(EXPERTS * CAP, MODEL_WIDTH)[slots]]
  transfers between devices with their start and end apart: 27 -> 69, of which waited for: 20 -> 31; matrix products, arithmetic and copies ran while one was open for 25% -> 10% of each run, Pallas kernels for 0% -> 15%
where the time goes in v1:
time: 835 us; the launch traced here: 823 us
  waiting for transfers between devices  402 us (48%)
  Pallas kernels  217 us (26%)
  starting transfers between devices  94.2 us (11%)
  other arithmetic  57.9 us (7%)
  local copies, waits for them, and re-layouts  32.1 us (4%)
  between operations  15.5 us (2%)
    reduce_scatter x5, waiting for transfers between devices, rs_ep(): return lax.psum_scatter(value, 'ep', scatter_dimension=axis, tiled=True)  170 us
    ppermute x47, waiting for transfers between devices, flip(): return lax.ppermute(value, 'tp', [(t, t ^ bits) for t in range(4)])  125 us
    pallas_call x2, Pallas kernels, run_experts(): pl.pallas_call(functools.partial(experts_body, count=count, carried=bool(...  84.9 us
    ppermute x8, waiting for transfers between devices, ring_gather(): left = lax.ppermute(left, 'ep', ahead)  71.6 us
    ppermute x47, starting transfers between devices, flip(): return lax.ppermute(value, 'tp', [(t, t ^ bits) for t in range(4)])  58.5 us
    pallas_call x2, Pallas kernels, attention_backward(): pl.pallas_call(functools.partial(attention_backward_body, count=count), o...  47.4 us
    ppermute x8, starting transfers between devices, ring_gather(): left = lax.ppermute(left, 'ep', ahead)  35.2 us
    ppermute x6, waiting for transfers between devices, ring_gather(): right = lax.ppermute(right, 'ep', back)  34 us
  transfers between devices with their start and end apart: 69, of which 31 were waited for; matrix products, arithmetic and copies ran while one was open for 10% of the time, Pallas kernels for 15%

profile of v1, /device:TPU:0, one launch (start us, length us, event | category | flops | bytes accessed | tf_op | source)
XLA Modules:
  0.0 822.9 jit_solution(16594118907945998593)
XLA Ops:
  31.3 8.9 %collective-permute-done.1.refs_2_ = bf16[256,1024]{1,0:T(8,128)(2,1)S(1)} collective-permute-done((bf16[256,1024]{1,0:T(8,128)(2,1)S(1)}, bf16[256,1024]{1,0:T(8,128)(2,1)S(1)}, u32[]{:S(2)}, u32[]{:S(2)}) %collective-permute-start.1) | collective-permute-done | bytes 524320 | tf_op jit(solution)/shard_map/ppermute | solution.py:540
  41.2 14.4 %attn_fwd.2 = (bf16[256,1024]{1,0:T(8,128)(2,1)}, bf16[256,1024]{1,0:T(8,128)(2,1)}, bf16[256,1024]{1,0:T(8,128)(2,1)}, bf16[256,1024]{1,0:T(8,128)(2,1)}, bf16[...) custom-call(s32[4]{0:T(128)} %add_multiply_fusion.2.starts_ref, ...), custom_call_target="tpu_custom_call" | custom-call | tf_op jit(solution)/shard_map/attn_fwd/pallas_call | solution.py:172
  60.2 12.8 %collective-permute-done.22.refs_2_ = bf16[256,1024]{1,0:T(8,128)(2,1)} collective-permute-done((bf16[256,1024]{1,0:T(8,128)(2,1)S(1)}, bf16[256,1024]{1,0:T(8,128)(2,1)}, u32[]{:S(2)}, u32[]{:S(2)}) %collective-permute-start.22) | collective-permute-done | bytes 524320 | tf_op jit(solution)/shard_map/ppermute | solution.py:540
  72.9 14.7 %attn_fwd.3 = (bf16[256,1024]{1,0:T(8,128)(2,1)}, bf16[256,1024]{1,0:T(8,128)(2,1)}, bf16[256,1024]{1,0:T(8,128)(2,1)}, bf16[256,1024]{1,0:T(8,128)(2,1)}, bf16[...) custom-call(s32[4]{0:T(128)} %add_multiply_fusion.2.starts_ref, ...), custom_call_target="tpu_custom_call" | custom-call | tf_op jit(solution)/shard_map/attn_fwd/pallas_call | solution.py:172
  91.8 8.8 %collective-permute-done.26 = bf16[256,1024]{1,0:T(8,128)(2,1)S(1)} collective-permute-done((bf16[256,1024]{1,0:T(8,128)(2,1)}, bf16[256,1024]{1,0:T(8,128)(2,1)S(1)}, u32[]{:S(2)}, u32[]{:S(2)}) %collective-permute-start.26) | collective-permute-done | bytes 524320 | tf_op jit(solution)/shard_map/ppermute | solution.py:540
  120.0 22.3 %collective-permute-done.6.refs_1_ = bf16[256,1152]{1,0:T(8,128)(2,1)S(1)} collective-permute-done((bf16[256,1152]{1,0:T(8,128)(2,1)S(1)}, bf16[256,1152]{1,0:T(8,128)(2,1)S(1)}, u32[]{:S(2)}, u32[]{:S(2)}) %collective-permute-start.6) | collective-permute-done | bytes 589856 | tf_op jit(solution)/shard_map/ppermute | solution.py:620
  143.2 15.1 %collective-permute-done.7.refs_2_ = bf16[256,1152]{1,0:T(8,128)(2,1)S(1)} collective-permute-done((bf16[256,1152]{1,0:T(8,128)(2,1)S(1)}, bf16[256,1152]{1,0:T(8,128)(2,1)S(1)}, u32[]{:S(2)}, u32[]{:S(2)}) %collective-permute-start.7) | collective-permute-done | bytes 589856 | tf_op jit(solution)/shard_map/ppermute | solution.py:623
  165.9 6.6 collective-permute-start.8
  172.5 6.1 collective-permute-done.28.refs_2_
  180.6 9.1 %collective-permute-done.8.refs_3_ = bf16[256,1152]{1,0:T(8,128)(2,1)S(1)} collective-permute-done((bf16[256,1152]{1,0:T(8,128)(2,1)S(1)}, bf16[256,1152]{1,0:T(8,128)(2,1)S(1)}, u32[]{:S(2)}, u32[]{:S(2)}) %collective-permute-start.8) | collective-permute-done | bytes 589856 | tf_op jit(solution)/shard_map/ppermute | solution.py:620
  194.1 16.0 %collective-permute-done.29.refs_3_ = bf16[256,1152]{1,0:T(8,128)(2,1)S(1)} collective-permute-done((bf16[256,1152]{1,0:T(8,128)(2,1)S(1)}, bf16[256,1152]{1,0:T(8,128)(2,1)S(1)}, u32[]{:S(2)}, u32[]{:S(2)}) %collective-permute-start.29) | collective-permute-done | bytes 589856 | tf_op jit(solution)/shard_map/ppermute | solution.py:620
  210.1 10.9 %collective-permute-start.10 = (bf16[256,1152]{1,0:T(8,128)(2,1)S(1)}, bf16[256,1152]{1,0:T(8,128)(2,1)S(1)}, u32[]{:S(2)}, u32[]{:S(2)}) collective-permute-start(bf16[256,1152]{1,0:T(8,128)(2,1)S(1)} %collective-permute-done.8.refs_3_), channel_id=1, source_target_pairs={{0,2},{2,4},{4,6},{6,7},{7,5},{5,3},{3,1},{1,0},{8,10},{10,12},{12... | collective-permute-start | bytes 1769480 | tf_op jit(solution)/shard_map/ppermute | solution.py:620
  221.0 5.7 collective-permute-done.30.refs_4_
  226.7 17.0 %collective-permute-done.10.refs_5_ = bf16[256,1152]{1,0:T(8,128)(2,1)S(1)} collective-permute-done((bf16[256,1152]{1,0:T(8,128)(2,1)S(1)}, bf16[256,1152]{1,0:T(8,128)(2,1)S(1)}, u32[]{:S(2)}, u32[]{:S(2)}) %collective-permute-start.10) | collective-permute-done | bytes 589856 | tf_op jit(solution)/shard_map/ppermute | solution.py:620
  243.8 6.9 collective-permute-start.31
  274.3 15.4 %dispatch.2 = (bf16[4,8,96,1024]{3,2,1,0:T(8,128)(2,1)}, bf16[4,8,96,1024]{3,2,1,0:T(8,128)(2,1)}, bf16[2048,384]{1,0:T(8,128)(2,1)}, bf16[2048,384]{1,0:T(8,128)(2,1)}) custom-call(s32[9]{0:T(128)} %pad_add_fusion.order_ref, bf16[2048,1024]{1,0:T(8,128)(2,1)} %all-gather.6.cloned.1.call-done.x_ref, bf16[1024,128]{1,0:T(8,128)(2,1)} %pad.8.router_ref, ...), custom_call_target="tpu_custom_call" | custom-call | tf_op jit(solution)/shard_map/dispatch/pallas_call | solution.py:352
  289.8 15.5 %dispatch.3 = (bf16[4,8,96,1024]{3,2,1,0:T(8,128)(2,1)}, bf16[4,8,96,1024]{3,2,1,0:T(8,128)(2,1)}, bf16[2048,384]{1,0:T(8,128)(2,1)}, bf16[2048,384]{1,0:T(8,128)(2,1)}) custom-call(s32[9]{0:T(128)} %pad_add_fusion.order_ref, bf16[2048,1024]{1,0:T(8,128)(2,1)} %all-gather.8.cloned.1.call-done.x_ref, bf16[1024,128]{1,0:T(8,128)(2,1)} %pad.8.router_ref, ...), custom_call_target="tpu_custom_call" | custom-call | tf_op jit(solution)/shard_map/dispatch/pallas_call | solution.py:352
  305.3 41.4 %experts.2 = (bf16[4,768,1024]{2,1,0:T(8,128)(2,1)}, bf16[4,768,1024]{2,1,0:T(8,128)(2,1)}, bf16[4,768,128]{2,1,0:T(8,128)(2,1)}, bf16[4,256,1024]{2,1,0:T(8,128...) custom-call(s32[5]{0:T(128)} %concatenate.30.place_ref, ...), custom_call_target="tpu_custom_call" | custom-call | tf_op jit(solution)/shard_map/experts/pallas_call | solution.py:470
  346.7 43.5 %experts.3 = (bf16[4,768,1024]{2,1,0:T(8,128)(2,1)}, bf16[4,768,1024]{2,1,0:T(8,128)(2,1)}, bf16[4,768,128]{2,1,0:T(8,128)(2,1)}, bf16[4,256,1024]{2,1,0:T(8,128...) custom-call(s32[5]{0:T(128)} %concatenate.30.place_ref, ...), custom_call_target="tpu_custom_call" | custom-call | tf_op jit(solution)/shard_map/experts/pallas_call | solution.py:470
  390.2 12.5 %combine.3 = (bf16[2048,1024]{1,0:T(8,128)(2,1)}, bf16[2048,1152]{1,0:T(8,128)(2,1)}) custom-call(bf16[4,8,96,1024]{3,2,1,0:T(8,128)(2,1)} %bitcast.123, bf16[4,8,96,1024]{3,2,1,0:T(8,128)(2,1)} %bitcast.124, bf16[4,8,96,128]{3,2,1,0:T(8,128)(2,1)} %bitcast.126, bf16[2048,384]{1,0:T(8,128)(2,1)} %get-tuple-element.103.pt_ref, ...), custom_call_target="tpu_custom_call" | custom-call | tf_op jit(solution)/shard_map/combine/pallas_call | solution.py:523
  402.8 12.5 %combine.2 = (bf16[2048,1024]{1,0:T(8,128)(2,1)}, bf16[2048,1152]{1,0:T(8,128)(2,1)}) custom-call(bf16[4,8,96,1024]{3,2,1,0:T(8,128)(2,1)} %bitcast.121, bf16[4,8,96,1024]{3,2,1,0:T(8,128)(2,1)} %bitcast.122, bf16[4,8,96,128]{3,2,1,0:T(8,128)(2,1)} %bitcast.125, bf16[2048,384]{1,0:T(8,128)(2,1)} %get-tuple-element.83.pt_ref, ...), custom_call_target="tpu_custom_call" | custom-call | tf_op jit(solution)/shard_map/combine/pallas_call | solution.py:523
  415.4 41.6 %reduce-scatter.6.cloned.1.call-done = bf16[256,1152]{1,0:T(8,128)(2,1)} async-done(((bf16[2048,1152]{1,0:T(8,128)(2,1)}), bf16[256,1152]{1,0:T(8,128)(2,1)}) %reduce-scatter.6.cloned.1.call-update) | async-done | bytes 589840 | tf_op jit(solution)/shard_map/reduce_scatter | solution.py:633
  480.7 31.9 %reduce-scatter.12.cloned.1.call-done = bf16[256,1152]{1,0:T(8,128)(2,1)} async-done(((bf16[2048,1152]{1,0:T(8,128)(2,1)}), bf16[256,1152]{1,0:T(8,128)(2,1)}) %reduce-scatter.12.cloned.1.call-update) | async-done | bytes 589840 | tf_op jit(solution)/shard_map/reduce_scatter | solution.py:633
  518.1 45.0 %reduce-scatter.10.cloned.1.call-done = bf16[256,1024]{1,0:T(8,128)(2,1)} async-done(((bf16[2048,1024]{1,0:T(8,128)(2,1)}), bf16[256,1024]{1,0:T(8,128)(2,1)}) %reduce-scatter.10.cloned.1.call-update) | async-done | bytes 524304 | tf_op jit(solution)/shard_map/reduce_scatter | solution.py:633
  563.1 51.3 %reduce-scatter.8.cloned.1.call-done = bf16[256,1024]{1,0:T(8,128)(2,1)} async-done(((bf16[2048,1024]{1,0:T(8,128)(2,1)}), bf16[256,1024]{1,0:T(8,128)(2,1)}) %reduce-scatter.8.cloned.1.call-update) | async-done | bytes 524304 | tf_op jit(solution)/shard_map/reduce_scatter | solution.py:633
  638.1 9.4 %collective-permute-done.41.refs_17_ = bf16[256,1024]{1,0:T(8,128)(2,1)S(1)} collective-permute-done((bf16[256,1024]{1,0:T(8,128)(2,1)}, bf16[256,1024]{1,0:T(8,128)(2,1)S(1)}, u32[]{:S(2)}, u32[]{:S(2)}) %collective-permute-start.41) | collective-permute-done | bytes 524320 | tf_op jit(solution)/shard_map/ppermute | solution.py:540
  650.1 23.6 %attn_bwd.3 = (bf16[256,1024]{1,0:T(8,128)(2,1)}, bf16[256,1024]{1,0:T(8,128)(2,1)}, bf16[256,1024]{1,0:T(8,128)(2,1)}, bf16[256,1024]{1,0:T(8,128)(2,1)}, bf16[1024,768]{1,0:T(8,128)(2,1)}, /*index=5*/f32[1,1024]{1,0:T(1,128)}) custom-call(s32[4]{0:T(128)} %add_multiply_fusion.2.starts_ref, bf16[256,1024]{1,0:T(8,128)(2,1)} %copy-done.12, ...), custom_call_target="tpu_custom_call" | custom-call | tf_op jit(solution)/shard_map/attn_bwd/pallas_call | solution.py:273
  676.7 23.8 %attn_bwd.2 = (bf16[256,1024]{1,0:T(8,128)(2,1)}, bf16[256,1024]{1,0:T(8,128)(2,1)}, bf16[256,1024]{1,0:T(8,128)(2,1)}, bf16[256,1024]{1,0:T(8,128)(2,1)}, bf16[1024,768]{1,0:T(8,128)(2,1)}, /*index=5*/f32[1,1024]{1,0:T(1,128)}) custom-call(s32[4]{0:T(128)} %add_multiply_fusion.2.starts_ref, bf16[256,1024]{1,0:T(8,128)(2,1)} %copy-done.11, ...), custom_call_target="tpu_custom_call" | custom-call | tf_op jit(solution)/shard_map/attn_bwd/pallas_call | solution.py:273
  720.8 26.4 %collective-permute-done.60 = bf16[2,512,256]{2,1,0:T(8,128)(2,1)S(1)} collective-permute-done((bf16[2,512,256]{2,1,0:T(8,128)(2,1)}, bf16[2,512,256]{2,1,0:T(8,128)(2,1)S(1)}, u32[]{:S(2)}, u32[]{:S(2)}) %collective-permute-start.60) | collective-permute-done | bytes 524320 | tf_op jit(solution)/shard_map/ppermute | solution.py:540
  756.3 12.9 %collective-permute-done.51 = bf16[2,256,1024]{2,1,0:T(8,128)(2,1)} collective-permute-done((bf16[2,256,1024]{2,1,0:T(8,128)(2,1)}, bf16[2,256,1024]{2,1,0:T(8,128)(2,1)}, u32[]{:S(2)}, u32[]{:S(2)}) %collective-permute-start.51) | collective-permute-done | bytes 1048608 | tf_op jit(solution)/shard_map/ppermute | solution.py:540
  771.5 9.4 %collective-permute-done.45 = bf16[256,1024]{1,0:T(8,128)(2,1)S(1)} collective-permute-done((bf16[256,1024]{1,0:T(8,128)(2,1)}, bf16[256,1024]{1,0:T(8,128)(2,1)S(1)}, u32[]{:S(2)}, u32[]{:S(2)}) %collective-permute-start.45) | collective-permute-done | bytes 524320 | tf_op jit(solution)/shard_map/ppermute | solution.py:540
  792.1 8.3 %collective-permute-done.39 = bf16[256,1024]{1,0:T(8,128)(2,1)S(1)} collective-permute-done((bf16[256,1024]{1,0:T(8,128)(2,1)S(1)}, bf16[256,1024]{1,0:T(8,128)(2,1)S(1)}, u32[]{:S(2)}, u32[]{:S(2)}) %collective-permute-start.39) | collective-permute-done | bytes 524320 | tf_op jit(solution)/shard_map/ppermute | solution.py:540
  (380 shorter events, 207.8 us)
Async XLA Ops:
  9.8 264.5 %all-gather.6.cloned.1.call-start = ((), (), s32[]{:S(2)}) async-start(), calls=%async_computation.6 | async-start | bytes 4718592 | tf_op jit(solution)/shard_map/all_gather | solution.py:629
  15.7 43.2 %collective-permute-start.21 = (bf16[256,1024]{1,0:T(8,128)(2,1)S(1)}, bf16[256,1024]{1,0:T(8,128)(2,1)S(1)}, u32[]{:S(2)}, u32[]{:S(2)}) collective-permute-start(bf16[256,1024]{1,0:T(8,128)(2,1)S(1)} %get-tuple-element.203.refs_0_), channel_id=1, source_target_pairs={{0,8},{8,0},{16,24},{24,16},{1,9},{9,1},{17,25},{25,17},{2,10},{10... | collective-permute-start | bytes 1572872 | tf_op jit(solution)/shard_map/ppermute | solution.py:540
  17.7 55.2 %collective-permute-start.22 = (bf16[256,1024]{1,0:T(8,128)(2,1)S(1)}, bf16[256,1024]{1,0:T(8,128)(2,1)}, u32[]{:S(2)}, u32[]{:S(2)}) collective-permute-start(bf16[256,1024]{1,0:T(8,128)(2,1)S(1)} %get-tuple-element.203.refs_0_), channel_id=1, source_target_pairs={{0,16},{8,24},{16,0},{24,8},{1,17},{9,25},{17,1},{25,9},{2,18},{10... | collective-permute-start | bytes 1572872 | tf_op jit(solution)/shard_map/ppermute | solution.py:540
  31.3 41.6 %collective-permute-start.23 = (bf16[256,1024]{1,0:T(8,128)(2,1)S(1)}, bf16[256,1024]{1,0:T(8,128)(2,1)}, u32[]{:S(2)}, u32[]{:S(2)}) collective-permute-start(bf16[256,1024]{1,0:T(8,128)(2,1)S(1)} %get-tuple-element.203.refs_0_), channel_id=1, source_target_pairs={{0,24},{8,16},{16,8},{24,0},{1,25},{9,17},{17,9},{25,1},{2,26},{10... | collective-permute-start | bytes 1572872 | tf_op jit(solution)/shard_map/ppermute | solution.py:540
  109.6 180.1 %all-gather.8.cloned.1.call-start = ((), (), s32[]{:S(2)}) async-start(), calls=%async_computation.7 | async-start | bytes 4718592 | tf_op jit(solution)/shard_map/all_gather | solution.py:629
  110.4 346.6 %reduce-scatter.6.cloned.1.call-start = ((), (), s32[]{:S(2)}) async-start(), calls=%async_computation.8 | async-start | bytes 5308416 | tf_op jit(solution)/shard_map/reduce_scatter | solution.py:633
  116.6 41.7 %collective-permute-start.7 = (bf16[256,1152]{1,0:T(8,128)(2,1)S(1)}, bf16[256,1152]{1,0:T(8,128)(2,1)S(1)}, u32[]{:S(2)}, u32[]{:S(2)}) collective-permute-start(bf16[256,1152]{1,0:T(8,128)(2,1)S(1)} %pad_maximum_fusion.5.refs_0_), channel_id=1, source_target_pairs={{2,0},{4,2},{6,4},{7,6},{5,7},{3,5},{1,3},{0,1},{10,8},{12,10},{14... | collective-permute-start | bytes 1769480 | tf_op jit(solution)/shard_map/ppermute | solution.py:623
  116.6 61.9 %collective-permute-start.17 = (bf16[4,512,256]{2,1,0:T(8,128)(2,1)S(1)}, bf16[4,512,256]{2,1,0:T(8,128)(2,1)S(1)}, u32[]{:S(2)}, u32[]{:S(2)}) collective-permute-start(bf16[4,512,256]{2,1,0:T(8,128)(2,1)S(1)} %copy-done.13), channel_id=1, source_target_pairs={{0,8},{8,0},{16,24},{24,16},{1,9},{9,1},{17,25},{25,17},{2,10},{10... | collective-permute-start | bytes 3145736 | tf_op jit(solution)/shard_map/ppermute | solution.py:540
  118.0 47.9 %collective-permute-start.27 = (bf16[256,1152]{1,0:T(8,128)(2,1)S(1)}, bf16[256,1152]{1,0:T(8,128)(2,1)S(1)}, u32[]{:S(2)}, u32[]{:S(2)}) collective-permute-start(bf16[256,1152]{1,0:T(8,128)(2,1)S(1)} %pad_maximum_fusion.6.refs_0_), channel_id=1, source_target_pairs={{0,2},{2,4},{4,6},{6,7},{7,5},{5,3},{3,1},{1,0},{8,10},{10,12},{12... | collective-permute-start | bytes 1769480 | tf_op jit(solution)/shard_map/ppermute | solution.py:620
  120.0 58.5 %collective-permute-start.28 = (bf16[256,1152]{1,0:T(8,128)(2,1)S(1)}, bf16[256,1152]{1,0:T(8,128)(2,1)S(1)}, u32[]{:S(2)}, u32[]{:S(2)}) collective-permute-start(bf16[256,1152]{1,0:T(8,128)(2,1)S(1)} %pad_maximum_fusion.6.refs_0_), channel_id=1, source_target_pairs={{2,0},{4,2},{6,4},{7,6},{5,7},{3,5},{1,3},{0,1},{10,8},{12,10},{14... | collective-permute-start | bytes 1769480 | tf_op jit(solution)/shard_map/ppermute | solution.py:623
  142.4 108.3 %collective-permute-start.13 = (bf16[4,256,1024]{2,1,0:T(8,128)(2,1)S(1)}, bf16[4,256,1024]{2,1,0:T(8,128)(2,1)S(1)}, u32[]{:S(2)}, u32[]{:S(2)}) collective-permute-start(bf16[4,256,1024]{2,1,0:T(8,128)(2,1)S(1)} %copy-done.7), channel_id=1, source_target_pairs={{0,8},{8,0},{16,24},{24,16},{1,9},{9,1},{17,25},{25,17},{2,10},{10... | collective-permute-start | bytes 6291464 | tf_op jit(solution)/shard_map/ppermute | solution.py:540
  158.3 92.4 %collective-permute-start.14 = (bf16[4,256,1024]{2,1,0:T(8,128)(2,1)S(1)}, bf16[4,256,1024]{2,1,0:T(8,128)(2,1)S(1)}, u32[]{:S(2)}, u32[]{:S(2)}) collective-permute-start(bf16[4,256,1024]{2,1,0:T(8,128)(2,1)S(1)} %copy-done.7), channel_id=1, source_target_pairs={{0,16},{8,24},{16,0},{24,8},{1,17},{9,25},{17,1},{25,9},{2,18},{10... | collective-permute-start | bytes 6291464 | tf_op jit(solution)/shard_map/ppermute | solution.py:540
  193.0 62.4 %collective-permute-start.18 = (bf16[4,512,256]{2,1,0:T(8,128)(2,1)S(1)}, bf16[4,512,256]{2,1,0:T(8,128)(2,1)S(1)}, u32[]{:S(2)}, u32[]{:S(2)}) collective-permute-start(bf16[4,512,256]{2,1,0:T(8,128)(2,1)S(1)} %copy-done.13), channel_id=1, source_target_pairs={{0,16},{8,24},{16,0},{24,8},{1,17},{9,25},{17,1},{25,9},{2,18},{10... | collective-permute-start | bytes 3145736 | tf_op jit(solution)/shard_map/ppermute | solution.py:540
  255.4 49.9 %collective-permute-start.15 = (bf16[2,256,1024]{2,1,0:T(8,128)(2,1)}, bf16[2,256,1024]{2,1,0:T(8,128)(2,1)}, u32[]{:S(2)}, u32[]{:S(2)}) collective-permute-start(bf16[2,256,1024]{2,1,0:T(8,128)(2,1)} %slice.223), channel_id=1, source_target_pairs={{0,8},{8,0},{16,24},{24,16},{1,9},{9,1},{17,25},{25,17},{2,10},{10... | collective-permute-start | bytes 3145736 | tf_op jit(solution)/shard_map/ppermute | solution.py:540
  256.6 48.7 %collective-permute-start.16 = (bf16[2,256,1024]{2,1,0:T(8,128)(2,1)}, bf16[2,256,1024]{2,1,0:T(8,128)(2,1)}, u32[]{:S(2)}, u32[]{:S(2)}) collective-permute-start(bf16[2,256,1024]{2,1,0:T(8,128)(2,1)} %slice.224), channel_id=1, source_target_pairs={{0,16},{8,24},{16,0},{24,8},{1,17},{9,25},{17,1},{25,9},{2,18},{10... | collective-permute-start | bytes 3145736 | tf_op jit(solution)/shard_map/ppermute | solution.py:540
  267.4 37.9 %collective-permute-start.19 = (bf16[2,512,256]{2,1,0:T(8,128)(2,1)}, bf16[2,512,256]{2,1,0:T(8,128)(2,1)}, u32[]{:S(2)}, u32[]{:S(2)}) collective-permute-start(bf16[2,512,256]{2,1,0:T(8,128)(2,1)} %slice.225), channel_id=1, source_target_pairs={{0,8},{8,0},{16,24},{24,16},{1,9},{9,1},{17,25},{25,17},{2,10},{10... | collective-permute-start | bytes 1572872 | tf_op jit(solution)/shard_map/ppermute | solution.py:540
  402.7 109.8 %reduce-scatter.12.cloned.1.call-start = ((), (), s32[]{:S(2)}) async-start(), calls=%async_computation.11 | async-start | bytes 5308416 | tf_op jit(solution)/shard_map/reduce_scatter | solution.py:633
  415.3 147.8 %reduce-scatter.10.cloned.1.call-start = ((), (), s32[]{:S(2)}) async-start(), calls=%async_computation.10 | async-start | bytes 4718592 | tf_op jit(solution)/shard_map/reduce_scatter | solution.py:633
  459.2 155.2 %reduce-scatter.8.cloned.1.call-start = ((), (), s32[]{:S(2)}) async-start(), calls=%async_computation.9 | async-start | bytes 4718592 | tf_op jit(solution)/shard_map/reduce_scatter | solution.py:633
  459.9 350.2 %reduce-scatter.14.cloned.1.call-start = ((), (), s32[]{:S(2)}) async-start(), calls=%async_computation.12 | async-start | bytes 1880064 | tf_op jit(solution)/shard_map/reduce_scatter | solution.py:633
  469.5 153.3 %collective-permute-start.50 = (bf16[2,256,1024]{2,1,0:T(8,128)(2,1)}, bf16[2,256,1024]{2,1,0:T(8,128)(2,1)}, u32[]{:S(2)}, u32[]{:S(2)}) collective-permute-start(bf16[2,256,1024]{2,1,0:T(8,128)(2,1)} %get-tuple-element.188), channel_id=1, source_target_pairs={{0,8},{8,0},{16,24},{24,16},{1,9},{9,1},{17,25},{25,17},{2,10},{10... | collective-permute-start | bytes 3145736 | tf_op jit(solution)/shard_map/ppermute | solution.py:540
  626.2 47.5 %collective-permute-start.34 = (bf16[256,1024]{1,0:T(8,128)(2,1)}, bf16[256,1024]{1,0:T(8,128)(2,1)S(1)}, u32[]{:S(2)}, u32[]{:S(2)}) collective-permute-start(bf16[256,1024]{1,0:T(8,128)(2,1)} %get-tuple-element.176.refs_15_), channel_id=1, source_target_pairs={{0,8},{8,0},{16,24},{24,16},{1,9},{9,1},{17,25},{25,17},{2,10},{10... | collective-permute-start | bytes 1572872 | tf_op jit(solution)/shard_map/ppermute | solution.py:540
  627.7 46.6 %collective-permute-start.35 = (bf16[256,1024]{1,0:T(8,128)(2,1)}, bf16[256,1024]{1,0:T(8,128)(2,1)S(1)}, u32[]{:S(2)}, u32[]{:S(2)}) collective-permute-start(bf16[256,1024]{1,0:T(8,128)(2,1)} %get-tuple-element.176.refs_15_), channel_id=1, source_target_pairs={{0,16},{8,24},{16,0},{24,8},{1,17},{9,25},{17,1},{25,9},{2,18},{10... | collective-permute-start | bytes 1572872 | tf_op jit(solution)/shard_map/ppermute | solution.py:540
  634.8 41.1 %collective-permute-start.36 = (bf16[256,1024]{1,0:T(8,128)(2,1)}, bf16[256,1024]{1,0:T(8,128)(2,1)S(1)}, u32[]{:S(2)}, u32[]{:S(2)}) collective-permute-start(bf16[256,1024]{1,0:T(8,128)(2,1)} %get-tuple-element.176.refs_15_), channel_id=1, source_target_pairs={{0,24},{8,16},{16,8},{24,0},{1,25},{9,17},{17,9},{25,1},{2,26},{10... | collective-permute-start | bytes 1572872 | tf_op jit(solution)/shard_map/ppermute | solution.py:540
  647.5 59.0 %collective-permute-start.53 = (bf16[2,256,1024]{2,1,0:T(8,128)(2,1)}, bf16[2,256,1024]{2,1,0:T(8,128)(2,1)}, u32[]{:S(2)}, u32[]{:S(2)}) collective-permute-start(bf16[2,256,1024]{2,1,0:T(8,128)(2,1)} %get-tuple-element.189), channel_id=1, source_target_pairs={{0,16},{8,24},{16,0},{24,8},{1,17},{9,25},{17,1},{25,9},{2,18},{10... | collective-permute-start | bytes 3145736 | tf_op jit(solution)/shard_map/ppermute | solution.py:540
  649.5 55.6 %collective-permute-start.55 = (bf16[2,512,256]{2,1,0:T(8,128)(2,1)}, bf16[2,512,256]{2,1,0:T(8,128)(2,1)}, u32[]{:S(2)}, u32[]{:S(2)}) collective-permute-start(bf16[2,512,256]{2,1,0:T(8,128)(2,1)} %slice.212), channel_id=1, source_target_pairs={{0,8},{8,0},{16,24},{24,16},{1,9},{9,1},{17,25},{25,17},{2,10},{10... | collective-permute-start | bytes 1572872 | tf_op jit(solution)/shard_map/ppermute | solution.py:540
  674.3 40.5 %collective-permute-start.57 = (bf16[2,512,256]{2,1,0:T(8,128)(2,1)}, bf16[2,512,256]{2,1,0:T(8,128)(2,1)}, u32[]{:S(2)}, u32[]{:S(2)}) collective-permute-start(bf16[2,512,256]{2,1,0:T(8,128)(2,1)} %add_convert_fusion.4), channel_id=1, source_target_pairs={{0,16},{8,24},{16,0},{24,8},{1,17},{9,25},{17,1},{25,9},{2,18},{10... | collective-permute-start | bytes 1572872 | tf_op jit(solution)/shard_map/ppermute | solution.py:540
  709.7 44.6 %collective-permute-start.49 = (bf16[2,256,1024]{2,1,0:T(8,128)(2,1)}, bf16[2,256,1024]{2,1,0:T(8,128)(2,1)}, u32[]{:S(2)}, u32[]{:S(2)}) collective-permute-start(bf16[2,256,1024]{2,1,0:T(8,128)(2,1)} %slice.202), channel_id=1, source_target_pairs={{0,8},{8,0},{16,24},{24,16},{1,9},{9,1},{17,25},{25,17},{2,10},{10... | collective-permute-start | bytes 3145736 | tf_op jit(solution)/shard_map/ppermute | solution.py:540
  714.8 41.0 %collective-permute-start.52 = (bf16[2,256,1024]{2,1,0:T(8,128)(2,1)}, bf16[2,256,1024]{2,1,0:T(8,128)(2,1)}, u32[]{:S(2)}, u32[]{:S(2)}) collective-permute-start(bf16[2,256,1024]{2,1,0:T(8,128)(2,1)} %slice.207), channel_id=1, source_target_pairs={{0,16},{8,24},{16,0},{24,8},{1,17},{9,25},{17,1},{25,9},{2,18},{10... | collective-permute-start | bytes 3145736 | tf_op jit(solution)/shard_map/ppermute | solution.py:540
  716.8 52.4 %collective-permute-start.51 = (bf16[2,256,1024]{2,1,0:T(8,128)(2,1)}, bf16[2,256,1024]{2,1,0:T(8,128)(2,1)}, u32[]{:S(2)}, u32[]{:S(2)}) collective-permute-start(bf16[2,256,1024]{2,1,0:T(8,128)(2,1)} %add_convert_fusion.2), channel_id=1, source_target_pairs={{0,16},{8,24},{16,0},{24,8},{1,17},{9,25},{17,1},{25,9},{2,18},{10... | collective-permute-start | bytes 3145736 | tf_op jit(solution)/shard_map/ppermute | solution.py:540
  717.6 53.0 %collective-permute-start.54 = (bf16[2,256,1024]{2,1,0:T(8,128)(2,1)}, bf16[2,256,1024]{2,1,0:T(8,128)(2,1)}, u32[]{:S(2)}, u32[]{:S(2)}) collective-permute-start(bf16[2,256,1024]{2,1,0:T(8,128)(2,1)} %add_convert_fusion.1), channel_id=1, source_target_pairs={{0,8},{8,0},{16,24},{24,16},{1,9},{9,1},{17,25},{25,17},{2,10},{10... | collective-permute-start | bytes 3145736 | tf_op jit(solution)/shard_map/ppermute | solution.py:540
  754.3 37.3 %collective-permute-start.44 = (bf16[256,1024]{1,0:T(8,128)(2,1)S(1)}, bf16[256,1024]{1,0:T(8,128)(2,1)S(1)}, u32[]{:S(2)}, u32[]{:S(2)}) collective-permute-start(bf16[256,1024]{1,0:T(8,128)(2,1)S(1)} %copy-done.73), channel_id=1, source_target_pairs={{0,16},{8,24},{16,0},{24,8},{1,17},{9,25},{17,1},{25,9},{2,18},{10... | collective-permute-start | bytes 1572872 | tf_op jit(solution)/shard_map/ppermute | solution.py:540
  (114 other events, 2488.5 us)
Sparse Core Ops, SparseCore 0:
  10.2 27.9 all-gather.3
  109.8 70.7 all-gather.5
  182.2 65.4 all-gather.7
  402.8 54.1 reduce-scatter.5
  459.1 53.3 reduce-scatter.11
  514.7 48.3 reduce-scatter.9
  566.0 48.3 reduce-scatter.7
  720.9 32.9 reduce-scatter.13

commit v2 on v1

--- a/solution.py
+++ b/solution.py
@@ -30,6 +30,16 @@
 row_params = pltpu.CompilerParams(
     vmem_limit_bytes=58 * 1024 * 1024, dimension_semantics=("arbitrary",)
 )
+
+
+def cost(gflops, megabytes):
+    return pl.CostEstimate(
+        flops=int(gflops * 1e9), transcendentals=0, bytes_accessed=int(megabytes * 1e6)
+    )
+
+
+def after(value, *others):
+    return lax.optimization_barrier((value, others))[0]
 
 
 def dot(a, b):
@@ -175,6 +185,7 @@
         in_specs=in_vmem(count + 6),
         scratch_shapes=[pltpu.VMEM((length, MODEL_WIDTH), bf16)],
         compiler_params=params,
+        cost_estimate=cost(11.0, 40.0),
         name="attn_fwd",
     )(starts, *pieces, gain, weights, cosine, sine, seg_col, seg_row)
     return results[:count], results[count:]
@@ -286,20 +297,16 @@
             pltpu.VMEM((length, heads), f32),
         ],
         compiler_params=params,
+        cost_estimate=cost(18.0, 65.0),
         name="attn_bwd",
     )(starts, *pieces, gain, weights, cosine, sine, seg_col, seg_row, *kept, *grad_pieces)
     return results[:count], results[count:]
 
 
-def dispatch_body(order_ref, x_ref, router_ref, *refs, local):
-    gm_pieces, (xd_ref, gd_ref, pt_ref, pgt_ref, gm_ref) = refs[:-5], refs[-5:]
+def dispatch_body(
+    offset_ref, x_ref, gm_ref, router_ref, xd_ref, gd_ref, pt_ref, pgt_ref, *, local
+):
     rows = x_ref.shape[0]
-    for index, piece in enumerate(gm_pieces):
-
-        @pl.when(pl.program_id(0) == index)
-        def _(piece=piece):
-            gm_ref[...] = piece[...]
-
     slots = local * CAP
     x = x_ref[...]
     mask = gm_ref[:, MODEL_WIDTH:]
@@ -312,7 +319,7 @@
     )
     place = dot(jnp.where(earlier, 1.0, 0.0).astype(bf16), mask)
     place = jnp.where(chosen, place, -1.0).astype(bf16)
-    offset = order_ref[pl.num_programs(0)]
+    offset = offset_ref[0]
 
     def pick(shape, slot_axis):
         slot = lax.broadcasted_iota(jnp.int32, shape, slot_axis)
@@ -344,29 +351,27 @@
     pgt_ref[...] = jnp.where(hit, dot(gates, spread), 0.0).astype(bf16)
 
 
-def dispatch(order, x, gm_pieces, router, local):
+def dispatch(offset, x, gm, router, local):
     blocks = x.shape[0] // ROW_BLOCK
     slots = local * CAP
     slotted = jax.ShapeDtypeStruct((local, blocks, CAP, MODEL_WIDTH), bf16)
-    slotted_spec = pl.BlockSpec((local, 1, CAP, MODEL_WIDTH), lambda s, o: (0, o[s], 0, 0))
+    slotted_spec = pl.BlockSpec((local, 1, CAP, MODEL_WIDTH), lambda s, o: (0, s, 0, 0))
     return pl.pallas_call(
         functools.partial(dispatch_body, local=local),
         grid_spec=pltpu.PrefetchScalarGridSpec(
             num_scalar_prefetch=1,
             grid=(blocks,),
             in_specs=[
-                pl.BlockSpec((ROW_BLOCK, MODEL_WIDTH), lambda s, o: (o[s], 0)),
+                pl.BlockSpec((ROW_BLOCK, MODEL_WIDTH), lambda s, o: (s, 0)),
+                pl.BlockSpec((ROW_BLOCK, MODEL_WIDTH + LANES), lambda s, o: (s, 0)),
                 pl.BlockSpec((MODEL_WIDTH, LANES), lambda s, o: (0, 0)),
-            ]
-            + [pl.BlockSpec((ROW_BLOCK, MODEL_WIDTH + LANES), lambda s, o: (0, 0))]
-            * len(gm_pieces),
+            ],
             out_specs=[
                 slotted_spec,
                 slotted_spec,
-                pl.BlockSpec((ROW_BLOCK, slots), lambda s, o: (o[s], 0)),
-                pl.BlockSpec((ROW_BLOCK, slots), lambda s, o: (o[s], 0)),
+                pl.BlockSpec((ROW_BLOCK, slots), lambda s, o: (s, 0)),
+                pl.BlockSpec((ROW_BLOCK, slots), lambda s, o: (s, 0)),
             ],
-            scratch_shapes=[pltpu.VMEM((ROW_BLOCK, MODEL_WIDTH + LANES), bf16)],
         ),
         out_shape=(
             slotted,
@@ -375,18 +380,20 @@
             jax.ShapeDtypeStruct((x.shape[0], slots), bf16),
         ),
         compiler_params=row_params,
+        cost_estimate=cost(11.0, 40.0),
         name="dispatch",
-    )(order, x, router, *gm_pieces)
+    )(offset, x, gm, router)
 
 
 def experts_body(place_ref, *refs, count, carried):
     xd_ref, gd_ref, refs = refs[0], refs[1], refs[2:]
     tables = count + 1 if count > 1 else count
     gu_pieces, d_pieces, refs = refs[:tables], refs[tables : 2 * tables], refs[2 * tables :]
-    old, refs = (refs[: 2 * count], refs[2 * count :]) if carried else ((), refs)
+    tables = 2 * count if count > 1 else count
+    old, refs = (refs[: 2 * tables], refs[2 * tables :]) if carried else ((), refs)
     out_ref, dx_ref, h_ref = refs[:3]
-    dgu_refs, dd_refs = refs[3 : 3 + count], refs[3 + count : 3 + 2 * count]
-    wgu_ref, wd_ref, act_sc, dh_sc = refs[3 + 2 * count :]
+    grad_refs = refs[3 : 3 + 2 * tables]
+    wgu_ref, wd_ref, act_sc, dh_sc = refs[3 + 2 * tables :]
     expert = pl.program_id(0)
     half = pl.num_programs(0) // 2
 
@@ -437,16 +444,29 @@
         dx_ref[0, rows, :] = dot_nt(dh_sc[rows, :], wgu_ref[...]).astype(bf16)
 
     for_blocks(total // chunk, chunk_step)
+    def put_grad(index, value):
+        if carried:
+            value = value + old[index][0].astype(f32)
+        grad_refs[index][0] = value.astype(bf16)
+
+    def put_halves(index, value):
+        if count == 1:
+            put_grad(index, value)
+            return
+
+        @pl.when(expert < half)
+        def _():
+            put_grad(2 * index, value)
+
+        @pl.when(expert >= half)
+        def _():
+            put_grad(2 * index + 1, value)
+
     for index in range(count):
-        rows = dgu_refs[index].shape[1]
+        rows = grad_refs[0].shape[1]
         begin = starts(index, rows)
-        grad_down = dot_tn(act_sc[...], gd_ref[0, :, pl.ds(begin, rows)])
-        grad_gate_up = dot_tn(xd_ref[0, :, pl.ds(begin, rows)], dh_sc[...])
-        if carried:
-            grad_gate_up = grad_gate_up + old[index][0].astype(f32)
-            grad_down = grad_down + old[count + index][0].astype(f32)
-        dgu_refs[index][0] = grad_gate_up.astype(bf16)
-        dd_refs[index][0] = grad_down.astype(bf16)
+        put_halves(index, dot_tn(xd_ref[0, :, pl.ds(begin, rows)], dh_sc[...]))
+        put_halves(count + index, dot_tn(act_sc[...], gd_ref[0, :, pl.ds(begin, rows)]))
 
 
 def run_experts(place, xd, gd, gu_pieces, d_pieces, old):
@@ -457,16 +477,27 @@
     def spec(a, b):
         return pl.BlockSpec((1, a, b), lambda e, o: (e, 0, 0))
 
+    half = local // 2
+
+    def half_specs(a, b):
+        return [
+            pl.BlockSpec((1, a, b), lambda e, o: (jnp.minimum(e, half - 1), 0, 0)),
+            pl.BlockSpec((1, a, b), lambda e, o: (jnp.maximum(e - half, 0), 0, 0)),
+        ]
+
     def piece_specs(a, b):
-        half = local // 2
         specs = [spec(a, b)] * min(count, 3)
-        if count > 1:
-            specs.append(pl.BlockSpec((1, a, b), lambda e, o: (jnp.minimum(e, half - 1), 0, 0)))
-            specs.append(pl.BlockSpec((1, a, b), lambda e, o: (jnp.maximum(e - half, 0), 0, 0)))
-        return specs
+        return specs + half_specs(a, b) if count > 1 else specs
 
     row_spec = spec(total, MODEL_WIDTH)
-    grad_specs = [spec(rows, 2 * FF)] * count + [spec(FF, rows)] * count
+    if count > 1:
+        both = half_specs(rows, 2 * FF), half_specs(FF, rows)
+        grad_specs = both[0] * count + both[1] * count
+        grad_rows = local // 2
+    else:
+        grad_specs = [spec(rows, 2 * FF), spec(FF, rows)]
+        grad_rows = local
+    repeats = len(grad_specs) // 2
     results = pl.pallas_call(
         functools.partial(experts_body, count=count, carried=bool(old)),
         grid_spec=pltpu.PrefetchScalarGridSpec(
@@ -489,9 +520,10 @@
             jax.ShapeDtypeStruct((local, total, MODEL_WIDTH), bf16),
             jax.ShapeDtypeStruct((local, total, LANES), bf16),
         )
-        + (jax.ShapeDtypeStruct((local, rows, 2 * FF), bf16),) * count
-        + (jax.ShapeDtypeStruct((local, FF, rows), bf16),) * count,
+        + (jax.ShapeDtypeStruct((grad_rows, rows, 2 * FF), bf16),) * repeats
+        + (jax.ShapeDtypeStruct((grad_rows, FF, rows), bf16),) * repeats,
         compiler_params=row_params,
+        cost_estimate=cost(30.0, 110.0),
         name="experts",
     )(place, xd, gd, *gu_pieces, *d_pieces, *old)
     return results[:3], results[3:]
@@ -532,6 +564,7 @@
             jax.ShapeDtypeStruct((pt.shape[0], MODEL_WIDTH + LANES), bf16),
         ),
         compiler_params=row_params,
+        cost_estimate=cost(9.0, 33.0),
         name="combine",
     )(slotted(out), slotted(dx), slotted(h), pt, pgt)
 
@@ -557,72 +590,54 @@
     return [lax.all_gather(value, "tp", axis=0, tiled=True)]
 
 
-def sum_rows(parts):
+def send_rows(parts):
     if square():
-        total = parts[0].astype(f32)
-        for bits in (1, 2, 3):
-            total = total + flip(parts[bits], bits).astype(f32)
-        return total
-    return lax.psum_scatter(parts[0], "tp", scatter_dimension=0, tiled=True).astype(f32)
-
-
-def gather_weights(value, axis):
+        return [parts[0]] + [flip(parts[bits], bits) for bits in (1, 2, 3)]
+    return [lax.psum_scatter(parts[0], "tp", scatter_dimension=0, tiled=True)]
+
+
+def add_rows(came):
+    total = came[0].astype(f32)
+    for part in came[1:]:
+        total = total + part.astype(f32)
+    return total
+
+
+def gather_weights_near(value, axis):
     if square():
-        half = value.shape[0] // 2
-        along_x = flip(value, 1)
-        along_y = flip(value, 2)
-        return [value, along_x, along_y, flip(along_y[:half], 1), flip(along_x[half:], 2)]
+        return [value, flip(value, 1), flip(value, 2)]
     return [lax.all_gather(value, "tp", axis=axis, tiled=True)]
 
 
-def sum_weights(parts, axis):
+def gather_weights_far(near):
     if square():
-        half = parts[0].shape[0] // 2
-        wide = [p.astype(f32) for p in parts]
-        top = flip(parts[1][:half], 1) + wide[0][:half]
-        top_far = flip(parts[3][:half], 1) + wide[2][:half]
-        low = flip(parts[2][half:], 2) + wide[0][half:]
-        low_far = flip(parts[3][half:], 2) + wide[1][half:]
-        top = top + flip(top_far.astype(bf16), 2)
-        low = low + flip(low_far.astype(bf16), 1)
-        return jnp.concatenate([top, low])
-    return lax.psum_scatter(parts[0], "tp", scatter_dimension=axis, tiled=True).astype(f32)
-
-
-def ring_devices():
-    size = lax.axis_size("ep")
-    return [2 * r if 2 * r < size else 2 * (size - 1 - r) + 1 for r in range(size)]
-
-
-def ring_order():
-    size = lax.axis_size("ep")
-    devices = ring_devices()
-    table = []
-    for me in range(size):
-        at = devices.index(me)
-        steps = [0]
-        for step in range(1, size // 2 + 1):
-            steps.append(-step)
-            if step < size // 2:
-                steps.append(step)
-        table.append([devices[(at + step) % size] for step in steps])
-    return jnp.asarray(table, jnp.int32)[lax.axis_index("ep")]
-
-
-def ring_gather(value):
-    size = lax.axis_size("ep")
-    devices = ring_devices()
-    ahead = [(devices[r], devices[(r + 1) % size]) for r in range(size)]
-    back = [(b, a) for a, b in ahead]
-    pieces = [value]
-    left = right = value
-    for step in range(1, size // 2 + 1):
-        left = lax.ppermute(left, "ep", ahead)
-        pieces.append(left)
-        if step < size // 2:
-            right = lax.ppermute(right, "ep", back)
-            pieces.append(right)
-    return pieces
+        half = near[0].shape[0] // 2
+        return [*near, flip(near[2][:half], 1), flip(near[1][half:], 2)]
+    return near
+
+
+def sum_weights_near(parts, axis):
+    if square():
+        own, along_x, along_y, across = parts[0:2], parts[2:4], parts[4:6], parts[6:8]
+        top = flip(along_x[0], 1).astype(f32) + own[0].astype(f32)
+        top_far = flip(across[0], 1).astype(f32) + along_y[0].astype(f32)
+        low = flip(along_y[1], 2).astype(f32) + own[1].astype(f32)
+        low_far = flip(across[1], 2).astype(f32) + along_x[1].astype(f32)
+        return top, low, top_far.astype(bf16), low_far.astype(bf16)
+    return (lax.psum_scatter(parts[0], "tp", scatter_dimension=axis, tiled=True),)
+
+
+def sum_weights_far(near):
+    if square():
+        top, low, top_far, low_far = near
+        return top, low, flip(top_far, 2), flip(low_far, 1)
+    return near
+
+
+def add_far(far):
+    if square():
+        return jnp.concatenate([far[0] + far[2], far[1] + far[3]])
+    return far[0].astype(f32)
 
 
 def ag_ep(value, axis=0):
@@ -673,8 +688,6 @@
     gain_two = norm_gains[1:2]
     router = jnp.pad(w_router, ((0, 0), (0, LANES - EXPERTS)))
 
-    order = jnp.concatenate([ring_order(), offset])
-
     weights = ag_ep(
         jnp.concatenate(
             [
@@ -684,16 +697,17 @@
             axis=1,
         )
     )
-    token_full = [gather_rows(tokens[m]) for m in range(micro)]
     lanes = jnp.arange(LANES, dtype=jnp.int32)
     masks = jnp.any(
         routes.reshape(micro, rows, -1)[..., None] == lanes, axis=2
     ).astype(bf16)
-    gm_full = [ring_gather(jnp.concatenate([cotangent[m], masks[m]], axis=-1)) for m in range(micro)]
-    gu_pieces = gather_weights(w_gate_up, 1)
-    d_pieces = gather_weights(w_down, 2)
-
     tables = [rope_tables(segment_ids[m]) for m in range(micro)]
+
+    token_full = []
+    for m in range(micro):
+        own = after(tokens[m], token_full[-1]) if token_full else tokens[m]
+        token_full.append(gather_rows(own))
+    weights = after(weights, token_full[0])
     fixed = []
     for m in range(micro):
         fixed.append(
@@ -703,15 +717,27 @@
             )
         )
 
+    gm_full = []
     kept = []
+    partial = []
+    for m in range(micro):
+        parts, saved = attention_forward(*fixed[m])
+        partial.append(parts)
+        kept.append(saved)
+    weights_in = after((w_gate_up, w_down), partial)
+    gu_near = gather_weights_near(weights_in[0], 1)
+    d_near = gather_weights_near(weights_in[1], 2)
+
     hiddens = []
     normed_twos = []
     scales = []
     gate_rows = []
+    x_full = []
     for m in range(micro):
-        parts, saved = attention_forward(*fixed[m])
-        kept.append(saved)
-        branch = sum_rows(parts)
+        came = send_rows(partial[m])
+        if m == 0:
+            came, token_full = lax.optimization_barrier((came, token_full))
+        branch = add_rows(after(came, normed_twos))
         hidden = tokens[m].astype(f32) + residual_scale * branch
         scale_two = lax.rsqrt(jnp.mean(hidden * hidden, axis=-1, keepdims=True) + epsilon)
         normed_two = (hidden * scale_two * gain_two).astype(bf16)
@@ -723,26 +749,49 @@
         hiddens.append(hidden)
         normed_twos.append(normed_two)
         scales.append(scale_two)
-
+        if m == micro - 1:
+            normed_two, gu_near, d_near = lax.optimization_barrier((normed_two, gu_near, d_near))
+        gm = jnp.concatenate([cotangent[m], masks[m]], axis=-1)
+        gm_full.append(ag_ep(after(gm, weights if m == 0 else normed_two)))
+        x_full.append(ag_ep(after(normed_two, gm_full[m]) if m == 0 else normed_two))
+
+    gu_pieces = gather_weights_far(gu_near)
+    d_pieces = gather_weights_far(d_near)
     old = ()
     mixes = []
-    outputs = []
+    grads = []
+    ready = ()
+    for m in range(micro):
+        x_in = after(x_full[m], ready) if ready else x_full[m]
+        xd, gd, pt, pgt = dispatch(offset, x_in, gm_full[m], router, local)
+        merged = (local, ep_size * CAP, MODEL_WIDTH)
+        (out, dx, h), old = run_experts(
+            place, xd.reshape(merged), gd.reshape(merged), gu_pieces, d_pieces, old
+        )
+        mix, grad = combine(out, dx, h, pt, pgt)
+        ready = (mix, grad)
+        mixes.append(mix)
+        grads.append(rs_ep(grad))
+    near_gate_up = sum_weights_near(old[: len(old) // 2], 1)
+    near_down = sum_weights_near(old[len(old) // 2 :], 2)
     input_grads = []
     acc_router = 0.0
     acc_gain_one = 0.0
     acc_gain_two = 0.0
     acc_weights = 0.0
     for m in range(micro):
-        x_full = ag_ep(normed_twos[m])
-        xd, gd, pt, pgt = dispatch(order, x_full, gm_full[m], router, local)
-        merged = (local, ep_size * CAP, MODEL_WIDTH)
-        (out, dx, h), old = run_experts(
-            place, xd.reshape(merged), gd.reshape(merged), gu_pieces, d_pieces, old
-        )
-        mix, grad = combine(out, dx, h, pt, pgt)
-        grad = rs_ep(grad).astype(f32)
-        mixes.append(mix)
-
+        grad = grads[m]
+        if m == micro - 1:
+            grad, near_gate_up, near_down, _ = lax.optimization_barrier(
+                (grad, near_gate_up, near_down, came)
+            )
+            far_down = sum_weights_far(near_down)
+            mixed = []
+            for n in range(micro):
+                mixed.append(rs_ep(after(mixes[n], grad, mixed)))
+        else:
+            grad, near_down = lax.optimization_barrier((grad, near_down))
+        grad = grad.astype(f32)
         h_rows = grad[:, MODEL_WIDTH:]
         grad_logits = (
             h_rows - gate_rows[m] * jnp.sum(h_rows, axis=-1, keepdims=True)
@@ -759,10 +808,14 @@
         )
         acc_gain_two = acc_gain_two + jnp.sum(grad_normed * hiddens[m] * scale, axis=0)
         grad_branch = gather_rows((residual_scale * grad_hidden).astype(bf16))
+        if m == micro - 1:
+            grad_branch, far_down = lax.optimization_barrier((grad_branch, far_down))
+            far_gate_up = sum_weights_far(near_gate_up)
         parts, (gweights, ggain) = attention_backward(*fixed[m], kept[m], grad_branch)
+        came = send_rows(parts)
         acc_weights = acc_weights + gweights.astype(f32)
         acc_gain_one = acc_gain_one + ggain[0]
-        grad_normed = sum_rows(parts)
+        grad_normed = add_rows(came)
         inputs = tokens[m].astype(f32)
         scale = lax.rsqrt(jnp.mean(inputs * inputs, axis=-1, keepdims=True) + epsilon)
         weighted = grad_normed * gain_one
@@ -770,15 +823,13 @@
         input_grads.append(
             grad_hidden + scale * weighted - inputs * scale * scale * scale * inner
         )
-
-    for m in range(micro):
-        mix, _ = lax.optimization_barrier((mixes[m], grad))
-        mix = rs_ep(mix).astype(f32)
-        outputs.append((hiddens[m] + residual_scale * mix).astype(bf16))
-
-    count = places.shape[0]
-    grad_gate_up = sum_weights(old[:count], 1)
-    grad_down = sum_weights(old[count:], 2)
+    mixed, _ = lax.optimization_barrier((mixed, parts))
+    outputs = [
+        (hiddens[m] + residual_scale * mixed[m].astype(f32)).astype(bf16) for m in range(micro)
+    ]
+    acc_weights, far_gate_up = lax.optimization_barrier((acc_weights, far_gate_up))
+    grad_gate_up = add_far(far_gate_up)
+    grad_down = add_far(far_down)
 
     small = jnp.concatenate(
         [
@@ -791,8 +842,10 @@
     ).astype(bf16)
     rows = MODEL_WIDTH // lax.axis_size("tp")
     if square():
-        small = sum_rows(
-            [lax.dynamic_slice_in_dim(small, places[k] * rows, rows) for k in range(4)]
+        small = add_rows(
+            send_rows(
+                [lax.dynamic_slice_in_dim(small, places[k] * rows, rows) for k in range(4)]
+            )
         ).astype(bf16)
     else:
         small = lax.psum_scatter(small, "tp", scatter_dimension=0, tiled=True)

time: 835 us -> 728 us (0.87)
  waiting for transfers between devices: 402 us -> 298 us
  starting transfers between devices: 94.2 us -> 56.8 us
  Pallas kernels: 217 us -> 243 us
  other arithmetic: 57.9 us -> 68.1 us
    ppermute x47, waiting for transfers between devices: 125 us -> 255 us  [flip(): return lax.ppermute(value, 'tp', [(t, t ^ bits) for t in range(4)])]
    reduce_scatter x5, waiting for transfers between devices: 170 us -> 41.6 us  [rs_ep(): return lax.psum_scatter(value, 'ep', scatter_dimension=axis, tiled=True)]
    ppermute x14 -> x0, waiting for transfers between devices: 106 us -> none  [the longest x8 71.6 us: ring_gather(): left = lax.ppermute(left, 'ep', ahead)]
    ppermute x14 -> x0, starting transfers between devices: 35.2 us -> none  [the longest x8 35.2 us: ring_gather(): left = lax.ppermute(left, 'ep', ahead)]
    pallas_call x2, Pallas kernels: 84.9 us -> 113 us  [run_experts(): pl.pallas_call(functools.partial(experts_body, count=count, carried=bool(...]
    add x2 -> x9, other arithmetic: 5.27 us -> 15.8 us  [the longest x4 4.32 us: add_far(): return jnp.concatenate([far[0] + far[2], far[1] + far[3]])]
  transfers between devices with their start and end apart: 69 -> 57, of which waited for: 31 -> 24; matrix products, arithmetic and copies ran while one was open for 10% -> 13% of each run, Pallas kernels for 15% -> 34%
where the time goes in v2:
time: 728 us; the launch traced here: 717 us
  waiting for transfers between devices  298 us (41%)
  Pallas kernels  243 us (33%)
  other arithmetic  68.1 us (9%)
  starting transfers between devices  56.8 us (8%)
  local copies, waits for them, and re-layouts  28.9 us (4%)
  between operations  15.4 us (2%)
    ppermute x47, waiting for transfers between devices, flip(): return lax.ppermute(value, 'tp', [(t, t ^ bits) for t in range(4)])  255 us
    pallas_call x2, Pallas kernels, run_experts(): pl.pallas_call(functools.partial(experts_body, count=count, carried=bool(...  113 us
    ppermute x47, starting transfers between devices, flip(): return lax.ppermute(value, 'tp', [(t, t ^ bits) for t in range(4)])  55.5 us
    pallas_call x2, Pallas kernels, attention_backward(): pl.pallas_call(functools.partial(attention_backward_body, count=count), o...  47.3 us
    reduce_scatter x5, waiting for transfers between devices, rs_ep(): return lax.psum_scatter(value, 'ep', scatter_dimension=axis, tiled=True)  41.6 us
    pallas_call x2, Pallas kernels, dispatch(): pl.pallas_call(functools.partial(dispatch_body, local=local), grid_spec=p...  29.7 us
    pallas_call x2, Pallas kernels, attention_forward(): pl.pallas_call(functools.partial(attention_forward_body, count=count), ou...  28.9 us
    pallas_call x2, Pallas kernels, combine(): pl.pallas_call(combine_body, grid=(blocks,), in_specs=[spec(MODEL_WIDTH),...  25 us
  transfers between devices with their start and end apart: 57, of which 24 were waited for; matrix products, arithmetic and copies ran while one was open for 13% of the time, Pallas kernels for 34%

profile of v2, /device:TPU:0, one launch (start us, length us, event | category | flops | bytes accessed | tf_op | source)
XLA Modules:
  0.0 716.9 jit_solution(17887144344236666967)
XLA Ops:
  12.0 3.9 collective-permute-start.2
  20.9 7.9 %collective-permute-done.2.refs_3_ = bf16[256,1024]{1,0:T(8,128)(2,1)S(1)} collective-permute-done((bf16[256,1024]{1,0:T(8,128)(2,1)S(1)}, bf16[256,1024]{1,0:T(8,128)(2,1)S(1)}, u32[]{:S(2)}, u32[]{:S(2)}) %collective-permute-start.2) | collective-permute-done | bytes 524320 | tf_op jit(solution)/shard_map/ppermute | solution.py:573
  28.8 10.4 %collective-permute-done.1.refs_2_ = bf16[256,1024]{1,0:T(8,128)(2,1)} collective-permute-done((bf16[256,1024]{1,0:T(8,128)(2,1)S(1)}, bf16[256,1024]{1,0:T(8,128)(2,1)}, u32[]{:S(2)}, u32[]{:S(2)}) %collective-permute-start.1) | collective-permute-done | bytes 524320 | tf_op jit(solution)/shard_map/ppermute | solution.py:573
  46.2 5.5 fusion.15
  55.1 14.5 %attn_fwd.2 = (bf16[256,1024]{1,0:T(8,128)(2,1)}, bf16[256,1024]{1,0:T(8,128)(2,1)}, bf16[256,1024]{1,0:T(8,128)(2,1)}, bf16[256,1024]{1,0:T(8,128)(2,1)}, bf16[...) custom-call(s32[4]{0:T(128)} %add_multiply_fusion.2.starts_ref, ...), custom_call_target="tpu_custom_call" | custom-call | flops 11000000512 | bytes 40000000 | tf_op jit(solution)/shard_map/attn_fwd/pallas_call | solution.py:182
  73.2 4.4 collective-permute-done.7.refs_2_
  78.8 11.2 %collective-permute-done.3 = bf16[256,1024]{1,0:T(8,128)(2,1)S(1)} collective-permute-done((bf16[256,1024]{1,0:T(8,128)(2,1)}, bf16[256,1024]{1,0:T(8,128)(2,1)S(1)}, u32[]{:S(2)}, u32[]{:S(2)}) %collective-permute-start.3) | collective-permute-done | bytes 524320 | tf_op jit(solution)/shard_map/ppermute | solution.py:573
  90.0 10.0 %collective-permute-done.5 = bf16[256,1024]{1,0:T(8,128)(2,1)S(1)} collective-permute-done((bf16[256,1024]{1,0:T(8,128)(2,1)}, bf16[256,1024]{1,0:T(8,128)(2,1)S(1)}, u32[]{:S(2)}, u32[]{:S(2)}) %collective-permute-start.5) | collective-permute-done | bytes 524320 | tf_op jit(solution)/shard_map/ppermute | solution.py:573
  103.9 14.3 %attn_fwd.3 = (bf16[256,1024]{1,0:T(8,128)(2,1)}, bf16[256,1024]{1,0:T(8,128)(2,1)}, bf16[256,1024]{1,0:T(8,128)(2,1)}, bf16[256,1024]{1,0:T(8,128)(2,1)}, bf16[...) custom-call(s32[4]{0:T(128)} %add_multiply_fusion.2.starts_ref, ...), custom_call_target="tpu_custom_call" | custom-call | flops 11000000512 | bytes 40000000 | tf_op jit(solution)/shard_map/attn_fwd/pallas_call | solution.py:182
  123.9 56.0 %collective-permute-done.9 = bf16[256,1024]{1,0:T(8,128)(2,1)S(1)} collective-permute-done((bf16[256,1024]{1,0:T(8,128)(2,1)}, bf16[256,1024]{1,0:T(8,128)(2,1)S(1)}, u32[]{:S(2)}, u32[]{:S(2)}) %collective-permute-start.9) | collective-permute-done | bytes 524320 | tf_op jit(solution)/shard_map/ppermute | solution.py:573
  181.9 9.0 %collective-permute-done.11 = bf16[256,1024]{1,0:T(8,128)(2,1)S(1)} collective-permute-done((bf16[256,1024]{1,0:T(8,128)(2,1)}, bf16[256,1024]{1,0:T(8,128)(2,1)S(1)}, u32[]{:S(2)}, u32[]{:S(2)}) %collective-permute-start.11) | collective-permute-done | bytes 524320 | tf_op jit(solution)/shard_map/ppermute | solution.py:573
  193.5 17.5 %collective-permute-done.15.refs_9_ = bf16[4,512,256]{2,1,0:T(8,128)(2,1)} collective-permute-done((bf16[4,512,256]{2,1,0:T(8,128)(2,1)}, bf16[4,512,256]{2,1,0:T(8,128)(2,1)}, u32[]{:S(2)}, u32[]{:S(2)}) %collective-permute-start.15) | collective-permute-done | bytes 1048608 | tf_op jit(solution)/shard_map/ppermute | solution.py:573
  226.2 15.0 %dispatch.2 = (bf16[4,8,96,1024]{3,2,1,0:T(8,128)(2,1)}, bf16[4,8,96,1024]{3,2,1,0:T(8,128)(2,1)}, bf16[2048,384]{1,0:T(8,128)(2,1)}, bf16[2048,384]{1,0:T(8,128)(2,1)}) custom-call(s32[1]{0:T(128)} %bitcast.11.offset_ref, bf16[2048,1024]{1,0:T(8,128)(2,1)} %all-gather.10.cloned.1.call-done.x_ref, bf16[2048,1152]{1,0:T(8,128)(2,1)} %all-gather.8.cloned.1.call-done.gm_ref, ...), custom_call_target="tpu_custom_call" | custom-call | flops 11000000512 | bytes 40000000 | tf_op jit(solution)/shard_map/dispatch/pallas_call | solution.py:359
  241.2 10.1 %collective-permute-done.18.refs_10_ = bf16[2,512,256]{2,1,0:T(8,128)(2,1)} collective-permute-done((bf16[2,512,256]{2,1,0:T(8,128)(2,1)}, bf16[2,512,256]{2,1,0:T(8,128)(2,1)}, u32[]{:S(2)}, u32[]{:S(2)}) %collective-permute-start.18) | collective-permute-done | bytes 524320 | tf_op jit(solution)/shard_map/ppermute | solution.py:573
  251.4 54.6 %experts.2 = (bf16[4,768,1024]{2,1,0:T(8,128)(2,1)}, bf16[4,768,1024]{2,1,0:T(8,128)(2,1)}, bf16[4,768,128]{2,1,0:T(8,128)(2,1)}, bf16[2,256,1024]{2,1,0:T(8,128...) custom-call(s32[5]{0:T(128)} %concatenate.27.place_ref, ...), custom_call_target="tpu_custom_call" | custom-call | flops 30000001024 | bytes 110000000 | tf_op jit(solution)/shard_map/experts/pallas_call | solution.py:501
  306.0 12.5 %combine.2 = (bf16[2048,1024]{1,0:T(8,128)(2,1)}, bf16[2048,1152]{1,0:T(8,128)(2,1)}) custom-call(bf16[4,8,96,1024]{3,2,1,0:T(8,128)(2,1)} %bitcast.143, bf16[4,8,96,1024]{3,2,1,0:T(8,128)(2,1)} %bitcast.144, bf16[4,8,96,128]{3,2,1,0:T(8,128)(2,1)} %bitcast.146, bf16[2048,384]{1,0:T(8,128)(2,1)} %get-tuple-element.183.pt_ref, ...), custom_call_target="tpu_custom_call" | custom-call | flops 8999999488 | bytes 33000000 | tf_op jit(solution)/shard_map/combine/pallas_call | solution.py:555
  318.6 14.7 %dispatch.3 = (bf16[4,8,96,1024]{3,2,1,0:T(8,128)(2,1)}, bf16[4,8,96,1024]{3,2,1,0:T(8,128)(2,1)}, bf16[2048,384]{1,0:T(8,128)(2,1)}, bf16[2048,384]{1,0:T(8,128)(2,1)}) custom-call(s32[1]{0:T(128)} %bitcast.11.offset_ref, bf16[2048,1024]{1,0:T(8,128)(2,1)} %all-gather.12.cloned.1.call-done.x_ref, bf16[2048,1152]{1,0:T(8,128)(2,1)} %all-gather.14.cloned.1.call-done.gm_ref, ...), custom_call_target="tpu_custom_call" | custom-call | flops 11000000512 | bytes 40000000 | tf_op jit(solution)/shard_map/dispatch/pallas_call | solution.py:359
  333.4 58.0 %experts.3 = (bf16[4,768,1024]{2,1,0:T(8,128)(2,1)}, bf16[4,768,1024]{2,1,0:T(8,128)(2,1)}, bf16[4,768,128]{2,1,0:T(8,128)(2,1)}, bf16[2,256,1024]{2,1,0:T(8,128...) custom-call(s32[5]{0:T(128)} %concatenate.27.place_ref, ...), custom_call_target="tpu_custom_call" | custom-call | flops 30000001024 | bytes 110000000 | tf_op jit(solution)/shard_map/experts/pallas_call | solution.py:501
  391.3 12.5 %combine.3 = (bf16[2048,1024]{1,0:T(8,128)(2,1)}, bf16[2048,1152]{1,0:T(8,128)(2,1)}) custom-call(bf16[4,8,96,1024]{3,2,1,0:T(8,128)(2,1)} %bitcast.139, bf16[4,8,96,1024]{3,2,1,0:T(8,128)(2,1)} %bitcast.140, bf16[4,8,96,128]{3,2,1,0:T(8,128)(2,1)} %bitcast.145, bf16[2048,384]{1,0:T(8,128)(2,1)} %get-tuple-element.211.pt_ref, ...), custom_call_target="tpu_custom_call" | custom-call | flops 8999999488 | bytes 33000000 | tf_op jit(solution)/shard_map/combine/pallas_call | solution.py:555
  412.2 7.0 collective-permute-done.24
  421.4 9.1 %collective-permute-done.26 = bf16[2,512,256]{2,1,0:T(8,128)(2,1)S(1)} collective-permute-done((bf16[2,512,256]{2,1,0:T(8,128)(2,1)}, bf16[2,512,256]{2,1,0:T(8,128)(2,1)S(1)}, u32[]{:S(2)}, u32[]{:S(2)}) %collective-permute-start.26) | collective-permute-done | bytes 524320 | tf_op jit(solution)/shard_map/ppermute | solution.py:573
  444.4 31.2 %collective-permute-done.22 = bf16[2,256,1024]{2,1,0:T(8,128)(2,1)} collective-permute-done((bf16[2,256,1024]{2,1,0:T(8,128)(2,1)}, bf16[2,256,1024]{2,1,0:T(8,128)(2,1)}, u32[]{:S(2)}, u32[]{:S(2)}) %collective-permute-start.22) | collective-permute-done | bytes 1048608 | tf_op jit(solution)/shard_map/ppermute | solution.py:573
  482.9 4.3 collective-permute-done.30.refs_18_
  487.2 7.8 %collective-permute-done.28.refs_16_ = bf16[256,1024]{1,0:T(8,128)(2,1)S(1)} collective-permute-done((bf16[256,1024]{1,0:T(8,128)(2,1)S(1)}, bf16[256,1024]{1,0:T(8,128)(2,1)S(1)}, u32[]{:S(2)}, u32[]{:S(2)}) %collective-permute-start.28) | collective-permute-done | bytes 524320 | tf_op jit(solution)/shard_map/ppermute | solution.py:573
  495.8 23.7 %attn_bwd.2 = (bf16[256,1024]{1,0:T(8,128)(2,1)}, bf16[256,1024]{1,0:T(8,128)(2,1)}, bf16[256,1024]{1,0:T(8,128)(2,1)}, bf16[256,1024]{1,0:T(8,128)(2,1)}, bf16[1024,768]{1,0:T(8,128)(2,1)}, /*index=5*/f32[1,1024]{1,0:T(1,128)}) custom-call(s32[4]{0:T(128)} %add_multiply_fusion.2.starts_ref, bf16[256,1024]{1,0:T(8,128)(2,1)} %copy-done.29, ...), custom_call_target="tpu_custom_call" | custom-call | flops 17999998976 | bytes 65000000 | tf_op jit(solution)/shard_map/attn_bwd/pallas_call | solution.py:284
  527.5 7.2 %collective-permute-done.31 = bf16[256,1024]{1,0:T(8,128)(2,1)} collective-permute-done((bf16[256,1024]{1,0:T(8,128)(2,1)}, bf16[256,1024]{1,0:T(8,128)(2,1)}, u32[]{:S(2)}, u32[]{:S(2)}) %collective-permute-start.31) | collective-permute-done | bytes 524320 | tf_op jit(solution)/shard_map/ppermute | solution.py:573
  534.7 8.1 %collective-permute-done.32 = bf16[256,1024]{1,0:T(8,128)(2,1)} collective-permute-done((bf16[256,1024]{1,0:T(8,128)(2,1)}, bf16[256,1024]{1,0:T(8,128)(2,1)}, u32[]{:S(2)}, u32[]{:S(2)}) %collective-permute-start.32) | collective-permute-done | bytes 524320 | tf_op jit(solution)/shard_map/ppermute | solution.py:573
  557.4 24.6 %collective-permute-done.37 = bf16[2,512,256]{2,1,0:T(8,128)(2,1)} collective-permute-done((bf16[2,512,256]{2,1,0:T(8,128)(2,1)S(1)}, bf16[2,512,256]{2,1,0:T(8,128)(2,1)}, u32[]{:S(2)}, u32[]{:S(2)}) %collective-permute-start.37) | collective-permute-done | bytes 524320 | tf_op jit(solution)/shard_map/ppermute | solution.py:573
  585.2 23.5 %attn_bwd.3 = (bf16[256,1024]{1,0:T(8,128)(2,1)}, bf16[256,1024]{1,0:T(8,128)(2,1)}, bf16[256,1024]{1,0:T(8,128)(2,1)}, bf16[256,1024]{1,0:T(8,128)(2,1)}, bf16[1024,768]{1,0:T(8,128)(2,1)}, /*index=5*/f32[1,1024]{1,0:T(1,128)}) custom-call(s32[4]{0:T(128)} %add_multiply_fusion.2.starts_ref, bf16[256,1024]{1,0:T(8,128)(2,1)} %get-tuple-element.151.refs_0_, ...), custom_call_target="tpu_custom_call" | custom-call | flops 17999998976 | bytes 65000000 | tf_op jit(solution)/shard_map/attn_bwd/pallas_call | solution.py:284
  630.0 7.6 %collective-permute-done.39 = bf16[256,1024]{1,0:T(8,128)(2,1)S(1)} collective-permute-done((bf16[256,1024]{1,0:T(8,128)(2,1)}, bf16[256,1024]{1,0:T(8,128)(2,1)S(1)}, u32[]{:S(2)}, u32[]{:S(2)}) %collective-permute-start.39) | collective-permute-done | bytes 524320 | tf_op jit(solution)/shard_map/ppermute | solution.py:573
  637.6 9.0 %collective-permute-done.40 = bf16[256,1024]{1,0:T(8,128)(2,1)S(1)} collective-permute-done((bf16[256,1024]{1,0:T(8,128)(2,1)}, bf16[256,1024]{1,0:T(8,128)(2,1)S(1)}, u32[]{:S(2)}, u32[]{:S(2)}) %collective-permute-start.40) | collective-permute-done | bytes 524320 | tf_op jit(solution)/shard_map/ppermute | solution.py:573
  665.7 41.5 %reduce-scatter.12.cloned.1.call-done = bf16[256,1024]{1,0:T(8,128)(2,1)} async-done(((bf16[2048,1024]{1,0:T(8,128)(2,1)}), bf16[256,1024]{1,0:T(8,128)(2,1)}) %reduce-scatter.12.cloned.1.call-update) | async-done | bytes 524304 | tf_op jit(solution)/shard_map/reduce_scatter | solution.py:648
  (311 shorter events, 154.7 us)
Async XLA Ops:
  7.2 32.3 %all-gather.6.cloned.1.call-start = ((), (), s32[]{:S(2)}) async-start(), calls=%async_computation.5 | async-start | bytes 1769472 | tf_op jit(solution)/shard_map/all_gather | solution.py:644
  9.9 92.7 %all-gather.8.cloned.1.call-start = ((), (), s32[]{:S(2)}) async-start(), calls=%async_computation.6 | async-start | bytes 5308416 | tf_op jit(solution)/shard_map/all_gather | solution.py:644
  39.5 186.7 %all-gather.10.cloned.1.call-start = ((), (), s32[]{:S(2)}) async-start(), calls=%async_computation.7 | async-start | bytes 4718592 | tf_op jit(solution)/shard_map/all_gather | solution.py:644
  102.6 216.0 %all-gather.12.cloned.1.call-start = ((), (), s32[]{:S(2)}) async-start(), calls=%async_computation.8 | async-start | bytes 4718592 | tf_op jit(solution)/shard_map/all_gather | solution.py:644
  118.2 93.5 %collective-permute-start.13 = (bf16[4,256,1024]{2,1,0:T(8,128)(2,1)}, bf16[4,256,1024]{2,1,0:T(8,128)(2,1)}, u32[]{:S(2)}, u32[]{:S(2)}) collective-permute-start(bf16[4,256,1024]{2,1,0:T(8,128)(2,1)} %refs_2_.1), channel_id=1, source_target_pairs={{0,16},{8,24},{16,0},{24,8},{1,17},{9,25},{17,1},{25,9},{2,18},{10... | collective-permute-start | bytes 6291464 | tf_op jit(solution)/shard_map/ppermute | solution.py:573
  120.0 91.7 %collective-permute-start.12 = (bf16[4,256,1024]{2,1,0:T(8,128)(2,1)}, bf16[4,256,1024]{2,1,0:T(8,128)(2,1)}, u32[]{:S(2)}, u32[]{:S(2)}) collective-permute-start(bf16[4,256,1024]{2,1,0:T(8,128)(2,1)} %refs_2_.1), channel_id=1, source_target_pairs={{0,8},{8,0},{16,24},{24,16},{1,9},{9,1},{17,25},{25,17},{2,10},{10... | collective-permute-start | bytes 6291464 | tf_op jit(solution)/shard_map/ppermute | solution.py:573
  120.4 59.5 %collective-permute-start.9 = (bf16[256,1024]{1,0:T(8,128)(2,1)}, bf16[256,1024]{1,0:T(8,128)(2,1)S(1)}, u32[]{:S(2)}, u32[]{:S(2)}) collective-permute-start(bf16[256,1024]{1,0:T(8,128)(2,1)} %get-tuple-element.165), channel_id=1, source_target_pairs={{0,8},{8,0},{16,24},{24,16},{1,9},{9,1},{17,25},{25,17},{2,10},{10... | collective-permute-start | bytes 1572872 | tf_op jit(solution)/shard_map/ppermute | solution.py:573
  122.0 58.2 %collective-permute-start.10 = (bf16[256,1024]{1,0:T(8,128)(2,1)}, bf16[256,1024]{1,0:T(8,128)(2,1)S(1)}, u32[]{:S(2)}, u32[]{:S(2)}) collective-permute-start(bf16[256,1024]{1,0:T(8,128)(2,1)} %get-tuple-element.166), channel_id=1, source_target_pairs={{0,16},{8,24},{16,0},{24,8},{1,17},{9,25},{17,1},{25,9},{2,18},{10... | collective-permute-start | bytes 1572872 | tf_op jit(solution)/shard_map/ppermute | solution.py:573
  122.3 68.6 %collective-permute-start.11 = (bf16[256,1024]{1,0:T(8,128)(2,1)}, bf16[256,1024]{1,0:T(8,128)(2,1)S(1)}, u32[]{:S(2)}, u32[]{:S(2)}) collective-permute-start(bf16[256,1024]{1,0:T(8,128)(2,1)} %get-tuple-element.167), channel_id=1, source_target_pairs={{0,24},{8,16},{16,8},{24,0},{1,25},{9,17},{17,9},{25,1},{2,26},{10... | collective-permute-start | bytes 1572872 | tf_op jit(solution)/shard_map/ppermute | solution.py:573
  179.9 31.1 %collective-permute-start.15 = (bf16[4,512,256]{2,1,0:T(8,128)(2,1)}, bf16[4,512,256]{2,1,0:T(8,128)(2,1)}, u32[]{:S(2)}, u32[]{:S(2)}) collective-permute-start(bf16[4,512,256]{2,1,0:T(8,128)(2,1)} %refs_7_.1), channel_id=1, source_target_pairs={{0,16},{8,24},{16,0},{24,8},{1,17},{9,25},{17,1},{25,9},{2,18},{10... | collective-permute-start | bytes 3145736 | tf_op jit(solution)/shard_map/ppermute | solution.py:573
  180.2 31.5 %collective-permute-start.14 = (bf16[4,512,256]{2,1,0:T(8,128)(2,1)}, bf16[4,512,256]{2,1,0:T(8,128)(2,1)}, u32[]{:S(2)}, u32[]{:S(2)}) collective-permute-start(bf16[4,512,256]{2,1,0:T(8,128)(2,1)} %refs_7_.1), channel_id=1, source_target_pairs={{0,8},{8,0},{16,24},{24,16},{1,9},{9,1},{17,25},{25,17},{2,10},{10... | collective-permute-start | bytes 3145736 | tf_op jit(solution)/shard_map/ppermute | solution.py:573
  211.7 106.9 %all-gather.14.cloned.1.call-start = ((), (), s32[]{:S(2)}) async-start(), calls=%async_computation.9 | async-start | bytes 5308416 | tf_op jit(solution)/shard_map/all_gather | solution.py:644
  212.3 223.4 %reduce-scatter.8.cloned.1.call-start = ((), (), s32[]{:S(2)}) async-start(), calls=%async_computation.11 | async-start | bytes 5308416 | tf_op jit(solution)/shard_map/reduce_scatter | solution.py:648
  215.9 35.4 %collective-permute-start.16 = (bf16[2,256,1024]{2,1,0:T(8,128)(2,1)}, bf16[2,256,1024]{2,1,0:T(8,128)(2,1)}, u32[]{:S(2)}, u32[]{:S(2)}) collective-permute-start(bf16[2,256,1024]{2,1,0:T(8,128)(2,1)} %slice.125), channel_id=1, source_target_pairs={{0,8},{8,0},{16,24},{24,16},{1,9},{9,1},{17,25},{25,17},{2,10},{10... | collective-permute-start | bytes 3145736 | tf_op jit(solution)/shard_map/ppermute | solution.py:573
  216.3 35.1 %collective-permute-start.17 = (bf16[2,256,1024]{2,1,0:T(8,128)(2,1)S(1)}, bf16[2,256,1024]{2,1,0:T(8,128)(2,1)}, u32[]{:S(2)}, u32[]{:S(2)}) collective-permute-start(bf16[2,256,1024]{2,1,0:T(8,128)(2,1)S(1)} %slice.126), channel_id=1, source_target_pairs={{0,16},{8,24},{16,0},{24,8},{1,17},{9,25},{17,1},{25,9},{2,18},{10... | collective-permute-start | bytes 3145736 | tf_op jit(solution)/shard_map/ppermute | solution.py:573
  318.5 209.0 %reduce-scatter.6.cloned.1.call-start = ((), (), s32[]{:S(2)}) async-start(), calls=%async_computation.10 | async-start | bytes 5308416 | tf_op jit(solution)/shard_map/reduce_scatter | solution.py:648
  403.9 218.3 %reduce-scatter.10.cloned.1.call-start = ((), (), s32[]{:S(2)}) async-start(), calls=%async_computation.12 | async-start | bytes 4718592 | tf_op jit(solution)/shard_map/reduce_scatter | solution.py:648
  410.8 68.9 %collective-permute-start.20 = (bf16[2,256,1024]{2,1,0:T(8,128)(2,1)}, bf16[2,256,1024]{2,1,0:T(8,128)(2,1)}, u32[]{:S(2)}, u32[]{:S(2)}) collective-permute-start(bf16[2,256,1024]{2,1,0:T(8,128)(2,1)} %get-tuple-element.214), channel_id=1, source_target_pairs={{0,8},{8,0},{16,24},{24,16},{1,9},{9,1},{17,25},{25,17},{2,10},{10... | collective-permute-start | bytes 3145736 | tf_op jit(solution)/shard_map/ppermute | solution.py:573
  419.2 105.3 %collective-permute-start.21 = (bf16[2,256,1024]{2,1,0:T(8,128)(2,1)}, bf16[2,256,1024]{2,1,0:T(8,128)(2,1)}, u32[]{:S(2)}, u32[]{:S(2)}) collective-permute-start(bf16[2,256,1024]{2,1,0:T(8,128)(2,1)} %get-tuple-element.216), channel_id=1, source_target_pairs={{0,16},{8,24},{16,0},{24,8},{1,17},{9,25},{17,1},{25,9},{2,18},{10... | collective-permute-start | bytes 3145736 | tf_op jit(solution)/shard_map/ppermute | solution.py:573
  430.5 45.0 %collective-permute-start.22 = (bf16[2,256,1024]{2,1,0:T(8,128)(2,1)}, bf16[2,256,1024]{2,1,0:T(8,128)(2,1)}, u32[]{:S(2)}, u32[]{:S(2)}) collective-permute-start(bf16[2,256,1024]{2,1,0:T(8,128)(2,1)} %get-tuple-element.218), channel_id=1, source_target_pairs={{0,8},{8,0},{16,24},{24,16},{1,9},{9,1},{17,25},{25,17},{2,10},{10... | collective-permute-start | bytes 3145736 | tf_op jit(solution)/shard_map/ppermute | solution.py:573
  441.5 45.7 %collective-permute-start.30 = (bf16[256,1024]{1,0:T(8,128)(2,1)S(1)}, bf16[256,1024]{1,0:T(8,128)(2,1)S(1)}, u32[]{:S(2)}, u32[]{:S(2)}) collective-permute-start(bf16[256,1024]{1,0:T(8,128)(2,1)S(1)} %get-tuple-element.322.refs_15_), channel_id=1, source_target_pairs={{0,24},{8,16},{16,8},{24,0},{1,25},{9,17},{17,9},{25,1},{2,26},{10... | collective-permute-start | bytes 1572872 | tf_op jit(solution)/shard_map/ppermute | solution.py:573
  442.6 44.6 %collective-permute-start.29 = (bf16[256,1024]{1,0:T(8,128)(2,1)S(1)}, bf16[256,1024]{1,0:T(8,128)(2,1)S(1)}, u32[]{:S(2)}, u32[]{:S(2)}) collective-permute-start(bf16[256,1024]{1,0:T(8,128)(2,1)S(1)} %get-tuple-element.322.refs_15_), channel_id=1, source_target_pairs={{0,16},{8,24},{16,0},{24,8},{1,17},{9,25},{17,1},{25,9},{2,18},{10... | collective-permute-start | bytes 1572872 | tf_op jit(solution)/shard_map/ppermute | solution.py:573
  479.7 43.4 %collective-permute-start.23 = (bf16[2,256,1024]{2,1,0:T(8,128)(2,1)}, bf16[2,256,1024]{2,1,0:T(8,128)(2,1)S(1)}, u32[]{:S(2)}, u32[]{:S(2)}) collective-permute-start(bf16[2,256,1024]{2,1,0:T(8,128)(2,1)} %get-tuple-element.220), channel_id=1, source_target_pairs={{0,16},{8,24},{16,0},{24,8},{1,17},{9,25},{17,1},{25,9},{2,18},{10... | collective-permute-start | bytes 3145736 | tf_op jit(solution)/shard_map/ppermute | solution.py:573
  542.8 117.2 %reduce-scatter.14.cloned.1.call-start = ((), (), s32[]{:S(2)}) async-start(), calls=%async_computation.14 | async-start | bytes 1880064 | tf_op jit(solution)/shard_map/reduce_scatter | solution.py:648
  549.9 35.2 %collective-permute-start.36 = (bf16[256,1024]{1,0:T(8,128)(2,1)}, bf16[256,1024]{1,0:T(8,128)(2,1)}, u32[]{:S(2)}, u32[]{:S(2)}) collective-permute-start(bf16[256,1024]{1,0:T(8,128)(2,1)} %get-tuple-element.257.refs_15_), channel_id=1, source_target_pairs={{0,24},{8,16},{16,8},{24,0},{1,25},{9,17},{17,9},{25,1},{2,26},{10... | collective-permute-start | bytes 1572872 | tf_op jit(solution)/shard_map/ppermute | solution.py:573
  551.1 34.1 %collective-permute-start.35 = (bf16[256,1024]{1,0:T(8,128)(2,1)}, bf16[256,1024]{1,0:T(8,128)(2,1)}, u32[]{:S(2)}, u32[]{:S(2)}) collective-permute-start(bf16[256,1024]{1,0:T(8,128)(2,1)} %get-tuple-element.257.refs_15_), channel_id=1, source_target_pairs={{0,16},{8,24},{16,0},{24,8},{1,17},{9,25},{17,1},{25,9},{2,18},{10... | collective-permute-start | bytes 1572872 | tf_op jit(solution)/shard_map/ppermute | solution.py:573
  552.5 32.7 %collective-permute-start.34 = (bf16[256,1024]{1,0:T(8,128)(2,1)}, bf16[256,1024]{1,0:T(8,128)(2,1)}, u32[]{:S(2)}, u32[]{:S(2)}) collective-permute-start(bf16[256,1024]{1,0:T(8,128)(2,1)} %get-tuple-element.257.refs_15_), channel_id=1, source_target_pairs={{0,8},{8,0},{16,24},{24,16},{1,9},{9,1},{17,25},{25,17},{2,10},{10... | collective-permute-start | bytes 1572872 | tf_op jit(solution)/shard_map/ppermute | solution.py:573
  553.4 28.5 %collective-permute-start.37 = (bf16[2,512,256]{2,1,0:T(8,128)(2,1)S(1)}, bf16[2,512,256]{2,1,0:T(8,128)(2,1)}, u32[]{:S(2)}, u32[]{:S(2)}) collective-permute-start(bf16[2,512,256]{2,1,0:T(8,128)(2,1)S(1)} %copy-done.25), channel_id=1, source_target_pairs={{0,16},{8,24},{16,0},{24,8},{1,17},{9,25},{17,1},{25,9},{2,18},{10... | collective-permute-start | bytes 1572872 | tf_op jit(solution)/shard_map/ppermute | solution.py:573
  554.2 29.6 %collective-permute-start.38 = (bf16[2,512,256]{2,1,0:T(8,128)(2,1)}, bf16[2,512,256]{2,1,0:T(8,128)(2,1)}, u32[]{:S(2)}, u32[]{:S(2)}) collective-permute-start(bf16[2,512,256]{2,1,0:T(8,128)(2,1)} %add_convert_fusion.4), channel_id=1, source_target_pairs={{0,8},{8,0},{16,24},{24,16},{1,9},{9,1},{17,25},{25,17},{2,10},{10... | collective-permute-start | bytes 1572872 | tf_op jit(solution)/shard_map/ppermute | solution.py:573
  581.9 36.8 %collective-permute-start.42 = (bf16[2,256,1024]{2,1,0:T(8,128)(2,1)}, bf16[2,256,1024]{2,1,0:T(8,128)(2,1)S(1)}, u32[]{:S(2)}, u32[]{:S(2)}) collective-permute-start(bf16[2,256,1024]{2,1,0:T(8,128)(2,1)} %add_convert_fusion.1), channel_id=1, source_target_pairs={{0,16},{8,24},{16,0},{24,8},{1,17},{9,25},{17,1},{25,9},{2,18},{10... | collective-permute-start | bytes 3145736 | tf_op jit(solution)/shard_map/ppermute | solution.py:573
  583.8 34.9 %collective-permute-start.43 = (bf16[2,256,1024]{2,1,0:T(8,128)(2,1)}, bf16[2,256,1024]{2,1,0:T(8,128)(2,1)}, u32[]{:S(2)}, u32[]{:S(2)}) collective-permute-start(bf16[2,256,1024]{2,1,0:T(8,128)(2,1)} %add_convert_fusion), channel_id=1, source_target_pairs={{0,8},{8,0},{16,24},{24,16},{1,9},{9,1},{17,25},{25,17},{2,10},{10... | collective-permute-start | bytes 3145736 | tf_op jit(solution)/shard_map/ppermute | solution.py:573
  621.9 85.3 %reduce-scatter.12.cloned.1.call-start = ((), (), s32[]{:S(2)}) async-start(), calls=%async_computation.13 | async-start | bytes 4718592 | tf_op jit(solution)/shard_map/reduce_scatter | solution.py:648
  (79 other events, 1273.3 us)
Sparse Core Ops, SparseCore 0:
  10.2 27.9 all-gather.5
  40.4 50.8 all-gather.7
  102.7 47.3 all-gather.9
  211.9 46.9 all-gather.11
  260.4 49.9 all-gather.13
  318.7 55.0 reduce-scatter.7
  404.0 55.1 reduce-scatter.5
  543.0 50.0 reduce-scatter.9
  622.0 34.7 reduce-scatter.13
  658.9 48.2 reduce-scatter.11

commit v3 on v2

--- a/solution.py
+++ b/solution.py
@@ -34,7 +34,7 @@
 
 def cost(gflops, megabytes):
     return pl.CostEstimate(
-        flops=int(gflops * 1e9), transcendentals=0, bytes_accessed=int(megabytes * 1e6)
+        flops=int(gflops * 1e6), transcendentals=0, bytes_accessed=int(megabytes * 1e3)
     )
 
 
@@ -303,13 +303,18 @@
     return results[:count], results[count:]
 
 
-def dispatch_body(
-    offset_ref, x_ref, gm_ref, router_ref, xd_ref, gd_ref, pt_ref, pgt_ref, *, local
-):
-    rows = x_ref.shape[0]
+def dispatch_body(offset_ref, *refs, local, count):
+    ins, (router_ref, xd_ref, gd_ref, pt_ref, pgt_ref) = refs[:count], refs[count:]
+    rows = ins[0].shape[0]
     slots = local * CAP
-    x = x_ref[...]
-    mask = gm_ref[:, MODEL_WIDTH:]
+    if count == 1:
+        x = ins[0][:, :MODEL_WIDTH]
+        grad = ins[0][:, MODEL_WIDTH : 2 * MODEL_WIDTH]
+        mask = ins[0][:, 2 * MODEL_WIDTH :]
+    else:
+        x = ins[0][...]
+        grad = ins[1][:, :MODEL_WIDTH]
+        mask = ins[1][:, MODEL_WIDTH:]
     chosen = mask.astype(f32) > 0.0
     logits = jnp.where(chosen, dot(x, router_ref[...]), masked_score)
     expo = jnp.where(chosen, jnp.exp(logits - jnp.max(logits, axis=-1, keepdims=True)), 0.0)
@@ -342,30 +347,29 @@
     send = jnp.where(hit, 1.0, 0.0).astype(bf16)
     send_gated = jnp.where(hit, dot_nt(spread, gates), 0.0).astype(bf16)
     xd_ref[...] = dot(send, x).astype(bf16).reshape(xd_ref.shape)
-    gd_ref[...] = (
-        (dot(send_gated, gm_ref[:, :MODEL_WIDTH]) * residual_scale).astype(bf16)
-    ).reshape(gd_ref.shape)
+    gd_ref[...] = ((dot(send_gated, grad) * residual_scale).astype(bf16)).reshape(gd_ref.shape)
     spread = pick((LANES, slots), 1)
     hit = dot(place, spread) == in_slot((rows, slots), 1)
     pt_ref[...] = jnp.where(hit, 1.0, 0.0).astype(bf16)
     pgt_ref[...] = jnp.where(hit, dot(gates, spread), 0.0).astype(bf16)
 
 
-def dispatch(offset, x, gm, router, local):
-    blocks = x.shape[0] // ROW_BLOCK
+def dispatch(offset, sources, router, local):
+    total = sources[0].shape[0]
+    blocks = total // ROW_BLOCK
     slots = local * CAP
     slotted = jax.ShapeDtypeStruct((local, blocks, CAP, MODEL_WIDTH), bf16)
     slotted_spec = pl.BlockSpec((local, 1, CAP, MODEL_WIDTH), lambda s, o: (0, s, 0, 0))
     return pl.pallas_call(
-        functools.partial(dispatch_body, local=local),
+        functools.partial(dispatch_body, local=local, count=len(sources)),
         grid_spec=pltpu.PrefetchScalarGridSpec(
             num_scalar_prefetch=1,
             grid=(blocks,),
             in_specs=[
-                pl.BlockSpec((ROW_BLOCK, MODEL_WIDTH), lambda s, o: (s, 0)),
-                pl.BlockSpec((ROW_BLOCK, MODEL_WIDTH + LANES), lambda s, o: (s, 0)),
-                pl.BlockSpec((MODEL_WIDTH, LANES), lambda s, o: (0, 0)),
-            ],
+                pl.BlockSpec((ROW_BLOCK, source.shape[1]), lambda s, o: (s, 0))
+                for source in sources
+            ]
+            + [pl.BlockSpec((MODEL_WIDTH, LANES), lambda s, o: (0, 0))],
             out_specs=[
                 slotted_spec,
                 slotted_spec,
@@ -376,51 +380,74 @@
         out_shape=(
             slotted,
             slotted,
-            jax.ShapeDtypeStruct((x.shape[0], slots), bf16),
-            jax.ShapeDtypeStruct((x.shape[0], slots), bf16),
+            jax.ShapeDtypeStruct((total, slots), bf16),
+            jax.ShapeDtypeStruct((total, slots), bf16),
         ),
         compiler_params=row_params,
         cost_estimate=cost(11.0, 40.0),
         name="dispatch",
-    )(offset, x, gm, router)
-
-
-def experts_body(place_ref, *refs, count, carried):
-    xd_ref, gd_ref, refs = refs[0], refs[1], refs[2:]
-    tables = count + 1 if count > 1 else count
-    gu_pieces, d_pieces, refs = refs[:tables], refs[tables : 2 * tables], refs[2 * tables :]
-    tables = 2 * count if count > 1 else count
-    old, refs = (refs[: 2 * tables], refs[2 * tables :]) if carried else ((), refs)
+    )(offset, *sources, router)
+
+
+def pack_weights(gate_up, down):
+    gu_rows = gate_up.shape[1]
+    count = MODEL_WIDTH // gu_rows
+    cut = FF // count
+    side = [down[:, k * cut : (k + 1) * cut, :] for k in range(count)]
+    return jnp.concatenate([gate_up, jnp.concatenate(side, axis=2)], axis=1)
+
+
+def unpack_weights(packed, gu_rows):
+    count = MODEL_WIDTH // gu_rows
+    side = packed[:, gu_rows:]
+    side = [side[:, :, k * gu_rows : (k + 1) * gu_rows] for k in range(count)]
+    return packed[:, :gu_rows], jnp.concatenate(side, axis=1)
+
+
+def experts_body(place_ref, xd_ref, gd_ref, *refs, base, slices, carried):
+    paired = slices == 4
+    kinds = 5 if paired else 1
+    w_refs, refs = refs[:kinds], refs[kinds:]
+    old, refs = (refs[:kinds], refs[kinds:]) if carried else ((), refs)
     out_ref, dx_ref, h_ref = refs[:3]
-    grad_refs = refs[3 : 3 + 2 * tables]
-    wgu_ref, wd_ref, act_sc, dh_sc = refs[3 + 2 * tables :]
+    grad_refs = refs[3 : 3 + kinds]
+    wgu_ref, wd_ref, act_sc, dh_sc = refs[3 + kinds :]
     expert = pl.program_id(0)
-    half = pl.num_programs(0) // 2
-
-    def starts(index, rows):
-        return pl.multiple_of(place_ref[1 + index] * rows, LANES)
-
-    def put(index, gu_piece, d_piece):
-        rows = gu_piece.shape[1]
-        begin = starts(index, rows)
-        wgu_ref[pl.ds(begin, rows), :] = gu_piece[0]
-        wd_ref[:, pl.ds(begin, rows)] = d_piece[0]
-
-    for index in range(min(count, 3)):
-        put(index, gu_pieces[index], d_pieces[index])
-    if count > 1:
-
-        @pl.when(expert < half)
+    gu_rows = MODEL_WIDTH // slices
+    cut = FF // slices
+
+    def begin_of(index):
+        if not paired:
+            return index * gu_rows
+        return pl.multiple_of(place_ref[1 + index] * gu_rows, LANES)
+
+    def put(index, ref, *lead):
+        begin = begin_of(index)
+        wgu_ref[pl.ds(begin, gu_rows), :] = ref[(*lead, slice(0, gu_rows), slice(None))]
+        for k in range(slices):
+            wd_ref[k * cut : (k + 1) * cut, pl.ds(begin, gu_rows)] = ref[
+                (*lead, slice(gu_rows, gu_rows + cut), slice(k * gu_rows, (k + 1) * gu_rows))
+            ]
+
+    if paired:
+        for index in range(3):
+            put(index, w_refs[index], 0)
+
+        @pl.when(expert == 0)
         def _():
-            put(3, gu_pieces[3], d_pieces[3])
-
-        @pl.when(expert >= half)
+            put(3, w_refs[3], 0)
+
+        @pl.when(expert == 1)
         def _():
-            put(3, gu_pieces[4], d_pieces[4])
+            put(3, w_refs[4], 0)
+
+    else:
+        for index in range(slices):
+            put(index, w_refs[0], index, 0)
 
     total = xd_ref.shape[1]
     chunk = ROW_BLOCK
-    own = place_ref[0] + expert
+    own = place_ref[0] + expert + base
     lane = lax.broadcasted_iota(jnp.int32, (chunk, LANES), 1)
 
     def chunk_step(index):
@@ -444,70 +471,72 @@
         dx_ref[0, rows, :] = dot_nt(dh_sc[rows, :], wgu_ref[...]).astype(bf16)
 
     for_blocks(total // chunk, chunk_step)
-    def put_grad(index, value):
+
+    def put_grad(kind, lead, gate_up, down):
+        ref = grad_refs[kind]
+        at = (*lead, slice(0, gu_rows), slice(None))
         if carried:
-            value = value + old[index][0].astype(f32)
-        grad_refs[index][0] = value.astype(bf16)
-
-    def put_halves(index, value):
-        if count == 1:
-            put_grad(index, value)
-            return
-
-        @pl.when(expert < half)
+            gate_up = gate_up + old[kind][at].astype(f32)
+        ref[at] = gate_up.astype(bf16)
+        for k in range(slices):
+            at = (*lead, slice(gu_rows, gu_rows + cut), slice(k * gu_rows, (k + 1) * gu_rows))
+            value = down[k * cut : (k + 1) * cut, :]
+            if carried:
+                value = value + old[kind][at].astype(f32)
+            ref[at] = value.astype(bf16)
+
+    targets = (
+        ((0, 0), (1, 0), (3, 0), (1, 1)),
+        ((0, 1), (4, 0), (2, 0), (2, 1)),
+    )
+    for index in range(slices):
+        begin = begin_of(index)
+        gate_up = dot_tn(xd_ref[0, :, pl.ds(begin, gu_rows)], dh_sc[...])
+        down = dot_tn(act_sc[...], gd_ref[0, :, pl.ds(begin, gu_rows)])
+        if not paired:
+            put_grad(0, (index, 0), gate_up, down)
+            continue
+
+        @pl.when(expert == 0)
         def _():
-            put_grad(2 * index, value)
-
-        @pl.when(expert >= half)
+            kind, lead = targets[0][index]
+            put_grad(kind, (lead,), gate_up, down)
+
+        @pl.when(expert == 1)
         def _():
-            put_grad(2 * index + 1, value)
-
-    for index in range(count):
-        rows = grad_refs[0].shape[1]
-        begin = starts(index, rows)
-        put_halves(index, dot_tn(xd_ref[0, :, pl.ds(begin, rows)], dh_sc[...]))
-        put_halves(count + index, dot_tn(act_sc[...], gd_ref[0, :, pl.ds(begin, rows)]))
-
-
-def run_experts(place, xd, gd, gu_pieces, d_pieces, old):
-    local, total = xd.shape[:2]
-    count = place.shape[0] - 1
-    rows = MODEL_WIDTH // count
-
-    def spec(a, b):
-        return pl.BlockSpec((1, a, b), lambda e, o: (e, 0, 0))
-
-    half = local // 2
-
-    def half_specs(a, b):
-        return [
-            pl.BlockSpec((1, a, b), lambda e, o: (jnp.minimum(e, half - 1), 0, 0)),
-            pl.BlockSpec((1, a, b), lambda e, o: (jnp.maximum(e - half, 0), 0, 0)),
-        ]
-
-    def piece_specs(a, b):
-        specs = [spec(a, b)] * min(count, 3)
-        return specs + half_specs(a, b) if count > 1 else specs
-
-    row_spec = spec(total, MODEL_WIDTH)
-    if count > 1:
-        both = half_specs(rows, 2 * FF), half_specs(FF, rows)
-        grad_specs = both[0] * count + both[1] * count
-        grad_rows = local // 2
+            kind, lead = targets[1][index]
+            put_grad(kind, (lead,), gate_up, down)
+
+
+def run_experts(place, xd, gd, pieces, old, base, here, slices):
+    total = xd.shape[1]
+    paired = slices == 4
+    packed = (MODEL_WIDTH + FF) // slices
+
+    def spec(rows, width, first=0):
+        return pl.BlockSpec((1, rows, width), lambda e, o: (e + first, 0, 0))
+
+    def fixed(count):
+        return pl.BlockSpec((count, packed, MODEL_WIDTH), lambda e, o: (0, 0, 0))
+
+    if paired:
+        w_specs = [spec(packed, MODEL_WIDTH)] * 3 + [fixed(1)] * 2
+        counts = (2, 2, 2, 1, 1)
+        grad_specs = [fixed(count) for count in counts]
+        grad_shapes = tuple(
+            jax.ShapeDtypeStruct((count, packed, MODEL_WIDTH), bf16) for count in counts
+        )
     else:
-        grad_specs = [spec(rows, 2 * FF), spec(FF, rows)]
-        grad_rows = local
-    repeats = len(grad_specs) // 2
+        w_specs = [pl.BlockSpec((slices, 1, packed, MODEL_WIDTH), lambda e, o: (0, e, 0, 0))]
+        grad_specs = w_specs
+        grad_shapes = (jax.ShapeDtypeStruct((slices, here, packed, MODEL_WIDTH), bf16),)
     results = pl.pallas_call(
-        functools.partial(experts_body, count=count, carried=bool(old)),
+        functools.partial(experts_body, base=base, slices=slices, carried=bool(old)),
         grid_spec=pltpu.PrefetchScalarGridSpec(
             num_scalar_prefetch=1,
-            grid=(local,),
-            in_specs=[row_spec, row_spec]
-            + piece_specs(rows, 2 * FF)
-            + piece_specs(FF, rows)
-            + (grad_specs if old else []),
-            out_specs=[row_spec, row_spec, spec(total, LANES)] + grad_specs,
+            grid=(here,),
+            in_specs=[spec(total, MODEL_WIDTH, base)] * 2 + w_specs + (grad_specs if old else []),
+            out_specs=[spec(total, MODEL_WIDTH)] * 2 + [spec(total, LANES)] + grad_specs,
             scratch_shapes=[
                 pltpu.VMEM((MODEL_WIDTH, 2 * FF), bf16),
                 pltpu.VMEM((FF, MODEL_WIDTH), bf16),
@@ -516,57 +545,73 @@
             ],
         ),
         out_shape=(
-            jax.ShapeDtypeStruct((local, total, MODEL_WIDTH), bf16),
-            jax.ShapeDtypeStruct((local, total, MODEL_WIDTH), bf16),
-            jax.ShapeDtypeStruct((local, total, LANES), bf16),
+            jax.ShapeDtypeStruct((here, total, MODEL_WIDTH), bf16),
+            jax.ShapeDtypeStruct((here, total, MODEL_WIDTH), bf16),
+            jax.ShapeDtypeStruct((here, total, LANES), bf16),
         )
-        + (jax.ShapeDtypeStruct((grad_rows, rows, 2 * FF), bf16),) * repeats
-        + (jax.ShapeDtypeStruct((grad_rows, FF, rows), bf16),) * repeats,
+        + grad_shapes,
         compiler_params=row_params,
-        cost_estimate=cost(30.0, 110.0),
+        cost_estimate=cost(20.0, 60.0),
         name="experts",
-    )(place, xd, gd, *gu_pieces, *d_pieces, *old)
+    )(place, xd, gd, *pieces, *old)
     return results[:3], results[3:]
 
 
-def combine_body(out_ref, dx_ref, h_ref, pt_ref, pgt_ref, mix_ref, grad_ref):
+def whole_slots(refs, slots, width):
+    return jnp.concatenate(
+        [ref[...].reshape(slots // len(refs), width) for ref in refs], axis=0
+    )
+
+
+def combine_grad_body(*refs, count):
+    dx_refs, h_refs, (pt_ref, grad_ref) = refs[:count], refs[count : 2 * count], refs[2 * count :]
     slots = pt_ref.shape[1]
-    mix_ref[...] = dot(pgt_ref[...], out_ref[...].reshape(slots, MODEL_WIDTH)).astype(bf16)
     grad_ref[:, :MODEL_WIDTH] = dot(
-        pt_ref[...], dx_ref[...].reshape(slots, MODEL_WIDTH)
+        pt_ref[...], whole_slots(dx_refs, slots, MODEL_WIDTH)
     ).astype(bf16)
-    grad_ref[:, MODEL_WIDTH:] = dot(pt_ref[...], h_ref[...].reshape(slots, LANES)).astype(bf16)
-
-
-def combine(out, dx, h, pt, pgt):
-    local = out.shape[0]
-    blocks = pt.shape[0] // ROW_BLOCK
-    slots = pt.shape[1]
-
-    def slotted(array):
-        return array.reshape(local, blocks, CAP, array.shape[-1])
-
-    def spec(width):
-        return pl.BlockSpec((local, 1, CAP, width), lambda s: (0, s, 0, 0))
-
-    def row_spec(width):
-        return pl.BlockSpec((ROW_BLOCK, width), lambda s: (s, 0))
-
+    grad_ref[:, MODEL_WIDTH:] = dot(pt_ref[...], whole_slots(h_refs, slots, LANES)).astype(bf16)
+
+
+def combine_mix_body(*refs, count):
+    out_refs, (pgt_ref, mix_ref) = refs[:count], refs[count:]
+    mix_ref[...] = dot(
+        pgt_ref[...], whole_slots(out_refs, pgt_ref.shape[1], MODEL_WIDTH)
+    ).astype(bf16)
+
+
+def combine_both_body(*refs, count):
+    out_refs, dx_refs, refs = refs[:count], refs[count : 2 * count], refs[2 * count :]
+    h_refs, (pgt_ref, pt_ref, both_ref) = refs[:count], refs[count:]
+    slots = pt_ref.shape[1]
+    both_ref[:, :MODEL_WIDTH] = dot(
+        pgt_ref[...], whole_slots(out_refs, slots, MODEL_WIDTH)
+    ).astype(bf16)
+    both_ref[:, MODEL_WIDTH : 2 * MODEL_WIDTH] = dot(
+        pt_ref[...], whole_slots(dx_refs, slots, MODEL_WIDTH)
+    ).astype(bf16)
+    both_ref[:, 2 * MODEL_WIDTH :] = dot(
+        pt_ref[...], whole_slots(h_refs, slots, LANES)
+    ).astype(bf16)
+
+
+def combine(body, arrays, count, tables, width, name):
+    total, slots = tables[0].shape
+    blocks = total // ROW_BLOCK
+    arrays = [array.reshape(array.shape[0], blocks, CAP, array.shape[-1]) for array in arrays]
+    in_specs = [
+        pl.BlockSpec((array.shape[0], 1, CAP, array.shape[-1]), lambda s: (0, s, 0, 0))
+        for array in arrays
+    ]
     return pl.pallas_call(
-        combine_body,
+        functools.partial(body, count=count),
         grid=(blocks,),
-        in_specs=[
-            spec(MODEL_WIDTH), spec(MODEL_WIDTH), spec(LANES), row_spec(slots), row_spec(slots)
-        ],
-        out_specs=[row_spec(MODEL_WIDTH), row_spec(MODEL_WIDTH + LANES)],
-        out_shape=(
-            jax.ShapeDtypeStruct((pt.shape[0], MODEL_WIDTH), bf16),
-            jax.ShapeDtypeStruct((pt.shape[0], MODEL_WIDTH + LANES), bf16),
-        ),
+        in_specs=in_specs + [pl.BlockSpec((ROW_BLOCK, slots), lambda s: (s, 0))] * len(tables),
+        out_specs=pl.BlockSpec((ROW_BLOCK, width), lambda s: (s, 0)),
+        out_shape=jax.ShapeDtypeStruct((total, width), bf16),
         compiler_params=row_params,
-        cost_estimate=cost(9.0, 33.0),
-        name="combine",
-    )(slotted(out), slotted(dx), slotted(h), pt, pgt)
+        cost_estimate=cost(5.0, 17.0),
+        name=name,
+    )(*arrays, *tables)
 
 
 def flip(value, bits):
@@ -603,40 +648,39 @@
     return total
 
 
-def gather_weights_near(value, axis):
+def gather_weights_near(packed):
     if square():
-        return [value, flip(value, 1), flip(value, 2)]
-    return [lax.all_gather(value, "tp", axis=axis, tiled=True)]
+        return [packed, flip(packed, 1), flip(packed, 2)]
+    return [lax.all_gather(packed, "tp")]
 
 
 def gather_weights_far(near):
     if square():
-        half = near[0].shape[0] // 2
-        return [*near, flip(near[2][:half], 1), flip(near[1][half:], 2)]
+        return [*near, flip(near[2][:1], 1), flip(near[1][1:], 2)]
     return near
 
 
-def sum_weights_near(parts, axis):
+def sum_weights_near(grads):
     if square():
-        own, along_x, along_y, across = parts[0:2], parts[2:4], parts[4:6], parts[6:8]
-        top = flip(along_x[0], 1).astype(f32) + own[0].astype(f32)
-        top_far = flip(across[0], 1).astype(f32) + along_y[0].astype(f32)
-        low = flip(along_y[1], 2).astype(f32) + own[1].astype(f32)
-        low_far = flip(across[1], 2).astype(f32) + along_x[1].astype(f32)
-        return top, low, top_far.astype(bf16), low_far.astype(bf16)
-    return (lax.psum_scatter(parts[0], "tp", scatter_dimension=axis, tiled=True),)
+        return [flip(grads[1], 1), flip(grads[2], 2), *grads]
+    return [lax.psum_scatter(grads[0], "tp", scatter_dimension=0)]
 
 
 def sum_weights_far(near):
     if square():
-        top, low, top_far, low_far = near
-        return top, low, flip(top_far, 2), flip(low_far, 1)
+        came_x, came_y, own, _, _, kept_y, kept_x = [value.astype(f32) for value in near]
+        first = came_x[:1] + own[:1]
+        second = came_y[:1] + own[1:]
+        far_first = flip((came_x[1:] + kept_y).astype(bf16), 2)
+        far_second = flip((came_y[1:] + kept_x).astype(bf16), 1)
+        return [first, second, far_first, far_second]
     return near
 
 
 def add_far(far):
     if square():
-        return jnp.concatenate([far[0] + far[2], far[1] + far[3]])
+        first, second, far_first, far_second = far
+        return jnp.concatenate([first + far_first, second + far_second])
     return far[0].astype(f32)
 
 
@@ -688,6 +732,7 @@
     gain_two = norm_gains[1:2]
     router = jnp.pad(w_router, ((0, 0), (0, LANES - EXPERTS)))
 
+    slices = lax.axis_size("tp")
     weights = ag_ep(
         jnp.concatenate(
             [
@@ -702,12 +747,16 @@
         routes.reshape(micro, rows, -1)[..., None] == lanes, axis=2
     ).astype(bf16)
     tables = [rope_tables(segment_ids[m]) for m in range(micro)]
+    packed_weights = pack_weights(w_gate_up, w_down)
+    here = local // 2
+    halves = range(2)
+    packed_weights = [packed_weights[h * here : (h + 1) * here] for h in halves]
 
     token_full = []
     for m in range(micro):
-        own = after(tokens[m], token_full[-1]) if token_full else tokens[m]
+        own = after(tokens[m], token_full[-1], tables) if token_full else tokens[m]
         token_full.append(gather_rows(own))
-    weights = after(weights, token_full[0])
+    weights = after(weights, token_full[0], tables)
     fixed = []
     for m in range(micro):
         fixed.append(
@@ -716,28 +765,22 @@
                 segment_ids[m][:, None], segment_ids[m][None, :],
             )
         )
-
-    gm_full = []
+    came = []
     kept = []
-    partial = []
-    for m in range(micro):
-        parts, saved = attention_forward(*fixed[m])
-        partial.append(parts)
-        kept.append(saved)
-    weights_in = after((w_gate_up, w_down), partial)
-    gu_near = gather_weights_near(weights_in[0], 1)
-    d_near = gather_weights_near(weights_in[1], 2)
-
     hiddens = []
     normed_twos = []
     scales = []
     gate_rows = []
-    x_full = []
+    full = []
     for m in range(micro):
-        came = send_rows(partial[m])
+        if m:
+            fixed[m] = (after(starts, normed_twos), *fixed[m][1:])
+        parts, saved = attention_forward(*fixed[m])
+        kept.append(saved)
+        came.append(send_rows(parts))
         if m == 0:
-            came, token_full = lax.optimization_barrier((came, token_full))
-        branch = add_rows(after(came, normed_twos))
+            near = [gather_weights_near(after(packed_weights[0], came[0]))]
+        branch = add_rows(came[m])
         hidden = tokens[m].astype(f32) + residual_scale * branch
         scale_two = lax.rsqrt(jnp.mean(hidden * hidden, axis=-1, keepdims=True) + epsilon)
         normed_two = (hidden * scale_two * gain_two).astype(bf16)
@@ -749,48 +792,64 @@
         hiddens.append(hidden)
         normed_twos.append(normed_two)
         scales.append(scale_two)
-        if m == micro - 1:
-            normed_two, gu_near, d_near = lax.optimization_barrier((normed_two, gu_near, d_near))
-        gm = jnp.concatenate([cotangent[m], masks[m]], axis=-1)
-        gm_full.append(ag_ep(after(gm, weights if m == 0 else normed_two)))
-        x_full.append(ag_ep(after(normed_two, gm_full[m]) if m == 0 else normed_two))
-
-    gu_pieces = gather_weights_far(gu_near)
-    d_pieces = gather_weights_far(d_near)
-    old = ()
+        if m == 0:
+            gm = jnp.concatenate([cotangent[m], masks[m]], axis=-1)
+            gm = ag_ep(after(gm, weights))
+            full.append([ag_ep(after(normed_two, gm)), gm])
+        else:
+            if m == micro - 1:
+                normed_two, near[0] = lax.optimization_barrier((normed_two, near[0]))
+            full.append([ag_ep(jnp.concatenate([normed_two, cotangent[m], masks[m]], axis=-1))])
+
+    pieces = [gather_weights_far(near[0])]
+    near.append(gather_weights_near(after(packed_weights[1], near[0])))
+    old = [(), ()]
     mixes = []
     grads = []
     ready = ()
     for m in range(micro):
-        x_in = after(x_full[m], ready) if ready else x_full[m]
-        xd, gd, pt, pgt = dispatch(offset, x_in, gm_full[m], router, local)
+        sources = after(full[m], ready) if m else full[m]
+        xd, gd, pt, pgt = dispatch(offset, sources, router, local)
+        if m == 0:
+            xd, near[1] = lax.optimization_barrier((xd, near[1]))
+            pieces.append(gather_weights_far(near[1]))
         merged = (local, ep_size * CAP, MODEL_WIDTH)
-        (out, dx, h), old = run_experts(
-            place, xd.reshape(merged), gd.reshape(merged), gu_pieces, d_pieces, old
-        )
-        mix, grad = combine(out, dx, h, pt, pgt)
-        ready = (mix, grad)
-        mixes.append(mix)
-        grads.append(rs_ep(grad))
-    near_gate_up = sum_weights_near(old[: len(old) // 2], 1)
-    near_down = sum_weights_near(old[len(old) // 2 :], 2)
+        xd = xd.reshape(merged)
+        gd = gd.reshape(merged)
+        done = []
+        for h in halves:
+            results, old[h] = run_experts(
+                place, xd, gd, pieces[h], old[h], h * here, here, slices
+            )
+            done.append(results)
+        outs, dxs, hs = zip(*done)
+        if m < micro - 1:
+            both = combine(
+                combine_both_body, [*outs, *dxs, *hs], 2, [pgt, pt], 2 * MODEL_WIDTH + LANES,
+                "combine",
+            )
+            ready = both
+            both = rs_ep(both)
+            mixes.append(both[:, :MODEL_WIDTH])
+            grads.append(both[:, MODEL_WIDTH:])
+        else:
+            grad = combine(
+                combine_grad_body, [*dxs, *hs], 2, [pt], MODEL_WIDTH + LANES, "combine_grad"
+            )
+            grads.append(rs_ep(grad))
+            near_first = sum_weights_near(old[0])
+            outs, pgt, near_first = lax.optimization_barrier((*after((outs, pgt), grad), near_first))
+            mix = combine(combine_mix_body, outs, 2, [pgt], MODEL_WIDTH, "combine_mix")
+            mixes.append(rs_ep(mix))
+    far_first = sum_weights_far(near_first)
     input_grads = []
     acc_router = 0.0
     acc_gain_one = 0.0
     acc_gain_two = 0.0
     acc_weights = 0.0
+    parts = ()
     for m in range(micro):
-        grad = grads[m]
-        if m == micro - 1:
-            grad, near_gate_up, near_down, _ = lax.optimization_barrier(
-                (grad, near_gate_up, near_down, came)
-            )
-            far_down = sum_weights_far(near_down)
-            mixed = []
-            for n in range(micro):
-                mixed.append(rs_ep(after(mixes[n], grad, mixed)))
-        else:
-            grad, near_down = lax.optimization_barrier((grad, near_down))
+        grad = after(grads[m], mix, parts)
         grad = grad.astype(f32)
         h_rows = grad[:, MODEL_WIDTH:]
         grad_logits = (
@@ -808,14 +867,19 @@
         )
         acc_gain_two = acc_gain_two + jnp.sum(grad_normed * hiddens[m] * scale, axis=0)
         grad_branch = gather_rows((residual_scale * grad_hidden).astype(bf16))
+        if m == 0:
+            near_second = sum_weights_near(after(old[1], grad_branch))
+            grad_branch, far_first = lax.optimization_barrier((grad_branch, far_first))
         if m == micro - 1:
-            grad_branch, far_down = lax.optimization_barrier((grad_branch, far_down))
-            far_gate_up = sum_weights_far(near_gate_up)
+            near_second, grad_branch = lax.optimization_barrier((near_second, grad_branch))
+            far_second = sum_weights_far(near_second)
         parts, (gweights, ggain) = attention_backward(*fixed[m], kept[m], grad_branch)
-        came = send_rows(parts)
+        back = send_rows(parts)
+        if m == micro - 1:
+            gweights, far_second = lax.optimization_barrier((gweights, far_second))
         acc_weights = acc_weights + gweights.astype(f32)
         acc_gain_one = acc_gain_one + ggain[0]
-        grad_normed = add_rows(came)
+        grad_normed = add_rows(back)
         inputs = tokens[m].astype(f32)
         scale = lax.rsqrt(jnp.mean(inputs * inputs, axis=-1, keepdims=True) + epsilon)
         weighted = grad_normed * gain_one
@@ -823,13 +887,13 @@
         input_grads.append(
             grad_hidden + scale * weighted - inputs * scale * scale * scale * inner
         )
-    mixed, _ = lax.optimization_barrier((mixed, parts))
+    hiddens, mixes, far_first = after((hiddens, mixes, far_first), parts)
     outputs = [
-        (hiddens[m] + residual_scale * mixed[m].astype(f32)).astype(bf16) for m in range(micro)
+        (hiddens[m] + residual_scale * mixes[m].astype(f32)).astype(bf16) for m in range(micro)
     ]
-    acc_weights, far_gate_up = lax.optimization_barrier((acc_weights, far_gate_up))
-    grad_gate_up = add_far(far_gate_up)
-    grad_down = add_far(far_down)
+    grad_gate_up, grad_down = unpack_weights(
+        jnp.concatenate([add_far(far_first), add_far(far_second)]), w_gate_up.shape[1]
+    )
 
     small = jnp.concatenate(
         [

time: 728 us -> 664 us (0.912)
  waiting for transfers between devices: 298 us -> 225 us
  Pallas kernels: 243 us -> 253 us
  local copies, waits for them, and re-layouts: 28.9 us -> 36.7 us
    ppermute x47 -> x43, waiting for transfers between devices: 255 us -> 211 us  [flip(): return lax.ppermute(value, 'tp', [(t, t ^ bits) for t in range(4)])]
    reduce_scatter x5 -> x4, waiting for transfers between devices: 41.6 us -> 7.04 us  [rs_ep(): return lax.psum_scatter(value, 'ep', scatter_dimension=axis, tiled=True)]
    convert_element_type x4 -> x9, other arithmetic: 5.91 us -> 16.4 us  [the longest x6 8.43 us: sum_weights_far(): value.astype(f32)]
    pallas_call x6 -> x9, Pallas kernels: 167 us -> 176 us  [the longest x4 116 us: run_experts(): pl.pallas_call(functools.partial(experts_body, base=base, slices=slices,...]
    add x9 -> x4, other arithmetic: 15.8 us -> 6.9 us  [add_far(): return jnp.concatenate([first + far_first, second + far_second])]
    slice x4 -> x10, local copies, waits for them, and re-layouts: 7.35 us -> 15.2 us  [the longest x4 8.34 us: gather_weights_far(): return [*near, flip(near[2][:1], 1), flip(near[1][1:], 2)]]
    ppermute x47 -> x43, starting transfers between devices: 55.5 us -> 52.9 us  [flip(): return lax.ppermute(value, 'tp', [(t, t ^ bits) for t in range(4)])]
  transfers between devices with their start and end apart: 57 -> 51, of which waited for: 24 -> 26; matrix products, arithmetic and copies ran while one was open for 13% -> 15% of each run, Pallas kernels for 34% -> 38%
where the time goes in v3:
time: 664 us; the launch traced here: 659 us
  Pallas kernels  253 us (38%)
  waiting for transfers between devices  225 us (34%)
  other arithmetic  66.1 us (10%)
  starting transfers between devices  54.4 us (8%)
  local copies, waits for them, and re-layouts  36.7 us (6%)
  between operations  15.3 us (2%)
  matrix products  8.94 us (1%)
    ppermute x43, waiting for transfers between devices, flip(): return lax.ppermute(value, 'tp', [(t, t ^ bits) for t in range(4)])  211 us
    pallas_call x4, Pallas kernels, run_experts(): pl.pallas_call(functools.partial(experts_body, base=base, slices=slices,...  116 us
    ppermute x43, starting transfers between devices, flip(): return lax.ppermute(value, 'tp', [(t, t ^ bits) for t in range(4)])  52.9 us
    pallas_call x2, Pallas kernels, attention_backward(): pl.pallas_call(functools.partial(attention_backward_body, count=count), o...  47.4 us
    pallas_call x3, Pallas kernels, combine(): pl.pallas_call(functools.partial(body, count=count), grid=(blocks,), in_s...  31.1 us
    pallas_call x2, Pallas kernels, dispatch(): pl.pallas_call(functools.partial(dispatch_body, local=local, count=len(so...  29.5 us
    pallas_call x2, Pallas kernels, attention_forward(): pl.pallas_call(functools.partial(attention_forward_body, count=count), ou...  28.9 us
  transfers between devices with their start and end apart: 51, of which 26 were waited for; matrix products, arithmetic and copies ran while one was open for 15% of the time, Pallas kernels for 38%

profile of v3, /device:TPU:0, one launch (start us, length us, event | category | flops | bytes accessed | tf_op | source)
XLA Modules:
  0.0 658.9 jit_solution(16183109622527298056)
XLA Ops:
  25.0 5.6 fusion.25
  30.6 8.4 %collective-permute-done.1.refs_2_ = bf16[256,1024]{1,0:T(8,128)(2,1)} collective-permute-done((bf16[256,1024]{1,0:T(8,128)(2,1)S(1)}, bf16[256,1024]{1,0:T(8,128)(2,1)}, u32[]{:S(2)}, u32[]{:S(2)}) %collective-permute-start.1) | collective-permute-done | bytes 524320 | tf_op jit(solution)/shard_map/ppermute | solution.py:618
  41.8 14.4 %attn_fwd.2 = (bf16[256,1024]{1,0:T(8,128)(2,1)}, bf16[256,1024]{1,0:T(8,128)(2,1)}, bf16[256,1024]{1,0:T(8,128)(2,1)}, bf16[256,1024]{1,0:T(8,128)(2,1)}, bf16[...) custom-call(s32[4]{0:T(128)} %add_multiply_fusion.2.starts_ref, ...), custom_call_target="tpu_custom_call" | custom-call | flops 11000000 | bytes 40000 | tf_op jit(solution)/shard_map/attn_fwd/pallas_call | solution.py:182
  59.8 12.5 %collective-permute-done.5 = bf16[256,1024]{1,0:T(8,128)(2,1)S(1)} collective-permute-done((bf16[256,1024]{1,0:T(8,128)(2,1)}, bf16[256,1024]{1,0:T(8,128)(2,1)S(1)}, u32[]{:S(2)}, u32[]{:S(2)}) %collective-permute-start.5) | collective-permute-done | bytes 524320 | tf_op jit(solution)/shard_map/ppermute | solution.py:618
  72.3 9.4 %collective-permute-done.4 = bf16[256,1024]{1,0:T(8,128)(2,1)S(1)} collective-permute-done((bf16[256,1024]{1,0:T(8,128)(2,1)}, bf16[256,1024]{1,0:T(8,128)(2,1)S(1)}, u32[]{:S(2)}, u32[]{:S(2)}) %collective-permute-start.4) | collective-permute-done | bytes 524320 | tf_op jit(solution)/shard_map/ppermute | solution.py:618
  84.5 6.5 all-gather.7.cloned.1.call-done.refs_1_
  103.0 5.4 collective-permute-done.6.refs_1_
  108.4 12.8 %collective-permute-done.7.refs_2_ = bf16[256,1024]{1,0:T(8,128)(2,1)} collective-permute-done((bf16[256,1024]{1,0:T(8,128)(2,1)S(1)}, bf16[256,1024]{1,0:T(8,128)(2,1)}, u32[]{:S(2)}, u32[]{:S(2)}) %collective-permute-start.7) | collective-permute-done | bytes 524320 | tf_op jit(solution)/shard_map/ppermute | solution.py:618
  121.2 14.4 %attn_fwd.3 = (bf16[256,1024]{1,0:T(8,128)(2,1)}, bf16[256,1024]{1,0:T(8,128)(2,1)}, bf16[256,1024]{1,0:T(8,128)(2,1)}, bf16[256,1024]{1,0:T(8,128)(2,1)}, bf16[...) custom-call(s32[4]{0:T(128)} %add_multiply_fusion.2.starts_ref, ...), custom_call_target="tpu_custom_call" | custom-call | flops 11000000 | bytes 40000 | tf_op jit(solution)/shard_map/attn_fwd/pallas_call | solution.py:182
  139.2 26.4 %collective-permute-done.11 = bf16[256,1024]{1,0:T(8,128)(2,1)S(1)} collective-permute-done((bf16[256,1024]{1,0:T(8,128)(2,1)}, bf16[256,1024]{1,0:T(8,128)(2,1)S(1)}, u32[]{:S(2)}, u32[]{:S(2)}) %collective-permute-start.11) | collective-permute-done | bytes 524320 | tf_op jit(solution)/shard_map/ppermute | solution.py:618
  165.6 10.7 %collective-permute-done.10 = bf16[256,1024]{1,0:T(8,128)(2,1)S(1)} collective-permute-done((bf16[256,1024]{1,0:T(8,128)(2,1)}, bf16[256,1024]{1,0:T(8,128)(2,1)S(1)}, u32[]{:S(2)}, u32[]{:S(2)}) %collective-permute-start.10) | collective-permute-done | bytes 524320 | tf_op jit(solution)/shard_map/ppermute | solution.py:618
  190.3 14.6 %dispatch.2 = (bf16[4,8,96,1024]{3,2,1,0:T(8,128)(2,1)}, bf16[4,8,96,1024]{3,2,1,0:T(8,128)(2,1)}, bf16[2048,384]{1,0:T(8,128)(2,1)}, bf16[2048,384]{1,0:T(8,128)(2,1)}) custom-call(s32[1]{0:T(128)} %bitcast.15.offset_ref, bf16[2048,1024]{1,0:T(8,128)(2,1)} %all-gather.9.cloned.1.call-done.refs_0_, bf16[2048,1152]{1,0:T(8,128)(2,1)} %all-gather.7.cloned.1.call-done.refs_1_, ...), custom_call_target="tpu_custom_call" | custom-call | flops 11000000 | bytes 40000 | tf_op jit(solution)/shard_map/dispatch/pallas_call | solution.py:363
  204.8 13.1 %collective-permute-done.14.refs_1_ = bf16[2,384,1024]{2,1,0:T(8,128)(2,1)} collective-permute-done((bf16[2,384,1024]{2,1,0:T(8,128)(2,1)}, bf16[2,384,1024]{2,1,0:T(8,128)(2,1)}, u32[]{:S(2)}, u32[]{:S(2)}) %collective-permute-start.14) | collective-permute-done | bytes 1572896 | tf_op jit(solution)/shard_map/ppermute | solution.py:618
  226.1 8.6 %collective-permute-done.16.refs_3_ = bf16[1,384,1024]{2,1,0:T(8,128)(2,1)} collective-permute-done((bf16[1,384,1024]{2,1,0:T(8,128)(2,1)}, bf16[1,384,1024]{2,1,0:T(8,128)(2,1)}, u32[]{:S(2)}, u32[]{:S(2)}) %collective-permute-start.16) | collective-permute-done | bytes 786464 | tf_op jit(solution)/shard_map/ppermute | solution.py:618
  235.3 27.6 %experts.4 = (bf16[2,768,1024]{2,1,0:T(8,128)(2,1)}, bf16[2,768,1024]{2,1,0:T(8,128)(2,1)}, bf16[2,768,128]{2,1,0:T(8,128)(2,1)}, bf16[2,384,1024]{2,1,0:T(8,128...) custom-call(s32[5]{0:T(128)} %concatenate.33.place_ref, ...), custom_call_target="tpu_custom_call" | custom-call | flops 20000000 | bytes 60000 | tf_op jit(solution)/shard_map/experts/pallas_call | solution.py:533
  263.0 28.1 %experts.5 = (bf16[2,768,1024]{2,1,0:T(8,128)(2,1)}, bf16[2,768,1024]{2,1,0:T(8,128)(2,1)}, bf16[2,768,128]{2,1,0:T(8,128)(2,1)}, bf16[2,384,1024]{2,1,0:T(8,128...) custom-call(s32[5]{0:T(128)} %concatenate.33.place_ref, ...), custom_call_target="tpu_custom_call" | custom-call | flops 20000000 | bytes 60000 | tf_op jit(solution)/shard_map/experts/pallas_call | solution.py:533
  291.1 13.3 %combine.1 = bf16[2048,2176]{1,0:T(8,128)(2,1)} custom-call(bf16[2,8,96,1024]{3,2,1,0:T(8,128)(2,1)} %bitcast.129, bf16[2,8,96,1024]{3,2,1,0:T(8,128)(2,1)} %bitcast.131, bf16[2,8,96,1024]{3,2,1,0:T(8,128)(2,1)} %bitcast.130, bf16[2,8,96,1024]{3,2,1,0:T(8,128)(2,1)} %bitcast.132, bf16[2,8,96,128]{3,2,1,0:T(8,128)(2,1)} %bitcast.142, ...), custom_call_target="tpu_custom_call" | custom-call | flops 5000000 | bytes 17000 | tf_op jit(solution)/shard_map/combine/pallas_call | solution.py:605
  304.5 15.0 %dispatch.3 = (bf16[4,8,96,1024]{3,2,1,0:T(8,128)(2,1)}, bf16[4,8,96,1024]{3,2,1,0:T(8,128)(2,1)}, bf16[2048,384]{1,0:T(8,128)(2,1)}, bf16[2048,384]{1,0:T(8,128)(2,1)}) custom-call(s32[1]{0:T(128)} %bitcast.15.offset_ref, bf16[2048,2176]{1,0:T(8,128)(2,1)} %all-gather.11.cloned.1.call-done.refs_0_, bf16[1024,128]{1,0:T(8,128)(2,1)} %pad.8.refs_2_.refs_1_), custom_call_target="tpu_custom_call" | custom-call | flops 11000000 | bytes 40000 | tf_op jit(solution)/shard_map/dispatch/pallas_call | solution.py:363
  319.4 30.0 %experts.6 = (bf16[2,768,1024]{2,1,0:T(8,128)(2,1)}, bf16[2,768,1024]{2,1,0:T(8,128)(2,1)}, bf16[2,768,128]{2,1,0:T(8,128)(2,1)}, bf16[2,384,1024]{2,1,0:T(8,128...) custom-call(s32[5]{0:T(128)} %concatenate.33.place_ref, ...), custom_call_target="tpu_custom_call" | custom-call | flops 20000000 | bytes 60000 | tf_op jit(solution)/shard_map/experts/pallas_call | solution.py:533
  349.4 30.2 %experts.7 = (bf16[2,768,1024]{2,1,0:T(8,128)(2,1)}, bf16[2,768,1024]{2,1,0:T(8,128)(2,1)}, bf16[2,768,128]{2,1,0:T(8,128)(2,1)}, bf16[2,384,1024]{2,1,0:T(8,128...) custom-call(s32[5]{0:T(128)} %concatenate.33.place_ref, ...), custom_call_target="tpu_custom_call" | custom-call | flops 20000000 | bytes 60000 | tf_op jit(solution)/shard_map/experts/pallas_call | solution.py:533
  379.6 9.1 %combine_grad.1 = bf16[2048,1152]{1,0:T(8,128)(2,1)} custom-call(bf16[2,8,96,1024]{3,2,1,0:T(8,128)(2,1)} %bitcast.135, bf16[2,8,96,1024]{3,2,1,0:T(8,128)(2,1)} %bitcast.136, bf16[2,8,96,128]{3,2,1,0:T(8,128)(2,1)} %bitcast.138, bf16[2,8,96,128]{3,2,1,0:T(8,128)(2,1)} %bitcast.139, bf16[2048,384]{1,0:T(8,128)(2,1)} %get-tuple-element.195.refs_4_), custom_call_target="tpu_custom_call" | custom-call | flops 5000000 | bytes 17000 | tf_op jit(solution)/shard_map/combine_grad/pallas_call | solution.py:605
  391.7 29.9 %collective-permute-done.20 = bf16[2,384,1024]{2,1,0:T(8,128)(2,1)} collective-permute-done((bf16[2,384,1024]{2,1,0:T(8,128)(2,1)}, bf16[2,384,1024]{2,1,0:T(8,128)(2,1)}, u32[]{:S(2)}, u32[]{:S(2)}) %collective-permute-start.20) | collective-permute-done | bytes 1572896 | tf_op jit(solution)/shard_map/ppermute | solution.py:618
  422.5 8.7 %combine_mix.1 = bf16[2048,1024]{1,0:T(8,128)(2,1)} custom-call(bf16[2,8,96,1024]{3,2,1,0:T(8,128)(2,1)} %bitcast.133, bf16[2,8,96,1024]{3,2,1,0:T(8,128)(2,1)} %bitcast.134, bf16[2048,384]{1,0:T(8,128)(2,1)} %get-tuple-element.206.refs_2_), custom_call_target="tpu_custom_call" | custom-call | flops 5000000 | bytes 17000 | tf_op jit(solution)/shard_map/combine_mix/pallas_call | solution.py:605
  457.5 5.7 collective-permute-done.25
  465.3 10.3 %collective-permute-done.22.refs_16_ = bf16[256,1024]{1,0:T(8,128)(2,1)} collective-permute-done((bf16[256,1024]{1,0:T(8,128)(2,1)}, bf16[256,1024]{1,0:T(8,128)(2,1)}, u32[]{:S(2)}, u32[]{:S(2)}) %collective-permute-start.22) | collective-permute-done | bytes 524320 | tf_op jit(solution)/shard_map/ppermute | solution.py:618
  475.6 8.4 %collective-permute-done.24.refs_18_ = bf16[256,1024]{1,0:T(8,128)(2,1)} collective-permute-done((bf16[256,1024]{1,0:T(8,128)(2,1)}, bf16[256,1024]{1,0:T(8,128)(2,1)}, u32[]{:S(2)}, u32[]{:S(2)}) %collective-permute-start.24) | collective-permute-done | bytes 524320 | tf_op jit(solution)/shard_map/ppermute | solution.py:618
  486.7 23.5 %attn_bwd.2 = (bf16[256,1024]{1,0:T(8,128)(2,1)}, bf16[256,1024]{1,0:T(8,128)(2,1)}, bf16[256,1024]{1,0:T(8,128)(2,1)}, bf16[256,1024]{1,0:T(8,128)(2,1)}, bf16[1024,768]{1,0:T(8,128)(2,1)}, /*index=5*/f32[1,1024]{1,0:T(1,128)}) custom-call(s32[4]{0:T(128)} %add_multiply_fusion.2.starts_ref, bf16[256,1024]{1,0:T(8,128)(2,1)} %copy-done.9, ...), custom_call_target="tpu_custom_call" | custom-call | flops 18000000 | bytes 65000 | tf_op jit(solution)/shard_map/attn_bwd/pallas_call | solution.py:284
  520.7 12.1 %collective-permute-done.29.refs_16_ = bf16[256,1024]{1,0:T(8,128)(2,1)} collective-permute-done((bf16[256,1024]{1,0:T(8,128)(2,1)}, bf16[256,1024]{1,0:T(8,128)(2,1)}, u32[]{:S(2)}, u32[]{:S(2)}) %collective-permute-start.29) | collective-permute-done | bytes 524320 | tf_op jit(solution)/shard_map/ppermute | solution.py:618
  534.6 14.2 %collective-permute-done.30.refs_17_ = bf16[256,1024]{1,0:T(8,128)(2,1)} collective-permute-done((bf16[256,1024]{1,0:T(8,128)(2,1)}, bf16[256,1024]{1,0:T(8,128)(2,1)}, u32[]{:S(2)}, u32[]{:S(2)}) %collective-permute-start.30) | collective-permute-done | bytes 524320 | tf_op jit(solution)/shard_map/ppermute | solution.py:618
  548.8 23.8 %attn_bwd.3 = (bf16[256,1024]{1,0:T(8,128)(2,1)}, bf16[256,1024]{1,0:T(8,128)(2,1)}, bf16[256,1024]{1,0:T(8,128)(2,1)}, bf16[256,1024]{1,0:T(8,128)(2,1)}, bf16[1024,768]{1,0:T(8,128)(2,1)}, /*index=5*/f32[1,1024]{1,0:T(1,128)}) custom-call(s32[4]{0:T(128)} %add_multiply_fusion.2.starts_ref, bf16[256,1024]{1,0:T(8,128)(2,1)} %copy-done.8, ...), custom_call_target="tpu_custom_call" | custom-call | flops 18000000 | bytes 65000 | tf_op jit(solution)/shard_map/attn_bwd/pallas_call | solution.py:284
  596.8 9.1 %collective-permute-done.40 = bf16[256,128]{1,0:T(8,128)(2,1)S(1)} collective-permute-done((bf16[256,128]{1,0:T(8,128)(2,1)S(1)}, bf16[256,128]{1,0:T(8,128)(2,1)S(1)}, u32[]{:S(2)}, u32[]{:S(2)}) %collective-permute-start.40) | collective-permute-done | bytes 65568 | tf_op jit(solution)/shard_map/ppermute | solution.py:618
  639.3 7.0 %reduce-scatter.11.cloned.1.call-done = bf16[136,768]{1,0:T(8,128)(2,1)} async-done(((bf16[1088,768]{1,0:T(8,128)(2,1)}), bf16[136,768]{1,0:T(8,128)(2,1)}) %reduce-scatter.11.cloned.1.call-update) | async-done | bytes 208912 | tf_op jit(solution)/shard_map/reduce_scatter | solution.py:692
  (292 shorter events, 174.8 us)
Async XLA Ops:
  7.2 31.8 %all-gather.5.cloned.1.call-start = ((), (), s32[]{:S(2)}) async-start(), calls=%async_computation.4 | async-start | bytes 1769472 | tf_op jit(solution)/shard_map/all_gather | solution.py:688
  9.9 81.1 %all-gather.7.cloned.1.call-start = ((), (), s32[]{:S(2)}) async-start(), calls=%async_computation.5 | async-start | bytes 5308416 | tf_op jit(solution)/shard_map/all_gather | solution.py:688
  14.3 24.7 %collective-permute-start.1 = (bf16[256,1024]{1,0:T(8,128)(2,1)S(1)}, bf16[256,1024]{1,0:T(8,128)(2,1)}, u32[]{:S(2)}, u32[]{:S(2)}) collective-permute-start(bf16[256,1024]{1,0:T(8,128)(2,1)S(1)} %get-tuple-element.339.refs_0_), channel_id=1, source_target_pairs={{0,16},{8,24},{16,0},{24,8},{1,17},{9,25},{17,1},{25,9},{2,18},{10... | collective-permute-start | bytes 1572872 | tf_op jit(solution)/shard_map/ppermute | solution.py:618
  39.1 151.2 %all-gather.9.cloned.1.call-start = ((), (), s32[]{:S(2)}) async-start(), calls=%async_computation.6 | async-start | bytes 4718592 | tf_op jit(solution)/shard_map/all_gather | solution.py:688
  57.8 23.9 %collective-permute-start.4 = (bf16[256,1024]{1,0:T(8,128)(2,1)}, bf16[256,1024]{1,0:T(8,128)(2,1)S(1)}, u32[]{:S(2)}, u32[]{:S(2)}) collective-permute-start(bf16[256,1024]{1,0:T(8,128)(2,1)} %get-tuple-element.145), channel_id=1, source_target_pairs={{0,16},{8,24},{16,0},{24,8},{1,17},{9,25},{17,1},{25,9},{2,18},{10... | collective-permute-start | bytes 1572872 | tf_op jit(solution)/shard_map/ppermute | solution.py:618
  91.0 213.4 %all-gather.11.cloned.1.call-start = ((), (), s32[]{:S(2)}) async-start(), calls=%async_computation.8 | async-start | bytes 10027008 | tf_op jit(solution)/shard_map/all_gather | solution.py:688
  95.1 26.1 %collective-permute-start.7 = (bf16[256,1024]{1,0:T(8,128)(2,1)S(1)}, bf16[256,1024]{1,0:T(8,128)(2,1)}, u32[]{:S(2)}, u32[]{:S(2)}) collective-permute-start(bf16[256,1024]{1,0:T(8,128)(2,1)S(1)} %get-tuple-element.148.refs_0_), channel_id=1, source_target_pairs={{0,16},{8,24},{16,0},{24,8},{1,17},{9,25},{17,1},{25,9},{2,18},{10... | collective-permute-start | bytes 1572872 | tf_op jit(solution)/shard_map/ppermute | solution.py:618
  96.5 24.7 %collective-permute-start.8 = (bf16[256,1024]{1,0:T(8,128)(2,1)S(1)}, bf16[256,1024]{1,0:T(8,128)(2,1)}, u32[]{:S(2)}, u32[]{:S(2)}) collective-permute-start(bf16[256,1024]{1,0:T(8,128)(2,1)S(1)} %get-tuple-element.148.refs_0_), channel_id=1, source_target_pairs={{0,24},{8,16},{16,8},{24,0},{1,25},{9,17},{17,9},{25,1},{2,26},{10... | collective-permute-start | bytes 1572872 | tf_op jit(solution)/shard_map/ppermute | solution.py:618
  99.1 79.0 %collective-permute-start.12 = (bf16[2,384,1024]{2,1,0:T(8,128)(2,1)}, bf16[2,384,1024]{2,1,0:T(8,128)(2,1)}, u32[]{:S(2)}, u32[]{:S(2)}) collective-permute-start(bf16[2,384,1024]{2,1,0:T(8,128)(2,1)} %get-tuple-element.157.refs_0_), channel_id=1, source_target_pairs={{0,8},{8,0},{16,24},{24,16},{1,9},{9,1},{17,25},{25,17},{2,10},{10... | collective-permute-start | bytes 4718600 | tf_op jit(solution)/shard_map/ppermute | solution.py:618
  100.5 77.5 %collective-permute-start.13 = (bf16[2,384,1024]{2,1,0:T(8,128)(2,1)}, bf16[2,384,1024]{2,1,0:T(8,128)(2,1)}, u32[]{:S(2)}, u32[]{:S(2)}) collective-permute-start(bf16[2,384,1024]{2,1,0:T(8,128)(2,1)} %get-tuple-element.157.refs_0_), channel_id=1, source_target_pairs={{0,16},{8,24},{16,0},{24,8},{1,17},{9,25},{17,1},{25,9},{2,18},{10... | collective-permute-start | bytes 4718600 | tf_op jit(solution)/shard_map/ppermute | solution.py:618
  135.6 29.9 %collective-permute-start.11 = (bf16[256,1024]{1,0:T(8,128)(2,1)}, bf16[256,1024]{1,0:T(8,128)(2,1)S(1)}, u32[]{:S(2)}, u32[]{:S(2)}) collective-permute-start(bf16[256,1024]{1,0:T(8,128)(2,1)} %get-tuple-element.152), channel_id=1, source_target_pairs={{0,24},{8,16},{16,8},{24,0},{1,25},{9,17},{17,9},{25,1},{2,26},{10... | collective-permute-start | bytes 1572872 | tf_op jit(solution)/shard_map/ppermute | solution.py:618
  137.2 39.1 %collective-permute-start.10 = (bf16[256,1024]{1,0:T(8,128)(2,1)}, bf16[256,1024]{1,0:T(8,128)(2,1)S(1)}, u32[]{:S(2)}, u32[]{:S(2)}) collective-permute-start(bf16[256,1024]{1,0:T(8,128)(2,1)} %get-tuple-element.151), channel_id=1, source_target_pairs={{0,16},{8,24},{16,0},{24,8},{1,17},{9,25},{17,1},{25,9},{2,18},{10... | collective-permute-start | bytes 1572872 | tf_op jit(solution)/shard_map/ppermute | solution.py:618
  138.1 38.1 %collective-permute-start.9 = (bf16[256,1024]{1,0:T(8,128)(2,1)}, bf16[256,1024]{1,0:T(8,128)(2,1)S(1)}, u32[]{:S(2)}, u32[]{:S(2)}) collective-permute-start(bf16[256,1024]{1,0:T(8,128)(2,1)} %get-tuple-element.150), channel_id=1, source_target_pairs={{0,8},{8,0},{16,24},{24,16},{1,9},{9,1},{17,25},{25,17},{2,10},{10... | collective-permute-start | bytes 1572872 | tf_op jit(solution)/shard_map/ppermute | solution.py:618
  180.0 265.3 %reduce-scatter.5.cloned.1.call-start = ((), (), s32[]{:S(2)}) async-start(), calls=%async_computation.7 | async-start | bytes 10027008 | tf_op jit(solution)/shard_map/reduce_scatter | solution.py:692
  180.3 37.6 %collective-permute-start.14 = (bf16[2,384,1024]{2,1,0:T(8,128)(2,1)}, bf16[2,384,1024]{2,1,0:T(8,128)(2,1)}, u32[]{:S(2)}, u32[]{:S(2)}) collective-permute-start(bf16[2,384,1024]{2,1,0:T(8,128)(2,1)} %get-tuple-element.164.refs_0_), channel_id=1, source_target_pairs={{0,8},{8,0},{16,24},{24,16},{1,9},{9,1},{17,25},{25,17},{2,10},{10... | collective-permute-start | bytes 4718600 | tf_op jit(solution)/shard_map/ppermute | solution.py:618
  180.9 37.6 %collective-permute-start.15 = (bf16[2,384,1024]{2,1,0:T(8,128)(2,1)}, bf16[2,384,1024]{2,1,0:T(8,128)(2,1)}, u32[]{:S(2)}, u32[]{:S(2)}) collective-permute-start(bf16[2,384,1024]{2,1,0:T(8,128)(2,1)} %get-tuple-element.164.refs_0_), channel_id=1, source_target_pairs={{0,16},{8,24},{16,0},{24,8},{1,17},{9,25},{17,1},{25,9},{2,18},{10... | collective-permute-start | bytes 4718600 | tf_op jit(solution)/shard_map/ppermute | solution.py:618
  186.6 48.2 %collective-permute-start.16 = (bf16[1,384,1024]{2,1,0:T(8,128)(2,1)}, bf16[1,384,1024]{2,1,0:T(8,128)(2,1)}, u32[]{:S(2)}, u32[]{:S(2)}) collective-permute-start(bf16[1,384,1024]{2,1,0:T(8,128)(2,1)} %slice.211), channel_id=1, source_target_pairs={{0,8},{8,0},{16,24},{24,16},{1,9},{9,1},{17,25},{25,17},{2,10},{10... | collective-permute-start | bytes 2359304 | tf_op jit(solution)/shard_map/ppermute | solution.py:618
  188.0 47.3 %collective-permute-start.17 = (bf16[1,384,1024]{2,1,0:T(8,128)(2,1)}, bf16[1,384,1024]{2,1,0:T(8,128)(2,1)}, u32[]{:S(2)}, u32[]{:S(2)}) collective-permute-start(bf16[1,384,1024]{2,1,0:T(8,128)(2,1)} %slice.212), channel_id=1, source_target_pairs={{0,16},{8,24},{16,0},{24,8},{1,17},{9,25},{17,1},{25,9},{2,18},{10... | collective-permute-start | bytes 2359304 | tf_op jit(solution)/shard_map/ppermute | solution.py:618
  220.5 42.4 %collective-permute-start.18 = (bf16[1,384,1024]{2,1,0:T(8,128)(2,1)}, bf16[1,384,1024]{2,1,0:T(8,128)(2,1)}, u32[]{:S(2)}, u32[]{:S(2)}) collective-permute-start(bf16[1,384,1024]{2,1,0:T(8,128)(2,1)} %slice.213), channel_id=1, source_target_pairs={{0,8},{8,0},{16,24},{24,16},{1,9},{9,1},{17,25},{25,17},{2,10},{10... | collective-permute-start | bytes 2359304 | tf_op jit(solution)/shard_map/ppermute | solution.py:618
  224.1 38.9 %collective-permute-start.19 = (bf16[1,384,1024]{2,1,0:T(8,128)(2,1)}, bf16[1,384,1024]{2,1,0:T(8,128)(2,1)}, u32[]{:S(2)}, u32[]{:S(2)}) collective-permute-start(bf16[1,384,1024]{2,1,0:T(8,128)(2,1)} %slice.214), channel_id=1, source_target_pairs={{0,16},{8,24},{16,0},{24,8},{1,17},{9,25},{17,1},{25,9},{2,18},{10... | collective-permute-start | bytes 2359304 | tf_op jit(solution)/shard_map/ppermute | solution.py:618
  304.4 205.9 %reduce-scatter.9.cloned.1.call-start = ((), (), s32[]{:S(2)}) async-start(), calls=%async_computation.10 | async-start | bytes 5308416 | tf_op jit(solution)/shard_map/reduce_scatter | solution.py:692
  388.8 183.9 %reduce-scatter.7.cloned.1.call-start = ((), (), s32[]{:S(2)}) async-start(), calls=%async_computation.9 | async-start | bytes 4718592 | tf_op jit(solution)/shard_map/reduce_scatter | solution.py:692
  388.8 32.8 %collective-permute-start.20 = (bf16[2,384,1024]{2,1,0:T(8,128)(2,1)}, bf16[2,384,1024]{2,1,0:T(8,128)(2,1)}, u32[]{:S(2)}, u32[]{:S(2)}) collective-permute-start(bf16[2,384,1024]{2,1,0:T(8,128)(2,1)} %get-tuple-element.199), channel_id=1, source_target_pairs={{0,8},{8,0},{16,24},{24,16},{1,9},{9,1},{17,25},{25,17},{2,10},{10... | collective-permute-start | bytes 4718600 | tf_op jit(solution)/shard_map/ppermute | solution.py:618
  390.3 32.2 %collective-permute-start.21 = (bf16[2,384,1024]{2,1,0:T(8,128)(2,1)}, bf16[2,384,1024]{2,1,0:T(8,128)(2,1)}, u32[]{:S(2)}, u32[]{:S(2)}) collective-permute-start(bf16[2,384,1024]{2,1,0:T(8,128)(2,1)} %get-tuple-element.200), channel_id=1, source_target_pairs={{0,16},{8,24},{16,0},{24,8},{1,17},{9,25},{17,1},{25,9},{2,18},{10... | collective-permute-start | bytes 4718600 | tf_op jit(solution)/shard_map/ppermute | solution.py:618
  431.2 215.0 %reduce-scatter.11.cloned.1.call-start = ((), (), s32[]{:S(2)}) async-start(), calls=%async_computation.11 | async-start | bytes 1880064 | tf_op jit(solution)/shard_map/reduce_scatter | solution.py:692
  451.0 24.5 %collective-permute-start.22 = (bf16[256,1024]{1,0:T(8,128)(2,1)}, bf16[256,1024]{1,0:T(8,128)(2,1)}, u32[]{:S(2)}, u32[]{:S(2)}) collective-permute-start(bf16[256,1024]{1,0:T(8,128)(2,1)} %get-tuple-element.237.refs_15_), channel_id=1, source_target_pairs={{0,8},{8,0},{16,24},{24,16},{1,9},{9,1},{17,25},{25,17},{2,10},{10... | collective-permute-start | bytes 1572872 | tf_op jit(solution)/shard_map/ppermute | solution.py:618
  452.9 31.0 %collective-permute-start.24 = (bf16[256,1024]{1,0:T(8,128)(2,1)}, bf16[256,1024]{1,0:T(8,128)(2,1)}, u32[]{:S(2)}, u32[]{:S(2)}) collective-permute-start(bf16[256,1024]{1,0:T(8,128)(2,1)} %get-tuple-element.237.refs_15_), channel_id=1, source_target_pairs={{0,24},{8,16},{16,8},{24,0},{1,25},{9,17},{17,9},{25,1},{2,26},{10... | collective-permute-start | bytes 1572872 | tf_op jit(solution)/shard_map/ppermute | solution.py:618
  484.0 64.8 %collective-permute-start.27 = (bf16[2,384,1024]{2,1,0:T(8,128)(2,1)}, bf16[2,384,1024]{2,1,0:T(8,128)(2,1)}, u32[]{:S(2)}, u32[]{:S(2)}) collective-permute-start(bf16[2,384,1024]{2,1,0:T(8,128)(2,1)} %get-tuple-element.227), channel_id=1, source_target_pairs={{0,8},{8,0},{16,24},{24,16},{1,9},{9,1},{17,25},{25,17},{2,10},{10... | collective-permute-start | bytes 4718600 | tf_op jit(solution)/shard_map/ppermute | solution.py:618
  485.0 63.8 %collective-permute-start.28 = (bf16[2,384,1024]{2,1,0:T(8,128)(2,1)}, bf16[2,384,1024]{2,1,0:T(8,128)(2,1)}, u32[]{:S(2)}, u32[]{:S(2)}) collective-permute-start(bf16[2,384,1024]{2,1,0:T(8,128)(2,1)} %get-tuple-element.228), channel_id=1, source_target_pairs={{0,16},{8,24},{16,0},{24,8},{1,17},{9,25},{17,1},{25,9},{2,18},{10... | collective-permute-start | bytes 4718600 | tf_op jit(solution)/shard_map/ppermute | solution.py:618
  516.2 32.6 %collective-permute-start.30 = (bf16[256,1024]{1,0:T(8,128)(2,1)}, bf16[256,1024]{1,0:T(8,128)(2,1)}, u32[]{:S(2)}, u32[]{:S(2)}) collective-permute-start(bf16[256,1024]{1,0:T(8,128)(2,1)} %get-tuple-element.246.refs_15_), channel_id=1, source_target_pairs={{0,16},{8,24},{16,0},{24,8},{1,17},{9,25},{17,1},{25,9},{2,18},{10... | collective-permute-start | bytes 1572872 | tf_op jit(solution)/shard_map/ppermute | solution.py:618
  516.2 32.6 %collective-permute-start.31 = (bf16[256,1024]{1,0:T(8,128)(2,1)}, bf16[256,1024]{1,0:T(8,128)(2,1)}, u32[]{:S(2)}, u32[]{:S(2)}) collective-permute-start(bf16[256,1024]{1,0:T(8,128)(2,1)} %get-tuple-element.246.refs_15_), channel_id=1, source_target_pairs={{0,24},{8,16},{16,8},{24,0},{1,25},{9,17},{17,9},{25,1},{2,26},{10... | collective-permute-start | bytes 1572872 | tf_op jit(solution)/shard_map/ppermute | solution.py:618
  532.8 60.4 %collective-permute-start.34 = (bf16[256,1024]{1,0:T(8,128)(2,1)}, bf16[256,1024]{1,0:T(8,128)(2,1)}, u32[]{:S(2)}, u32[]{:S(2)}) collective-permute-start(bf16[256,1024]{1,0:T(8,128)(2,1)} %get-tuple-element.244), channel_id=1, source_target_pairs={{0,24},{8,16},{16,8},{24,0},{1,25},{9,17},{17,9},{25,1},{2,26},{10... | collective-permute-start | bytes 1572872 | tf_op jit(solution)/shard_map/ppermute | solution.py:618
  (66 other events, 778.9 us)
Sparse Core Ops, SparseCore 0:
  10.2 27.7 all-gather.4
  40.2 50.7 all-gather.6
  92.6 45.6 all-gather.8
  180.1 84.2 all-gather.10
  304.5 93.1 reduce-scatter.4
  399.9 53.3 reduce-scatter.8
  456.1 48.3 reduce-scatter.6
  613.3 32.8 reduce-scatter.10

commit v4 on v3

--- a/solution.py
+++ b/solution.py
@@ -774,9 +774,11 @@
     full = []
     for m in range(micro):
         if m:
-            fixed[m] = (after(starts, normed_twos), *fixed[m][1:])
+            fixed[m] = (after(starts, normed_twos), token_full[m], *fixed[m][2:])
         parts, saved = attention_forward(*fixed[m])
         kept.append(saved)
+        if m == 0:
+            parts, token_full = lax.optimization_barrier((parts, token_full))
         came.append(send_rows(parts))
         if m == 0:
             near = [gather_weights_near(after(packed_weights[0], came[0]))]
@@ -802,7 +804,7 @@
             full.append([ag_ep(jnp.concatenate([normed_two, cotangent[m], masks[m]], axis=-1))])
 
     pieces = [gather_weights_far(near[0])]
-    near.append(gather_weights_near(after(packed_weights[1], near[0])))
+    near.append(gather_weights_near(after(packed_weights[1], pieces[0])))
     old = [(), ()]
     mixes = []
     grads = []
@@ -810,9 +812,6 @@
     for m in range(micro):
         sources = after(full[m], ready) if m else full[m]
         xd, gd, pt, pgt = dispatch(offset, sources, router, local)
-        if m == 0:
-            xd, near[1] = lax.optimization_barrier((xd, near[1]))
-            pieces.append(gather_weights_far(near[1]))
         merged = (local, ep_size * CAP, MODEL_WIDTH)
         xd = xd.reshape(merged)
         gd = gd.reshape(merged)
@@ -822,6 +821,9 @@
                 place, xd, gd, pieces[h], old[h], h * here, here, slices
             )
             done.append(results)
+            if m == 0 and h == 0:
+                near[1] = after(near[1], results)
+                pieces.append(gather_weights_far(near[1]))
         outs, dxs, hs = zip(*done)
         if m < micro - 1:
             both = combine(
@@ -833,23 +835,25 @@
             mixes.append(both[:, :MODEL_WIDTH])
             grads.append(both[:, MODEL_WIDTH:])
         else:
+            near_first = sum_weights_near(old[0])
+            dxs, near_first = lax.optimization_barrier((dxs, near_first))
+            near_second = sum_weights_near(old[1])
             grad = combine(
                 combine_grad_body, [*dxs, *hs], 2, [pt], MODEL_WIDTH + LANES, "combine_grad"
             )
             grads.append(rs_ep(grad))
-            near_first = sum_weights_near(old[0])
-            outs, pgt, near_first = lax.optimization_barrier((*after((outs, pgt), grad), near_first))
-            mix = combine(combine_mix_body, outs, 2, [pgt], MODEL_WIDTH, "combine_mix")
-            mixes.append(rs_ep(mix))
-    far_first = sum_weights_far(near_first)
     input_grads = []
     acc_router = 0.0
     acc_gain_one = 0.0
     acc_gain_two = 0.0
     acc_weights = 0.0
     parts = ()
+    backs = []
+    grad_hiddens = []
     for m in range(micro):
-        grad = after(grads[m], mix, parts)
+        grad = grads[m]
+        if m:
+            grad, far_first = after((grad, far_first), parts)
         grad = grad.astype(f32)
         h_rows = grad[:, MODEL_WIDTH:]
         grad_logits = (
@@ -866,35 +870,29 @@
             - hiddens[m] * scale * scale * scale * inner
         )
         acc_gain_two = acc_gain_two + jnp.sum(grad_normed * hiddens[m] * scale, axis=0)
-        grad_branch = gather_rows((residual_scale * grad_hidden).astype(bf16))
+        grad_branch = (residual_scale * grad_hidden).astype(bf16)
         if m == 0:
-            near_second = sum_weights_near(after(old[1], grad_branch))
-            grad_branch, far_first = lax.optimization_barrier((grad_branch, far_first))
+            outs, pgt, grad_branch, near_second = lax.optimization_barrier(
+                (outs, pgt, grad_branch, near_second)
+            )
+            mix = combine(combine_mix_body, outs, 2, [pgt], MODEL_WIDTH, "combine_mix")
+            mixes.append(rs_ep(mix))
+        grad_branch = gather_rows(grad_branch)
+        if m == 0:
+            grad_branch = after(grad_branch, mix)
+            far_first = sum_weights_far(after(near_first, grad_branch))
         if m == micro - 1:
-            near_second, grad_branch = lax.optimization_barrier((near_second, grad_branch))
-            far_second = sum_weights_far(near_second)
+            far_second = sum_weights_far(after(near_second, grad_branch))
         parts, (gweights, ggain) = attention_backward(*fixed[m], kept[m], grad_branch)
-        back = send_rows(parts)
+        backs.append(parts)
+        grad_hiddens.append(grad_hidden)
         if m == micro - 1:
-            gweights, far_second = lax.optimization_barrier((gweights, far_second))
+            parts, gweights, ggain, far_second, mixes = lax.optimization_barrier(
+                (parts, gweights, ggain, far_second, mixes)
+            )
+            backs[-1] = parts
         acc_weights = acc_weights + gweights.astype(f32)
         acc_gain_one = acc_gain_one + ggain[0]
-        grad_normed = add_rows(back)
-        inputs = tokens[m].astype(f32)
-        scale = lax.rsqrt(jnp.mean(inputs * inputs, axis=-1, keepdims=True) + epsilon)
-        weighted = grad_normed * gain_one
-        inner = jnp.mean(weighted * inputs, axis=-1, keepdims=True)
-        input_grads.append(
-            grad_hidden + scale * weighted - inputs * scale * scale * scale * inner
-        )
-    hiddens, mixes, far_first = after((hiddens, mixes, far_first), parts)
-    outputs = [
-        (hiddens[m] + residual_scale * mixes[m].astype(f32)).astype(bf16) for m in range(micro)
-    ]
-    grad_gate_up, grad_down = unpack_weights(
-        jnp.concatenate([add_far(far_first), add_far(far_second)]), w_gate_up.shape[1]
-    )
-
     small = jnp.concatenate(
         [
             acc_router[:, :EXPERTS],
@@ -913,6 +911,24 @@
         ).astype(bf16)
     else:
         small = lax.psum_scatter(small, "tp", scatter_dimension=0, tiled=True)
+    backs = [send_rows(after(parts, small)) for parts in backs]
+    for m in range(micro):
+        grad_normed = add_rows(backs[m])
+        inputs = tokens[m].astype(f32)
+        scale = lax.rsqrt(jnp.mean(inputs * inputs, axis=-1, keepdims=True) + epsilon)
+        weighted = grad_normed * gain_one
+        inner = jnp.mean(weighted * inputs, axis=-1, keepdims=True)
+        input_grads.append(
+            grad_hiddens[m] + scale * weighted - inputs * scale * scale * scale * inner
+        )
+    hiddens, mixes, far_first = after((hiddens, mixes, far_first), parts)
+    outputs = [
+        (hiddens[m] + residual_scale * mixes[m].astype(f32)).astype(bf16) for m in range(micro)
+    ]
+    grad_gate_up, grad_down = unpack_weights(
+        jnp.concatenate([add_far(far_first), add_far(far_second)]), w_gate_up.shape[1]
+    )
+
     columns = acc_weights.shape[1]
     own_rows = MODEL_WIDTH // ep_size
     small_rows = rows // ep_size

time: 664 us -> 625 us (0.941)
  waiting for transfers between devices: 225 us -> 186 us
    ppermute x43, waiting for transfers between devices: 211 us -> 185 us  [flip(): return lax.ppermute(value, 'tp', [(t, t ^ bits) for t in range(4)])]
  transfers between devices with their start and end apart: 51 -> 51, of which waited for: 26 -> 21; matrix products, arithmetic and copies ran while one was open for 15% -> 15% of each run, Pallas kernels for 38% -> 41%
where the time goes in v4:
time: 625 us; the launch traced here: 619 us
  Pallas kernels  253 us (40%)
  waiting for transfers between devices  186 us (30%)
  other arithmetic  71.2 us (11%)
  starting transfers between devices  51.6 us (8%)
  local copies, waits for them, and re-layouts  31.9 us (5%)
  between operations  15.4 us (2%)
  matrix products  9.76 us (2%)
    ppermute x43, waiting for transfers between devices, flip(): return lax.ppermute(value, 'tp', [(t, t ^ bits) for t in range(4)])  185 us
    pallas_call x4, Pallas kernels, run_experts(): pl.pallas_call(functools.partial(experts_body, base=base, slices=slices,...  116 us
    ppermute x43, starting transfers between devices, flip(): return lax.ppermute(value, 'tp', [(t, t ^ bits) for t in range(4)])  50.1 us
    pallas_call x2, Pallas kernels, attention_backward(): pl.pallas_call(functools.partial(attention_backward_body, count=count), o...  47.3 us
    pallas_call x3, Pallas kernels, combine(): pl.pallas_call(functools.partial(body, count=count), grid=(blocks,), in_s...  31 us
    pallas_call x2, Pallas kernels, dispatch(): pl.pallas_call(functools.partial(dispatch_body, local=local, count=len(so...  29.5 us
    pallas_call x2, Pallas kernels, attention_forward(): pl.pallas_call(functools.partial(attention_forward_body, count=count), ou...  29.2 us
  transfers between devices with their start and end apart: 51, of which 21 were waited for; matrix products, arithmetic and copies ran while one was open for 15% of the time, Pallas kernels for 41%

profile of v4, /device:TPU:0, one launch (start us, length us, event | category | flops | bytes accessed | tf_op | source)
XLA Modules:
  0.0 619.4 jit_solution(10005822924541899827)
XLA Ops:
  11.3 3.0 collective-permute-start
  16.0 2.9 fusion.3
  24.9 5.6 fusion.25
  30.6 8.5 %collective-permute-done.1.refs_2_ = bf16[256,1024]{1,0:T(8,128)(2,1)} collective-permute-done((bf16[256,1024]{1,0:T(8,128)(2,1)S(1)}, bf16[256,1024]{1,0:T(8,128)(2,1)}, u32[]{:S(2)}, u32[]{:S(2)}) %collective-permute-start.1) | collective-permute-done | bytes 524320 | tf_op jit(solution)/shard_map/ppermute | solution.py:618
  45.2 14.8 %attn_fwd.2 = (bf16[256,1024]{1,0:T(8,128)(2,1)}, bf16[256,1024]{1,0:T(8,128)(2,1)}, bf16[256,1024]{1,0:T(8,128)(2,1)}, bf16[256,1024]{1,0:T(8,128)(2,1)}, bf16[...) custom-call(s32[4]{0:T(128)} %add_multiply_fusion.2.starts_ref, ...), custom_call_target="tpu_custom_call" | custom-call | flops 11000000 | bytes 40000 | tf_op jit(solution)/shard_map/attn_fwd/pallas_call | solution.py:182
  60.0 5.0 collective-permute-done.4.refs_2_
  68.6 11.5 %collective-permute-done.6 = bf16[256,1024]{1,0:T(8,128)(2,1)S(1)} collective-permute-done((bf16[256,1024]{1,0:T(8,128)(2,1)}, bf16[256,1024]{1,0:T(8,128)(2,1)S(1)}, u32[]{:S(2)}, u32[]{:S(2)}) %collective-permute-start.6) | collective-permute-done | bytes 524320 | tf_op jit(solution)/shard_map/ppermute | solution.py:618
  80.1 10.5 %collective-permute-done.7 = bf16[256,1024]{1,0:T(8,128)(2,1)S(1)} collective-permute-done((bf16[256,1024]{1,0:T(8,128)(2,1)}, bf16[256,1024]{1,0:T(8,128)(2,1)S(1)}, u32[]{:S(2)}, u32[]{:S(2)}) %collective-permute-start.7) | collective-permute-done | bytes 524320 | tf_op jit(solution)/shard_map/ppermute | solution.py:618
  100.9 14.4 %attn_fwd.3 = (bf16[256,1024]{1,0:T(8,128)(2,1)}, bf16[256,1024]{1,0:T(8,128)(2,1)}, bf16[256,1024]{1,0:T(8,128)(2,1)}, bf16[256,1024]{1,0:T(8,128)(2,1)}, bf16[...) custom-call(s32[4]{0:T(128)} %add_multiply_fusion.2.starts_ref, ...), custom_call_target="tpu_custom_call" | custom-call | flops 11000000 | bytes 40000 | tf_op jit(solution)/shard_map/attn_fwd/pallas_call | solution.py:182
  118.8 37.1 %collective-permute-done.10 = bf16[256,1024]{1,0:T(8,128)(2,1)S(1)} collective-permute-done((bf16[256,1024]{1,0:T(8,128)(2,1)}, bf16[256,1024]{1,0:T(8,128)(2,1)S(1)}, u32[]{:S(2)}, u32[]{:S(2)}) %collective-permute-start.10) | collective-permute-done | bytes 524320 | tf_op jit(solution)/shard_map/ppermute | solution.py:618
  164.7 14.2 %collective-permute-done.14.refs_3_ = bf16[1,384,1024]{2,1,0:T(8,128)(2,1)S(1)} collective-permute-done((bf16[1,384,1024]{2,1,0:T(8,128)(2,1)S(1)}, bf16[1,384,1024]{2,1,0:T(8,128)(2,1)S(1)}, u32[]{:S(2)}, u32[]{:S(2)}) %collective-permute-start.14) | collective-permute-done | bytes 786464 | tf_op jit(solution)/shard_map/ppermute | solution.py:618
  185.4 14.6 %dispatch.2 = (bf16[4,8,96,1024]{3,2,1,0:T(8,128)(2,1)}, bf16[4,8,96,1024]{3,2,1,0:T(8,128)(2,1)}, bf16[2048,384]{1,0:T(8,128)(2,1)}, bf16[2048,384]{1,0:T(8,128)(2,1)}) custom-call(s32[1]{0:T(128)} %bitcast.16.offset_ref, bf16[2048,1024]{1,0:T(8,128)(2,1)} %all-gather.11.cloned.1.call-done.refs_0_, bf16[2048,1152]{1,0:T(8,128)(2,1)} %all-gather.9.cloned.1.call-done.refs_1_, ...), custom_call_target="tpu_custom_call" | custom-call | flops 11000000 | bytes 40000 | tf_op jit(solution)/shard_map/dispatch/pallas_call | solution.py:363
  200.0 27.8 %experts.4 = (bf16[2,768,1024]{2,1,0:T(8,128)(2,1)}, bf16[2,768,1024]{2,1,0:T(8,128)(2,1)}, bf16[2,768,128]{2,1,0:T(8,128)(2,1)}, bf16[2,384,1024]{2,1,0:T(8,128...) custom-call(s32[5]{0:T(128)} %concatenate.33.place_ref, ...), custom_call_target="tpu_custom_call" | custom-call | flops 20000000 | bytes 60000 | tf_op jit(solution)/shard_map/experts/pallas_call | solution.py:533
  232.0 12.6 %collective-permute-done.18.refs_3_ = bf16[1,384,1024]{2,1,0:T(8,128)(2,1)S(1)} collective-permute-done((bf16[1,384,1024]{2,1,0:T(8,128)(2,1)S(1)}, bf16[1,384,1024]{2,1,0:T(8,128)(2,1)S(1)}, u32[]{:S(2)}, u32[]{:S(2)}) %collective-permute-start.18) | collective-permute-done | bytes 786464 | tf_op jit(solution)/shard_map/ppermute | solution.py:618
  247.5 28.0 %experts.5 = (bf16[2,768,1024]{2,1,0:T(8,128)(2,1)}, bf16[2,768,1024]{2,1,0:T(8,128)(2,1)}, bf16[2,768,128]{2,1,0:T(8,128)(2,1)}, bf16[2,384,1024]{2,1,0:T(8,128...) custom-call(s32[5]{0:T(128)} %concatenate.33.place_ref, ...), custom_call_target="tpu_custom_call" | custom-call | flops 20000000 | bytes 60000 | tf_op jit(solution)/shard_map/experts/pallas_call | solution.py:533
  275.5 13.3 %combine.1 = bf16[2048,2176]{1,0:T(8,128)(2,1)} custom-call(bf16[2,8,96,1024]{3,2,1,0:T(8,128)(2,1)} %bitcast.129, bf16[2,8,96,1024]{3,2,1,0:T(8,128)(2,1)} %bitcast.131, bf16[2,8,96,1024]{3,2,1,0:T(8,128)(2,1)} %bitcast.130, bf16[2,8,96,1024]{3,2,1,0:T(8,128)(2,1)} %bitcast.132, bf16[2,8,96,128]{3,2,1,0:T(8,128)(2,1)} %bitcast.142, ...), custom_call_target="tpu_custom_call" | custom-call | flops 5000000 | bytes 17000 | tf_op jit(solution)/shard_map/combine/pallas_call | solution.py:605
  288.8 14.9 %dispatch.3 = (bf16[4,8,96,1024]{3,2,1,0:T(8,128)(2,1)}, bf16[4,8,96,1024]{3,2,1,0:T(8,128)(2,1)}, bf16[2048,384]{1,0:T(8,128)(2,1)}, bf16[2048,384]{1,0:T(8,128)(2,1)}) custom-call(s32[1]{0:T(128)} %bitcast.16.offset_ref, bf16[2048,2176]{1,0:T(8,128)(2,1)} %all-gather.7.cloned.1.call-done.refs_0_, bf16[1024,128]{1,0:T(8,128)(2,1)} %pad.8.refs_2_.refs_1_), custom_call_target="tpu_custom_call" | custom-call | flops 11000000 | bytes 40000 | tf_op jit(solution)/shard_map/dispatch/pallas_call | solution.py:363
  303.8 30.2 %experts.6 = (bf16[2,768,1024]{2,1,0:T(8,128)(2,1)}, bf16[2,768,1024]{2,1,0:T(8,128)(2,1)}, bf16[2,768,128]{2,1,0:T(8,128)(2,1)}, bf16[2,384,1024]{2,1,0:T(8,128...) custom-call(s32[5]{0:T(128)} %concatenate.33.place_ref, ...), custom_call_target="tpu_custom_call" | custom-call | flops 20000000 | bytes 60000 | tf_op jit(solution)/shard_map/experts/pallas_call | solution.py:533
  335.9 30.4 %experts.7 = (bf16[2,768,1024]{2,1,0:T(8,128)(2,1)}, bf16[2,768,1024]{2,1,0:T(8,128)(2,1)}, bf16[2,768,128]{2,1,0:T(8,128)(2,1)}, bf16[2,384,1024]{2,1,0:T(8,128...) custom-call(s32[5]{0:T(128)} %concatenate.33.place_ref, ...), custom_call_target="tpu_custom_call" | custom-call | flops 20000000 | bytes 60000 | tf_op jit(solution)/shard_map/experts/pallas_call | solution.py:533
  366.5 9.1 %combine_grad.1 = bf16[2048,1152]{1,0:T(8,128)(2,1)} custom-call(bf16[2,8,96,1024]{3,2,1,0:T(8,128)(2,1)} %bitcast.135, bf16[2,8,96,1024]{3,2,1,0:T(8,128)(2,1)} %bitcast.136, bf16[2,8,96,128]{3,2,1,0:T(8,128)(2,1)} %bitcast.138, bf16[2,8,96,128]{3,2,1,0:T(8,128)(2,1)} %bitcast.139, bf16[2048,384]{1,0:T(8,128)(2,1)} %get-tuple-element.233.refs_4_), custom_call_target="tpu_custom_call" | custom-call | flops 5000000 | bytes 17000 | tf_op jit(solution)/shard_map/combine_grad/pallas_call | solution.py:605
  389.1 20.7 %collective-permute-done.22 = bf16[2,384,1024]{2,1,0:T(8,128)(2,1)} collective-permute-done((bf16[2,384,1024]{2,1,0:T(8,128)(2,1)}, bf16[2,384,1024]{2,1,0:T(8,128)(2,1)}, u32[]{:S(2)}, u32[]{:S(2)}) %collective-permute-start.22) | collective-permute-done | bytes 1572896 | tf_op jit(solution)/shard_map/ppermute | solution.py:618
  411.1 8.6 %combine_mix.1 = bf16[2048,1024]{1,0:T(8,128)(2,1)} custom-call(bf16[2,8,96,1024]{3,2,1,0:T(8,128)(2,1)} %bitcast.133, bf16[2,8,96,1024]{3,2,1,0:T(8,128)(2,1)} %bitcast.134, bf16[2048,384]{1,0:T(8,128)(2,1)} %get-tuple-element.250.refs_2_), custom_call_target="tpu_custom_call" | custom-call | flops 5000000 | bytes 17000 | tf_op jit(solution)/shard_map/combine_mix/pallas_call | solution.py:605
  423.5 10.1 %collective-permute-done.24.refs_16_ = bf16[256,1024]{1,0:T(8,128)(2,1)S(1)} collective-permute-done((bf16[256,1024]{1,0:T(8,128)(2,1)}, bf16[256,1024]{1,0:T(8,128)(2,1)S(1)}, u32[]{:S(2)}, u32[]{:S(2)}) %collective-permute-start.24) | collective-permute-done | bytes 524320 | tf_op jit(solution)/shard_map/ppermute | solution.py:618
  433.6 5.8 collective-permute-done.25.refs_17_
  449.2 23.5 %attn_bwd.2 = (bf16[256,1024]{1,0:T(8,128)(2,1)}, bf16[256,1024]{1,0:T(8,128)(2,1)}, bf16[256,1024]{1,0:T(8,128)(2,1)}, bf16[256,1024]{1,0:T(8,128)(2,1)}, bf16[1024,768]{1,0:T(8,128)(2,1)}, /*index=5*/f32[1,1024]{1,0:T(1,128)}) custom-call(s32[4]{0:T(128)} %add_multiply_fusion.2.starts_ref, bf16[256,1024]{1,0:T(8,128)(2,1)} %copy-done.12, ...), custom_call_target="tpu_custom_call" | custom-call | flops 18000000 | bytes 65000 | tf_op jit(solution)/shard_map/attn_bwd/pallas_call | solution.py:284
  482.2 7.5 %collective-permute-done.29.refs_16_ = bf16[256,1024]{1,0:T(8,128)(2,1)} collective-permute-done((bf16[256,1024]{1,0:T(8,128)(2,1)}, bf16[256,1024]{1,0:T(8,128)(2,1)}, u32[]{:S(2)}, u32[]{:S(2)}) %collective-permute-start.29) | collective-permute-done | bytes 524320 | tf_op jit(solution)/shard_map/ppermute | solution.py:618
  489.7 6.8 %collective-permute-done.30.refs_17_ = bf16[256,1024]{1,0:T(8,128)(2,1)} collective-permute-done((bf16[256,1024]{1,0:T(8,128)(2,1)}, bf16[256,1024]{1,0:T(8,128)(2,1)}, u32[]{:S(2)}, u32[]{:S(2)}) %collective-permute-start.30) | collective-permute-done | bytes 524320 | tf_op jit(solution)/shard_map/ppermute | solution.py:618
  510.4 23.8 %attn_bwd.3 = (bf16[256,1024]{1,0:T(8,128)(2,1)}, bf16[256,1024]{1,0:T(8,128)(2,1)}, bf16[256,1024]{1,0:T(8,128)(2,1)}, bf16[256,1024]{1,0:T(8,128)(2,1)}, bf16[1024,768]{1,0:T(8,128)(2,1)}, /*index=5*/f32[1,1024]{1,0:T(1,128)}) custom-call(s32[4]{0:T(128)} %add_multiply_fusion.2.starts_ref, bf16[256,1024]{1,0:T(8,128)(2,1)} %copy-done.11, ...), custom_call_target="tpu_custom_call" | custom-call | flops 18000000 | bytes 65000 | tf_op jit(solution)/shard_map/attn_bwd/pallas_call | solution.py:284
  540.8 3.2 convert_add_fusion.5
  557.7 3.0 pad_maximum_fusion
  575.2 16.2 %collective-permute-done.38 = bf16[256,1024]{1,0:T(8,128)(2,1)S(1)} collective-permute-done((bf16[256,1024]{1,0:T(8,128)(2,1)S(1)}, bf16[256,1024]{1,0:T(8,128)(2,1)S(1)}, u32[]{:S(2)}, u32[]{:S(2)}) %collective-permute-start.38) | collective-permute-done | bytes 524320 | tf_op jit(solution)/shard_map/ppermute | solution.py:618
  592.7 10.0 %collective-permute-done.41 = bf16[256,1024]{1,0:T(8,128)(2,1)S(1)} collective-permute-done((bf16[256,1024]{1,0:T(8,128)(2,1)S(1)}, bf16[256,1024]{1,0:T(8,128)(2,1)S(1)}, u32[]{:S(2)}, u32[]{:S(2)}) %collective-permute-start.41) | collective-permute-done | bytes 524320 | tf_op jit(solution)/shard_map/ppermute | solution.py:618
  (341 shorter events, 156.4 us)
Async XLA Ops:
  7.2 31.8 %all-gather.5.cloned.1.call-start = ((), (), s32[]{:S(2)}) async-start(), calls=%async_computation.4 | async-start | bytes 1769472 | tf_op jit(solution)/shard_map/all_gather | solution.py:688
  9.9 83.3 %all-gather.9.cloned.1.call-start = ((), (), s32[]{:S(2)}) async-start(), calls=%async_computation.6 | async-start | bytes 5308416 | tf_op jit(solution)/shard_map/all_gather | solution.py:688
  14.3 24.7 %collective-permute-start.1 = (bf16[256,1024]{1,0:T(8,128)(2,1)S(1)}, bf16[256,1024]{1,0:T(8,128)(2,1)}, u32[]{:S(2)}, u32[]{:S(2)}) collective-permute-start(bf16[256,1024]{1,0:T(8,128)(2,1)S(1)} %get-tuple-element.383.refs_0_), channel_id=1, source_target_pairs={{0,16},{8,24},{16,0},{24,8},{1,17},{9,25},{17,1},{25,9},{2,18},{10... | collective-permute-start | bytes 1572872 | tf_op jit(solution)/shard_map/ppermute | solution.py:618
  39.1 146.3 %all-gather.11.cloned.1.call-start = ((), (), s32[]{:S(2)}) async-start(), calls=%async_computation.7 | async-start | bytes 4718592 | tf_op jit(solution)/shard_map/all_gather | solution.py:688
  40.6 24.4 %collective-permute-start.4 = (bf16[256,1024]{1,0:T(8,128)(2,1)S(1)}, bf16[256,1024]{1,0:T(8,128)(2,1)S(1)}, u32[]{:S(2)}, u32[]{:S(2)}) collective-permute-start(bf16[256,1024]{1,0:T(8,128)(2,1)S(1)} %get-tuple-element.175.refs_0_), channel_id=1, source_target_pairs={{0,16},{8,24},{16,0},{24,8},{1,17},{9,25},{17,1},{25,9},{2,18},{10... | collective-permute-start | bytes 1572872 | tf_op jit(solution)/shard_map/ppermute | solution.py:618
  41.4 23.6 %collective-permute-start.5 = (bf16[256,1024]{1,0:T(8,128)(2,1)S(1)}, bf16[256,1024]{1,0:T(8,128)(2,1)S(1)}, u32[]{:S(2)}, u32[]{:S(2)}) collective-permute-start(bf16[256,1024]{1,0:T(8,128)(2,1)S(1)} %get-tuple-element.175.refs_0_), channel_id=1, source_target_pairs={{0,24},{8,16},{16,8},{24,0},{1,25},{9,17},{17,9},{25,1},{2,26},{10... | collective-permute-start | bytes 1572872 | tf_op jit(solution)/shard_map/ppermute | solution.py:618
  66.2 24.5 %collective-permute-start.7 = (bf16[256,1024]{1,0:T(8,128)(2,1)}, bf16[256,1024]{1,0:T(8,128)(2,1)S(1)}, u32[]{:S(2)}, u32[]{:S(2)}) collective-permute-start(bf16[256,1024]{1,0:T(8,128)(2,1)} %get-tuple-element.172), channel_id=1, source_target_pairs={{0,16},{8,24},{16,0},{24,8},{1,17},{9,25},{17,1},{25,9},{2,18},{10... | collective-permute-start | bytes 1572872 | tf_op jit(solution)/shard_map/ppermute | solution.py:618
  93.2 195.6 %all-gather.7.cloned.1.call-start = ((), (), s32[]{:S(2)}) async-start(), calls=%async_computation.5 | async-start | bytes 10027008 | tf_op jit(solution)/shard_map/all_gather | solution.py:688
  97.7 60.0 %collective-permute-start.12 = (bf16[2,384,1024]{2,1,0:T(8,128)(2,1)}, bf16[2,384,1024]{2,1,0:T(8,128)(2,1)}, u32[]{:S(2)}, u32[]{:S(2)}) collective-permute-start(bf16[2,384,1024]{2,1,0:T(8,128)(2,1)} %get-tuple-element.194.refs_0_), channel_id=1, source_target_pairs={{0,8},{8,0},{16,24},{24,16},{1,9},{9,1},{17,25},{25,17},{2,10},{10... | collective-permute-start | bytes 4718600 | tf_op jit(solution)/shard_map/ppermute | solution.py:618
  98.0 59.7 %collective-permute-start.13 = (bf16[2,384,1024]{2,1,0:T(8,128)(2,1)}, bf16[2,384,1024]{2,1,0:T(8,128)(2,1)}, u32[]{:S(2)}, u32[]{:S(2)}) collective-permute-start(bf16[2,384,1024]{2,1,0:T(8,128)(2,1)} %get-tuple-element.194.refs_0_), channel_id=1, source_target_pairs={{0,16},{8,24},{16,0},{24,8},{1,17},{9,25},{17,1},{25,9},{2,18},{10... | collective-permute-start | bytes 4718600 | tf_op jit(solution)/shard_map/ppermute | solution.py:618
  115.2 40.7 %collective-permute-start.10 = (bf16[256,1024]{1,0:T(8,128)(2,1)}, bf16[256,1024]{1,0:T(8,128)(2,1)S(1)}, u32[]{:S(2)}, u32[]{:S(2)}) collective-permute-start(bf16[256,1024]{1,0:T(8,128)(2,1)} %get-tuple-element.181), channel_id=1, source_target_pairs={{0,16},{8,24},{16,0},{24,8},{1,17},{9,25},{17,1},{25,9},{2,18},{10... | collective-permute-start | bytes 1572872 | tf_op jit(solution)/shard_map/ppermute | solution.py:618
  115.8 40.1 %collective-permute-start.11 = (bf16[256,1024]{1,0:T(8,128)(2,1)}, bf16[256,1024]{1,0:T(8,128)(2,1)S(1)}, u32[]{:S(2)}, u32[]{:S(2)}) collective-permute-start(bf16[256,1024]{1,0:T(8,128)(2,1)} %get-tuple-element.182), channel_id=1, source_target_pairs={{0,24},{8,16},{16,8},{24,0},{1,25},{9,17},{17,9},{25,1},{2,26},{10... | collective-permute-start | bytes 1572872 | tf_op jit(solution)/shard_map/ppermute | solution.py:618
  117.3 38.6 %collective-permute-start.9 = (bf16[256,1024]{1,0:T(8,128)(2,1)}, bf16[256,1024]{1,0:T(8,128)(2,1)S(1)}, u32[]{:S(2)}, u32[]{:S(2)}) collective-permute-start(bf16[256,1024]{1,0:T(8,128)(2,1)} %get-tuple-element.180), channel_id=1, source_target_pairs={{0,8},{8,0},{16,24},{24,16},{1,9},{9,1},{17,25},{25,17},{2,10},{10... | collective-permute-start | bytes 1572872 | tf_op jit(solution)/shard_map/ppermute | solution.py:618
  159.6 223.4 %reduce-scatter.7.cloned.1.call-start = ((), (), s32[]{:S(2)}) async-start(), calls=%async_computation.9 | async-start | bytes 10027008 | tf_op jit(solution)/shard_map/reduce_scatter | solution.py:692
  180.4 47.3 %collective-permute-start.16 = (bf16[2,384,1024]{2,1,0:T(8,128)(2,1)}, bf16[2,384,1024]{2,1,0:T(8,128)(2,1)}, u32[]{:S(2)}, u32[]{:S(2)}) collective-permute-start(bf16[2,384,1024]{2,1,0:T(8,128)(2,1)} %get-tuple-element.201.refs_0_), channel_id=1, source_target_pairs={{0,8},{8,0},{16,24},{24,16},{1,9},{9,1},{17,25},{25,17},{2,10},{10... | collective-permute-start | bytes 4718600 | tf_op jit(solution)/shard_map/ppermute | solution.py:618
  181.9 45.9 %collective-permute-start.17 = (bf16[2,384,1024]{2,1,0:T(8,128)(2,1)}, bf16[2,384,1024]{2,1,0:T(8,128)(2,1)}, u32[]{:S(2)}, u32[]{:S(2)}) collective-permute-start(bf16[2,384,1024]{2,1,0:T(8,128)(2,1)} %get-tuple-element.201.refs_0_), channel_id=1, source_target_pairs={{0,16},{8,24},{16,0},{24,8},{1,17},{9,25},{17,1},{25,9},{2,18},{10... | collective-permute-start | bytes 4718600 | tf_op jit(solution)/shard_map/ppermute | solution.py:618
  288.8 184.0 %reduce-scatter.5.cloned.1.call-start = ((), (), s32[]{:S(2)}) async-start(), calls=%async_computation.8 | async-start | bytes 5308416 | tf_op jit(solution)/shard_map/reduce_scatter | solution.py:692
  334.0 32.4 %collective-permute-start.20 = (bf16[2,384,1024]{2,1,0:T(8,128)(2,1)}, bf16[2,384,1024]{2,1,0:T(8,128)(2,1)}, u32[]{:S(2)}, u32[]{:S(2)}) collective-permute-start(bf16[2,384,1024]{2,1,0:T(8,128)(2,1)} %get-tuple-element.224), channel_id=1, source_target_pairs={{0,8},{8,0},{16,24},{24,16},{1,9},{9,1},{17,25},{25,17},{2,10},{10... | collective-permute-start | bytes 4718600 | tf_op jit(solution)/shard_map/ppermute | solution.py:618
  334.9 31.5 %collective-permute-start.21 = (bf16[2,384,1024]{2,1,0:T(8,128)(2,1)}, bf16[2,384,1024]{2,1,0:T(8,128)(2,1)}, u32[]{:S(2)}, u32[]{:S(2)}) collective-permute-start(bf16[2,384,1024]{2,1,0:T(8,128)(2,1)} %get-tuple-element.225), channel_id=1, source_target_pairs={{0,16},{8,24},{16,0},{24,8},{1,17},{9,25},{17,1},{25,9},{2,18},{10... | collective-permute-start | bytes 4718600 | tf_op jit(solution)/shard_map/ppermute | solution.py:618
  375.6 158.7 %reduce-scatter.9.cloned.1.call-start = ((), (), s32[]{:S(2)}) async-start(), calls=%async_computation.10 | async-start | bytes 4718592 | tf_op jit(solution)/shard_map/reduce_scatter | solution.py:692
  378.5 31.3 %collective-permute-start.22 = (bf16[2,384,1024]{2,1,0:T(8,128)(2,1)}, bf16[2,384,1024]{2,1,0:T(8,128)(2,1)}, u32[]{:S(2)}, u32[]{:S(2)}) collective-permute-start(bf16[2,384,1024]{2,1,0:T(8,128)(2,1)} %get-tuple-element.242), channel_id=1, source_target_pairs={{0,8},{8,0},{16,24},{24,16},{1,9},{9,1},{17,25},{25,17},{2,10},{10... | collective-permute-start | bytes 4718600 | tf_op jit(solution)/shard_map/ppermute | solution.py:618
  379.7 31.4 %collective-permute-start.23 = (bf16[2,384,1024]{2,1,0:T(8,128)(2,1)}, bf16[2,384,1024]{2,1,0:T(8,128)(2,1)}, u32[]{:S(2)}, u32[]{:S(2)}) collective-permute-start(bf16[2,384,1024]{2,1,0:T(8,128)(2,1)} %get-tuple-element.243), channel_id=1, source_target_pairs={{0,16},{8,24},{16,0},{24,8},{1,17},{9,25},{17,1},{25,9},{2,18},{10... | collective-permute-start | bytes 4718600 | tf_op jit(solution)/shard_map/ppermute | solution.py:618
  419.7 187.1 %reduce-scatter.11.cloned.1.call-start = ((), (), s32[]{:S(2)}) async-start(), calls=%async_computation.11 | async-start | bytes 1880064 | tf_op jit(solution)/shard_map/reduce_scatter | solution.py:692
  446.9 25.8 %collective-permute-start.27 = (bf16[1,384,1024]{2,1,0:T(8,128)(2,1)}, bf16[1,384,1024]{2,1,0:T(8,128)(2,1)}, u32[]{:S(2)}, u32[]{:S(2)}) collective-permute-start(bf16[1,384,1024]{2,1,0:T(8,128)(2,1)} %get-tuple-element.371), channel_id=1, source_target_pairs={{0,16},{8,24},{16,0},{24,8},{1,17},{9,25},{17,1},{25,9},{2,18},{10... | collective-permute-start | bytes 2359304 | tf_op jit(solution)/shard_map/ppermute | solution.py:618
  448.0 24.7 %collective-permute-start.28 = (bf16[1,384,1024]{2,1,0:T(8,128)(2,1)}, bf16[1,384,1024]{2,1,0:T(8,128)(2,1)}, u32[]{:S(2)}, u32[]{:S(2)}) collective-permute-start(bf16[1,384,1024]{2,1,0:T(8,128)(2,1)} %get-tuple-element.368), channel_id=1, source_target_pairs={{0,8},{8,0},{16,24},{24,16},{1,9},{9,1},{17,25},{25,17},{2,10},{10... | collective-permute-start | bytes 2359304 | tf_op jit(solution)/shard_map/ppermute | solution.py:618
  503.6 30.7 %collective-permute-start.32 = (bf16[1,384,1024]{2,1,0:T(8,128)(2,1)}, bf16[1,384,1024]{2,1,0:T(8,128)(2,1)}, u32[]{:S(2)}, u32[]{:S(2)}) collective-permute-start(bf16[1,384,1024]{2,1,0:T(8,128)(2,1)} %get-tuple-element.367), channel_id=1, source_target_pairs={{0,16},{8,24},{16,0},{24,8},{1,17},{9,25},{17,1},{25,9},{2,18},{10... | collective-permute-start | bytes 2359304 | tf_op jit(solution)/shard_map/ppermute | solution.py:618
  504.0 30.2 %collective-permute-start.33 = (bf16[1,384,1024]{2,1,0:T(8,128)(2,1)}, bf16[1,384,1024]{2,1,0:T(8,128)(2,1)}, u32[]{:S(2)}, u32[]{:S(2)}) collective-permute-start(bf16[1,384,1024]{2,1,0:T(8,128)(2,1)} %get-tuple-element.364), channel_id=1, source_target_pairs={{0,8},{8,0},{16,24},{24,16},{1,9},{9,1},{17,25},{25,17},{2,10},{10... | collective-permute-start | bytes 2359304 | tf_op jit(solution)/shard_map/ppermute | solution.py:618
  565.5 25.9 %collective-permute-start.38 = (bf16[256,1024]{1,0:T(8,128)(2,1)S(1)}, bf16[256,1024]{1,0:T(8,128)(2,1)S(1)}, u32[]{:S(2)}, u32[]{:S(2)}) collective-permute-start(bf16[256,1024]{1,0:T(8,128)(2,1)S(1)} %copy-done.67), channel_id=1, source_target_pairs={{0,16},{8,24},{16,0},{24,8},{1,17},{9,25},{17,1},{25,9},{2,18},{10... | collective-permute-start | bytes 1572872 | tf_op jit(solution)/shard_map/ppermute | solution.py:618
  567.1 24.3 %collective-permute-start.39 = (bf16[256,1024]{1,0:T(8,128)(2,1)S(1)}, bf16[256,1024]{1,0:T(8,128)(2,1)S(1)}, u32[]{:S(2)}, u32[]{:S(2)}) collective-permute-start(bf16[256,1024]{1,0:T(8,128)(2,1)S(1)} %copy-done.66), channel_id=1, source_target_pairs={{0,24},{8,16},{16,8},{24,0},{1,25},{9,17},{17,9},{25,1},{2,26},{10... | collective-permute-start | bytes 1572872 | tf_op jit(solution)/shard_map/ppermute | solution.py:618
  568.8 23.9 %collective-permute-start.40 = (bf16[256,1024]{1,0:T(8,128)(2,1)S(1)}, bf16[256,1024]{1,0:T(8,128)(2,1)S(1)}, u32[]{:S(2)}, u32[]{:S(2)}) collective-permute-start(bf16[256,1024]{1,0:T(8,128)(2,1)S(1)} %copy-done.70), channel_id=1, source_target_pairs={{0,8},{8,0},{16,24},{24,16},{1,9},{9,1},{17,25},{25,17},{2,10},{10... | collective-permute-start | bytes 1572872 | tf_op jit(solution)/shard_map/ppermute | solution.py:618
  569.0 33.6 %collective-permute-start.41 = (bf16[256,1024]{1,0:T(8,128)(2,1)S(1)}, bf16[256,1024]{1,0:T(8,128)(2,1)S(1)}, u32[]{:S(2)}, u32[]{:S(2)}) collective-permute-start(bf16[256,1024]{1,0:T(8,128)(2,1)S(1)} %copy-done.69), channel_id=1, source_target_pairs={{0,16},{8,24},{16,0},{24,8},{1,17},{9,25},{17,1},{25,9},{2,18},{10... | collective-permute-start | bytes 1572872 | tf_op jit(solution)/shard_map/ppermute | solution.py:618
  572.5 30.1 %collective-permute-start.42 = (bf16[256,1024]{1,0:T(8,128)(2,1)S(1)}, bf16[256,1024]{1,0:T(8,128)(2,1)S(1)}, u32[]{:S(2)}, u32[]{:S(2)}) collective-permute-start(bf16[256,1024]{1,0:T(8,128)(2,1)S(1)} %copy-done.68), channel_id=1, source_target_pairs={{0,24},{8,16},{16,8},{24,0},{1,25},{9,17},{17,9},{25,1},{2,26},{10... | collective-permute-start | bytes 1572872 | tf_op jit(solution)/shard_map/ppermute | solution.py:618
  (91 other events, 1003.5 us)
Sparse Core Ops, SparseCore 0:
  10.2 27.7 all-gather.4
  40.2 50.7 all-gather.8
  93.3 44.9 all-gather.10
  159.7 84.2 all-gather.6
  288.9 94.1 reduce-scatter.6
  385.2 53.3 reduce-scatter.4
  441.4 48.3 reduce-scatter.8
  557.5 36.1 reduce-scatter.10

commit v5 on v4

--- a/solution.py
+++ b/solution.py
@@ -666,22 +666,31 @@
     return [lax.psum_scatter(grads[0], "tp", scatter_dimension=0)]
 
 
-def sum_weights_far(near):
+def far_sums(near):
     if square():
-        came_x, came_y, own, _, _, kept_y, kept_x = [value.astype(f32) for value in near]
-        first = came_x[:1] + own[:1]
-        second = came_y[:1] + own[1:]
-        far_first = flip((came_x[1:] + kept_y).astype(bf16), 2)
-        far_second = flip((came_y[1:] + kept_x).astype(bf16), 1)
-        return [first, second, far_first, far_second]
-    return near
-
-
-def add_far(far):
+        came_x, came_y, _, _, _, kept_y, kept_x = near
+        first = came_x[1:].astype(f32) + kept_y.astype(f32)
+        second = came_y[1:].astype(f32) + kept_x.astype(f32)
+        return [first.astype(bf16), second.astype(bf16)]
+    return []
+
+
+def send_far(sums):
     if square():
-        first, second, far_first, far_second = far
-        return jnp.concatenate([first + far_first, second + far_second])
-    return far[0].astype(f32)
+        return [flip(sums[0], 2), flip(sums[1], 1)]
+    return []
+
+
+def add_far(near, far):
+    if square():
+        came_x, came_y, own = [value.astype(f32) for value in near[:3]]
+        return jnp.concatenate(
+            [
+                came_x[:1] + own[:1] + far[0].astype(f32),
+                came_y[:1] + own[1:] + far[1].astype(f32),
+            ]
+        )
+    return near[0].astype(f32)
 
 
 def ag_ep(value, axis=0):
@@ -767,19 +776,23 @@
         )
     came = []
     kept = []
+    for m in range(micro):
+        if m:
+            fixed[m] = (after(starts, parts), token_full[m], *fixed[m][2:])
+        parts, saved = attention_forward(*fixed[m])
+        kept.append(saved)
+        if m == 0:
+            parts, token_full = lax.optimization_barrier((parts, token_full))
+        if m == micro - 1:
+            came[0] = after(came[0], parts)
+        came.append(send_rows(parts))
+
     hiddens = []
     normed_twos = []
     scales = []
     gate_rows = []
     full = []
     for m in range(micro):
-        if m:
-            fixed[m] = (after(starts, normed_twos), token_full[m], *fixed[m][2:])
-        parts, saved = attention_forward(*fixed[m])
-        kept.append(saved)
-        if m == 0:
-            parts, token_full = lax.optimization_barrier((parts, token_full))
-        came.append(send_rows(parts))
         if m == 0:
             near = [gather_weights_near(after(packed_weights[0], came[0]))]
         branch = add_rows(came[m])
@@ -804,7 +817,7 @@
             full.append([ag_ep(jnp.concatenate([normed_two, cotangent[m], masks[m]], axis=-1))])
 
     pieces = [gather_weights_far(near[0])]
-    near.append(gather_weights_near(after(packed_weights[1], pieces[0])))
+    near.append(gather_weights_near(after(packed_weights[1], near[0])))
     old = [(), ()]
     mixes = []
     grads = []
@@ -837,11 +850,14 @@
         else:
             near_first = sum_weights_near(old[0])
             dxs, near_first = lax.optimization_barrier((dxs, near_first))
-            near_second = sum_weights_near(old[1])
             grad = combine(
                 combine_grad_body, [*dxs, *hs], 2, [pt], MODEL_WIDTH + LANES, "combine_grad"
             )
             grads.append(rs_ep(grad))
+            outs, pgt = after((outs, pgt), grad)
+            mix = combine(combine_mix_body, outs, 2, [pgt], MODEL_WIDTH, "combine_mix")
+            mixes.append(rs_ep(mix))
+            grads[0] = after(grads[0], mix)
     input_grads = []
     acc_router = 0.0
     acc_gain_one = 0.0
@@ -853,7 +869,7 @@
     for m in range(micro):
         grad = grads[m]
         if m:
-            grad, far_first = after((grad, far_first), parts)
+            grad, near_second = after((grad, near_second), parts)
         grad = grad.astype(f32)
         h_rows = grad[:, MODEL_WIDTH:]
         grad_logits = (
@@ -871,24 +887,18 @@
         )
         acc_gain_two = acc_gain_two + jnp.sum(grad_normed * hiddens[m] * scale, axis=0)
         grad_branch = (residual_scale * grad_hidden).astype(bf16)
-        if m == 0:
-            outs, pgt, grad_branch, near_second = lax.optimization_barrier(
-                (outs, pgt, grad_branch, near_second)
-            )
-            mix = combine(combine_mix_body, outs, 2, [pgt], MODEL_WIDTH, "combine_mix")
-            mixes.append(rs_ep(mix))
         grad_branch = gather_rows(grad_branch)
         if m == 0:
-            grad_branch = after(grad_branch, mix)
-            far_first = sum_weights_far(after(near_first, grad_branch))
+            near_second = sum_weights_near(after(old[1], grad_branch))
         if m == micro - 1:
-            far_second = sum_weights_far(after(near_second, grad_branch))
+            far_first = send_far(after(far_sums(near_first), grad_branch))
+            far_second = send_far(after(far_sums(near_second), grad_branch))
         parts, (gweights, ggain) = attention_backward(*fixed[m], kept[m], grad_branch)
         backs.append(parts)
         grad_hiddens.append(grad_hidden)
         if m == micro - 1:
-            parts, gweights, ggain, far_second, mixes = lax.optimization_barrier(
-                (parts, gweights, ggain, far_second, mixes)
+            parts, gweights, ggain, far_first, mixes = lax.optimization_barrier(
+                (parts, gweights, ggain, far_first, mixes)
             )
             backs[-1] = parts
         acc_weights = acc_weights + gweights.astype(f32)
@@ -911,24 +921,6 @@
         ).astype(bf16)
     else:
         small = lax.psum_scatter(small, "tp", scatter_dimension=0, tiled=True)
-    backs = [send_rows(after(parts, small)) for parts in backs]
-    for m in range(micro):
-        grad_normed = add_rows(backs[m])
-        inputs = tokens[m].astype(f32)
-        scale = lax.rsqrt(jnp.mean(inputs * inputs, axis=-1, keepdims=True) + epsilon)
-        weighted = grad_normed * gain_one
-        inner = jnp.mean(weighted * inputs, axis=-1, keepdims=True)
-        input_grads.append(
-            grad_hiddens[m] + scale * weighted - inputs * scale * scale * scale * inner
-        )
-    hiddens, mixes, far_first = after((hiddens, mixes, far_first), parts)
-    outputs = [
-        (hiddens[m] + residual_scale * mixes[m].astype(f32)).astype(bf16) for m in range(micro)
-    ]
-    grad_gate_up, grad_down = unpack_weights(
-        jnp.concatenate([add_far(far_first), add_far(far_second)]), w_gate_up.shape[1]
-    )
-
     columns = acc_weights.shape[1]
     own_rows = MODEL_WIDTH // ep_size
     small_rows = rows // ep_size
@@ -942,7 +934,25 @@
         ],
         axis=1,
     )
-    summed = rs_ep(packed.reshape(-1, columns)).astype(f32)
+    packed = packed.reshape(-1, columns)
+    summed = rs_ep(packed).astype(f32)
+    hiddens, mixes, far_first, far_second = after((hiddens, mixes, far_first, far_second), packed)
+    backs = [send_rows(after(parts, packed)) for parts in backs]
+    for m in range(micro):
+        grad_normed = add_rows(backs[m])
+        inputs = tokens[m].astype(f32)
+        scale = lax.rsqrt(jnp.mean(inputs * inputs, axis=-1, keepdims=True) + epsilon)
+        weighted = grad_normed * gain_one
+        inner = jnp.mean(weighted * inputs, axis=-1, keepdims=True)
+        input_grads.append(
+            grad_hiddens[m] + scale * weighted - inputs * scale * scale * scale * inner
+        )
+    outputs = [
+        (hiddens[m] + residual_scale * mixes[m].astype(f32)).astype(bf16) for m in range(micro)
+    ]
+    grad_gate_up, grad_down = unpack_weights(
+        jnp.concatenate([add_far(near_first, far_first), add_far(near_second, far_second)]), w_gate_up.shape[1]
+    )
     split = local_heads * GROUP_COLS
     grad_qkv = summed[:own_rows, :split].reshape(own_rows, local_heads, GROUP_COLS)
     grad_out = summed[:own_rows, split:].T.reshape(local_heads, LANES, own_rows)

time: 625 us -> 611 us (0.978)
  waiting for transfers between devices: 186 us -> 177 us
    ppermute x43, waiting for transfers between devices: 185 us -> 177 us  [flip(): return lax.ppermute(value, 'tp', [(t, t ^ bits) for t in range(4)])]
    convert_element_type x9 -> x7, other arithmetic: 15.2 us -> 17.6 us  [the longest x4 9.53 us: far_sums(): return [first.astype(bf16), second.astype(bf16)]]
  transfers between devices with their start and end apart: 51 -> 51, of which waited for: 21 -> 23; matrix products, arithmetic and copies ran while one was open for 15% -> 16% of each run, Pallas kernels for 41% -> 42%
where the time goes in v5:
time: 611 us; the launch traced here: 604 us
  Pallas kernels  254 us (42%)
  waiting for transfers between devices  177 us (29%)
  other arithmetic  65.3 us (11%)
  starting transfers between devices  49 us (8%)
  local copies, waits for them, and re-layouts  34.7 us (6%)
  between operations  15.2 us (2%)
  matrix products  8.99 us (1%)
    ppermute x43, waiting for transfers between devices, flip(): return lax.ppermute(value, 'tp', [(t, t ^ bits) for t in range(4)])  177 us
    pallas_call x4, Pallas kernels, run_experts(): pl.pallas_call(functools.partial(experts_body, base=base, slices=slices,...  116 us
    ppermute x43, starting transfers between devices, flip(): return lax.ppermute(value, 'tp', [(t, t ^ bits) for t in range(4)])  47.9 us
    pallas_call x2, Pallas kernels, attention_backward(): pl.pallas_call(functools.partial(attention_backward_body, count=count), o...  47.5 us
    pallas_call x3, Pallas kernels, combine(): pl.pallas_call(functools.partial(body, count=count), grid=(blocks,), in_s...  31.1 us
    pallas_call x2, Pallas kernels, dispatch(): pl.pallas_call(functools.partial(dispatch_body, local=local, count=len(so...  29.6 us
    pallas_call x2, Pallas kernels, attention_forward(): pl.pallas_call(functools.partial(attention_forward_body, count=count), ou...  29.3 us
  transfers between devices with their start and end apart: 51, of which 23 were waited for; matrix products, arithmetic and copies ran while one was open for 16% of the time, Pallas kernels for 42%

profile of v5, /device:TPU:0, one launch (start us, length us, event | category | flops | bytes accessed | tf_op | source)
XLA Modules:
  0.0 604.2 jit_solution(11229817421871597211)
XLA Ops:
  25.6 5.6 fusion.25
  31.2 7.8 %collective-permute-done.1.refs_2_ = bf16[256,1024]{1,0:T(8,128)(2,1)} collective-permute-done((bf16[256,1024]{1,0:T(8,128)(2,1)S(1)}, bf16[256,1024]{1,0:T(8,128)(2,1)}, u32[]{:S(2)}, u32[]{:S(2)}) %collective-permute-start.1) | collective-permute-done | bytes 524320 | tf_op jit(solution)/shard_map/ppermute | solution.py:618
  45.1 14.7 %attn_fwd.2 = (bf16[256,1024]{1,0:T(8,128)(2,1)}, bf16[256,1024]{1,0:T(8,128)(2,1)}, bf16[256,1024]{1,0:T(8,128)(2,1)}, bf16[256,1024]{1,0:T(8,128)(2,1)}, bf16[...) custom-call(s32[4]{0:T(128)} %add_multiply_fusion.2.starts_ref, ...), custom_call_target="tpu_custom_call" | custom-call | flops 11000000 | bytes 40000 | tf_op jit(solution)/shard_map/attn_fwd/pallas_call | solution.py:182
  59.8 5.2 collective-permute-done.4.refs_2_
  69.6 14.6 %attn_fwd.3 = (bf16[256,1024]{1,0:T(8,128)(2,1)}, bf16[256,1024]{1,0:T(8,128)(2,1)}, bf16[256,1024]{1,0:T(8,128)(2,1)}, bf16[256,1024]{1,0:T(8,128)(2,1)}, bf16[...) custom-call(s32[4]{0:T(128)} %add_multiply_fusion.2.starts_ref, ...), custom_call_target="tpu_custom_call" | custom-call | flops 11000000 | bytes 40000 | tf_op jit(solution)/shard_map/attn_fwd/pallas_call | solution.py:182
  87.7 16.3 %collective-permute-done.7 = bf16[256,1024]{1,0:T(8,128)(2,1)S(1)} collective-permute-done((bf16[256,1024]{1,0:T(8,128)(2,1)}, bf16[256,1024]{1,0:T(8,128)(2,1)S(1)}, u32[]{:S(2)}, u32[]{:S(2)}) %collective-permute-start.7) | collective-permute-done | bytes 524320 | tf_op jit(solution)/shard_map/ppermute | solution.py:618
  104.0 10.1 %collective-permute-done.10 = bf16[256,1024]{1,0:T(8,128)(2,1)S(1)} collective-permute-done((bf16[256,1024]{1,0:T(8,128)(2,1)}, bf16[256,1024]{1,0:T(8,128)(2,1)S(1)}, u32[]{:S(2)}, u32[]{:S(2)}) %collective-permute-start.10) | collective-permute-done | bytes 524320 | tf_op jit(solution)/shard_map/ppermute | solution.py:618
  123.5 33.2 %collective-permute-done.12.refs_1_ = bf16[2,384,1024]{2,1,0:T(8,128)(2,1)S(1)} collective-permute-done((bf16[2,384,1024]{2,1,0:T(8,128)(2,1)S(1)}, bf16[2,384,1024]{2,1,0:T(8,128)(2,1)S(1)}, u32[]{:S(2)}, u32[]{:S(2)}) %collective-permute-start.12) | collective-permute-done | bytes 1572896 | tf_op jit(solution)/shard_map/ppermute | solution.py:618
  170.0 14.7 %dispatch.2 = (bf16[4,8,96,1024]{3,2,1,0:T(8,128)(2,1)}, bf16[4,8,96,1024]{3,2,1,0:T(8,128)(2,1)}, bf16[2048,384]{1,0:T(8,128)(2,1)}, bf16[2048,384]{1,0:T(8,128)(2,1)}) custom-call(s32[1]{0:T(128)} %bitcast.15.offset_ref, bf16[2048,1024]{1,0:T(8,128)(2,1)} %all-gather.11.cloned.1.call-done.refs_0_, bf16[2048,1152]{1,0:T(8,128)(2,1)} %all-gather.9.cloned.1.call-done.refs_1_, ...), custom_call_target="tpu_custom_call" | custom-call | flops 11000000 | bytes 40000 | tf_op jit(solution)/shard_map/dispatch/pallas_call | solution.py:363
  184.7 27.6 %collective-permute-done.14.refs_3_ = bf16[1,384,1024]{2,1,0:T(8,128)(2,1)} collective-permute-done((bf16[1,384,1024]{2,1,0:T(8,128)(2,1)}, bf16[1,384,1024]{2,1,0:T(8,128)(2,1)}, u32[]{:S(2)}, u32[]{:S(2)}) %collective-permute-start.14) | collective-permute-done | bytes 786464 | tf_op jit(solution)/shard_map/ppermute | solution.py:618
  212.3 27.8 %experts.4 = (bf16[2,768,1024]{2,1,0:T(8,128)(2,1)}, bf16[2,768,1024]{2,1,0:T(8,128)(2,1)}, bf16[2,768,128]{2,1,0:T(8,128)(2,1)}, bf16[2,384,1024]{2,1,0:T(8,128...) custom-call(s32[5]{0:T(128)} %concatenate.33.place_ref, ...), custom_call_target="tpu_custom_call" | custom-call | flops 20000000 | bytes 60000 | tf_op jit(solution)/shard_map/experts/pallas_call | solution.py:533
  244.6 13.5 %collective-permute-done.18.refs_3_ = bf16[1,384,1024]{2,1,0:T(8,128)(2,1)S(1)} collective-permute-done((bf16[1,384,1024]{2,1,0:T(8,128)(2,1)S(1)}, bf16[1,384,1024]{2,1,0:T(8,128)(2,1)S(1)}, u32[]{:S(2)}, u32[]{:S(2)}) %collective-permute-start.18) | collective-permute-done | bytes 786464 | tf_op jit(solution)/shard_map/ppermute | solution.py:618
  261.5 27.8 %experts.5 = (bf16[2,768,1024]{2,1,0:T(8,128)(2,1)}, bf16[2,768,1024]{2,1,0:T(8,128)(2,1)}, bf16[2,768,128]{2,1,0:T(8,128)(2,1)}, bf16[2,384,1024]{2,1,0:T(8,128...) custom-call(s32[5]{0:T(128)} %concatenate.33.place_ref, ...), custom_call_target="tpu_custom_call" | custom-call | flops 20000000 | bytes 60000 | tf_op jit(solution)/shard_map/experts/pallas_call | solution.py:533
  289.3 13.2 %combine.1 = bf16[2048,2176]{1,0:T(8,128)(2,1)} custom-call(bf16[2,8,96,1024]{3,2,1,0:T(8,128)(2,1)} %bitcast.129, bf16[2,8,96,1024]{3,2,1,0:T(8,128)(2,1)} %bitcast.131, bf16[2,8,96,1024]{3,2,1,0:T(8,128)(2,1)} %bitcast.130, bf16[2,8,96,1024]{3,2,1,0:T(8,128)(2,1)} %bitcast.132, bf16[2,8,96,128]{3,2,1,0:T(8,128)(2,1)} %bitcast.142, ...), custom_call_target="tpu_custom_call" | custom-call | flops 5000000 | bytes 17000 | tf_op jit(solution)/shard_map/combine/pallas_call | solution.py:605
  302.6 15.0 %dispatch.3 = (bf16[4,8,96,1024]{3,2,1,0:T(8,128)(2,1)}, bf16[4,8,96,1024]{3,2,1,0:T(8,128)(2,1)}, bf16[2048,384]{1,0:T(8,128)(2,1)}, bf16[2048,384]{1,0:T(8,128)(2,1)}) custom-call(s32[1]{0:T(128)} %bitcast.15.offset_ref, bf16[2048,2176]{1,0:T(8,128)(2,1)} %all-gather.7.cloned.1.call-done.refs_0_, bf16[1024,128]{1,0:T(8,128)(2,1)} %pad.8.refs_2_.refs_1_), custom_call_target="tpu_custom_call" | custom-call | flops 11000000 | bytes 40000 | tf_op jit(solution)/shard_map/dispatch/pallas_call | solution.py:363
  317.6 30.1 %experts.6 = (bf16[2,768,1024]{2,1,0:T(8,128)(2,1)}, bf16[2,768,1024]{2,1,0:T(8,128)(2,1)}, bf16[2,768,128]{2,1,0:T(8,128)(2,1)}, bf16[2,384,1024]{2,1,0:T(8,128...) custom-call(s32[5]{0:T(128)} %concatenate.33.place_ref, ...), custom_call_target="tpu_custom_call" | custom-call | flops 20000000 | bytes 60000 | tf_op jit(solution)/shard_map/experts/pallas_call | solution.py:533
  349.3 30.5 %experts.7 = (bf16[2,768,1024]{2,1,0:T(8,128)(2,1)}, bf16[2,768,1024]{2,1,0:T(8,128)(2,1)}, bf16[2,768,128]{2,1,0:T(8,128)(2,1)}, bf16[2,384,1024]{2,1,0:T(8,128...) custom-call(s32[5]{0:T(128)} %concatenate.33.place_ref, ...), custom_call_target="tpu_custom_call" | custom-call | flops 20000000 | bytes 60000 | tf_op jit(solution)/shard_map/experts/pallas_call | solution.py:533
  380.7 9.1 %combine_grad.1 = bf16[2048,1152]{1,0:T(8,128)(2,1)} custom-call(bf16[2,8,96,1024]{3,2,1,0:T(8,128)(2,1)} %bitcast.134, bf16[2,8,96,1024]{3,2,1,0:T(8,128)(2,1)} %bitcast.136, bf16[2,8,96,128]{3,2,1,0:T(8,128)(2,1)} %bitcast.138, bf16[2,8,96,128]{3,2,1,0:T(8,128)(2,1)} %bitcast.139, bf16[2048,384]{1,0:T(8,128)(2,1)} %get-tuple-element.230.refs_4_), custom_call_target="tpu_custom_call" | custom-call | flops 5000000 | bytes 17000 | tf_op jit(solution)/shard_map/combine_grad/pallas_call | solution.py:605
  390.0 8.7 %combine_mix.1 = bf16[2048,1024]{1,0:T(8,128)(2,1)} custom-call(bf16[2,8,96,1024]{3,2,1,0:T(8,128)(2,1)} %bitcast.133, bf16[2,8,96,1024]{3,2,1,0:T(8,128)(2,1)} %bitcast.135, bf16[2048,384]{1,0:T(8,128)(2,1)} %get-tuple-element.241.refs_2_), custom_call_target="tpu_custom_call" | custom-call | flops 5000000 | bytes 17000 | tf_op jit(solution)/shard_map/combine_mix/pallas_call | solution.py:605
  412.1 10.9 %collective-permute-done.22.refs_16_ = bf16[256,1024]{1,0:T(8,128)(2,1)S(1)} collective-permute-done((bf16[256,1024]{1,0:T(8,128)(2,1)S(1)}, bf16[256,1024]{1,0:T(8,128)(2,1)S(1)}, u32[]{:S(2)}, u32[]{:S(2)}) %collective-permute-start.22) | collective-permute-done | bytes 524320 | tf_op jit(solution)/shard_map/ppermute | solution.py:618
  422.9 6.1 %collective-permute-done.23.refs_17_ = bf16[256,1024]{1,0:T(8,128)(2,1)S(1)} collective-permute-done((bf16[256,1024]{1,0:T(8,128)(2,1)S(1)}, bf16[256,1024]{1,0:T(8,128)(2,1)S(1)}, u32[]{:S(2)}, u32[]{:S(2)}) %collective-permute-start.23) | collective-permute-done | bytes 524320 | tf_op jit(solution)/shard_map/ppermute | solution.py:618
  442.3 23.5 %attn_bwd.2 = (bf16[256,1024]{1,0:T(8,128)(2,1)}, bf16[256,1024]{1,0:T(8,128)(2,1)}, bf16[256,1024]{1,0:T(8,128)(2,1)}, bf16[256,1024]{1,0:T(8,128)(2,1)}, bf16[1024,768]{1,0:T(8,128)(2,1)}, /*index=5*/f32[1,1024]{1,0:T(1,128)}) custom-call(s32[4]{0:T(128)} %add_multiply_fusion.2.starts_ref, bf16[256,1024]{1,0:T(8,128)(2,1)} %copy-done.10, ...), custom_call_target="tpu_custom_call" | custom-call | flops 18000000 | bytes 65000 | tf_op jit(solution)/shard_map/attn_bwd/pallas_call | solution.py:284
  476.5 5.9 collective-permute-done.27.refs_16_
  482.4 4.9 collective-permute-done.28.refs_17_
  487.3 6.6 %collective-permute-done.29.refs_18_ = bf16[256,1024]{1,0:T(8,128)(2,1)} collective-permute-done((bf16[256,1024]{1,0:T(8,128)(2,1)}, bf16[256,1024]{1,0:T(8,128)(2,1)}, u32[]{:S(2)}, u32[]{:S(2)}) %collective-permute-start.29) | collective-permute-done | bytes 524320 | tf_op jit(solution)/shard_map/ppermute | solution.py:618
  498.1 3.6 convert_element_type.283
  507.8 23.9 %attn_bwd.3 = (bf16[256,1024]{1,0:T(8,128)(2,1)}, bf16[256,1024]{1,0:T(8,128)(2,1)}, bf16[256,1024]{1,0:T(8,128)(2,1)}, bf16[256,1024]{1,0:T(8,128)(2,1)}, bf16[1024,768]{1,0:T(8,128)(2,1)}, /*index=5*/f32[1,1024]{1,0:T(1,128)}) custom-call(s32[4]{0:T(128)} %add_multiply_fusion.2.starts_ref, bf16[256,1024]{1,0:T(8,128)(2,1)} %copy-done.9, ...), custom_call_target="tpu_custom_call" | custom-call | flops 18000000 | bytes 65000 | tf_op jit(solution)/shard_map/attn_bwd/pallas_call | solution.py:284
  546.1 3.8 fusion.9
  562.6 6.9 %collective-permute-done.37 = bf16[256,1024]{1,0:T(8,128)(2,1)S(1)} collective-permute-done((bf16[256,1024]{1,0:T(8,128)(2,1)S(1)}, bf16[256,1024]{1,0:T(8,128)(2,1)S(1)}, u32[]{:S(2)}, u32[]{:S(2)}) %collective-permute-start.37) | collective-permute-done | bytes 524320 | tf_op jit(solution)/shard_map/ppermute | solution.py:618
  572.3 3.9 collective-permute-done.38
  576.2 4.6 collective-permute-done.40
  580.8 6.7 %collective-permute-done.41 = bf16[256,1024]{1,0:T(8,128)(2,1)S(1)} collective-permute-done((bf16[256,1024]{1,0:T(8,128)(2,1)S(1)}, bf16[256,1024]{1,0:T(8,128)(2,1)S(1)}, u32[]{:S(2)}, u32[]{:S(2)}) %collective-permute-start.41) | collective-permute-done | bytes 524320 | tf_op jit(solution)/shard_map/ppermute | solution.py:618
  (326 shorter events, 152.4 us)
Async XLA Ops:
  7.2 31.8 %all-gather.5.cloned.1.call-start = ((), (), s32[]{:S(2)}) async-start(), calls=%async_computation.4 | async-start | bytes 1769472 | tf_op jit(solution)/shard_map/all_gather | solution.py:697
  9.9 107.6 %all-gather.9.cloned.1.call-start = ((), (), s32[]{:S(2)}) async-start(), calls=%async_computation.6 | async-start | bytes 5308416 | tf_op jit(solution)/shard_map/all_gather | solution.py:697
  14.3 24.7 %collective-permute-start.1 = (bf16[256,1024]{1,0:T(8,128)(2,1)S(1)}, bf16[256,1024]{1,0:T(8,128)(2,1)}, u32[]{:S(2)}, u32[]{:S(2)}) collective-permute-start(bf16[256,1024]{1,0:T(8,128)(2,1)S(1)} %get-tuple-element.367.refs_0_), channel_id=1, source_target_pairs={{0,16},{8,24},{16,0},{24,8},{1,17},{9,25},{17,1},{25,9},{2,18},{10... | collective-permute-start | bytes 1572872 | tf_op jit(solution)/shard_map/ppermute | solution.py:618
  15.8 23.2 %collective-permute-start.2 = (bf16[256,1024]{1,0:T(8,128)(2,1)S(1)}, bf16[256,1024]{1,0:T(8,128)(2,1)}, u32[]{:S(2)}, u32[]{:S(2)}) collective-permute-start(bf16[256,1024]{1,0:T(8,128)(2,1)S(1)} %get-tuple-element.367.refs_0_), channel_id=1, source_target_pairs={{0,24},{8,16},{16,8},{24,0},{1,25},{9,17},{17,9},{25,1},{2,26},{10... | collective-permute-start | bytes 1572872 | tf_op jit(solution)/shard_map/ppermute | solution.py:618
  39.1 131.0 %all-gather.11.cloned.1.call-start = ((), (), s32[]{:S(2)}) async-start(), calls=%async_computation.7 | async-start | bytes 4718592 | tf_op jit(solution)/shard_map/all_gather | solution.py:697
  40.6 24.4 %collective-permute-start.4 = (bf16[256,1024]{1,0:T(8,128)(2,1)S(1)}, bf16[256,1024]{1,0:T(8,128)(2,1)S(1)}, u32[]{:S(2)}, u32[]{:S(2)}) collective-permute-start(bf16[256,1024]{1,0:T(8,128)(2,1)S(1)} %get-tuple-element.168.refs_0_), channel_id=1, source_target_pairs={{0,16},{8,24},{16,0},{24,8},{1,17},{9,25},{17,1},{25,9},{2,18},{10... | collective-permute-start | bytes 1572872 | tf_op jit(solution)/shard_map/ppermute | solution.py:618
  41.4 23.6 %collective-permute-start.5 = (bf16[256,1024]{1,0:T(8,128)(2,1)S(1)}, bf16[256,1024]{1,0:T(8,128)(2,1)S(1)}, u32[]{:S(2)}, u32[]{:S(2)}) collective-permute-start(bf16[256,1024]{1,0:T(8,128)(2,1)S(1)} %get-tuple-element.168.refs_0_), channel_id=1, source_target_pairs={{0,24},{8,16},{16,8},{24,0},{1,25},{9,17},{17,9},{25,1},{2,26},{10... | collective-permute-start | bytes 1572872 | tf_op jit(solution)/shard_map/ppermute | solution.py:618
  67.2 36.8 %collective-permute-start.7 = (bf16[256,1024]{1,0:T(8,128)(2,1)}, bf16[256,1024]{1,0:T(8,128)(2,1)S(1)}, u32[]{:S(2)}, u32[]{:S(2)}) collective-permute-start(bf16[256,1024]{1,0:T(8,128)(2,1)} %get-tuple-element.165), channel_id=1, source_target_pairs={{0,16},{8,24},{16,0},{24,8},{1,17},{9,25},{17,1},{25,9},{2,18},{10... | collective-permute-start | bytes 1572872 | tf_op jit(solution)/shard_map/ppermute | solution.py:618
  68.1 35.9 %collective-permute-start.8 = (bf16[256,1024]{1,0:T(8,128)(2,1)}, bf16[256,1024]{1,0:T(8,128)(2,1)S(1)}, u32[]{:S(2)}, u32[]{:S(2)}) collective-permute-start(bf16[256,1024]{1,0:T(8,128)(2,1)} %get-tuple-element.166), channel_id=1, source_target_pairs={{0,24},{8,16},{16,8},{24,0},{1,25},{9,17},{17,9},{25,1},{2,26},{10... | collective-permute-start | bytes 1572872 | tf_op jit(solution)/shard_map/ppermute | solution.py:618
  84.2 29.9 %collective-permute-start.10 = (bf16[256,1024]{1,0:T(8,128)(2,1)}, bf16[256,1024]{1,0:T(8,128)(2,1)S(1)}, u32[]{:S(2)}, u32[]{:S(2)}) collective-permute-start(bf16[256,1024]{1,0:T(8,128)(2,1)} %get-tuple-element.174), channel_id=1, source_target_pairs={{0,16},{8,24},{16,0},{24,8},{1,17},{9,25},{17,1},{25,9},{2,18},{10... | collective-permute-start | bytes 1572872 | tf_op jit(solution)/shard_map/ppermute | solution.py:618
  85.6 28.5 %collective-permute-start.11 = (bf16[256,1024]{1,0:T(8,128)(2,1)}, bf16[256,1024]{1,0:T(8,128)(2,1)S(1)}, u32[]{:S(2)}, u32[]{:S(2)}) collective-permute-start(bf16[256,1024]{1,0:T(8,128)(2,1)} %get-tuple-element.175), channel_id=1, source_target_pairs={{0,24},{8,16},{16,8},{24,0},{1,25},{9,17},{17,9},{25,1},{2,26},{10... | collective-permute-start | bytes 1572872 | tf_op jit(solution)/shard_map/ppermute | solution.py:618
  86.8 27.3 %collective-permute-start.9 = (bf16[256,1024]{1,0:T(8,128)(2,1)}, bf16[256,1024]{1,0:T(8,128)(2,1)S(1)}, u32[]{:S(2)}, u32[]{:S(2)}) collective-permute-start(bf16[256,1024]{1,0:T(8,128)(2,1)} %get-tuple-element.173), channel_id=1, source_target_pairs={{0,8},{8,0},{16,24},{24,16},{1,9},{9,1},{17,25},{25,17},{2,10},{10... | collective-permute-start | bytes 1572872 | tf_op jit(solution)/shard_map/ppermute | solution.py:618
  117.5 185.1 %all-gather.7.cloned.1.call-start = ((), (), s32[]{:S(2)}) async-start(), calls=%async_computation.5 | async-start | bytes 10027008 | tf_op jit(solution)/shard_map/all_gather | solution.py:697
  121.4 35.3 %collective-permute-start.12 = (bf16[2,384,1024]{2,1,0:T(8,128)(2,1)S(1)}, bf16[2,384,1024]{2,1,0:T(8,128)(2,1)S(1)}, u32[]{:S(2)}, u32[]{:S(2)}) collective-permute-start(bf16[2,384,1024]{2,1,0:T(8,128)(2,1)S(1)} %get-tuple-element.191.refs_0_), channel_id=1, source_target_pairs={{0,8},{8,0},{16,24},{24,16},{1,9},{9,1},{17,25},{25,17},{2,10},{10... | collective-permute-start | bytes 4718600 | tf_op jit(solution)/shard_map/ppermute | solution.py:618
  122.5 35.3 %collective-permute-start.13 = (bf16[2,384,1024]{2,1,0:T(8,128)(2,1)S(1)}, bf16[2,384,1024]{2,1,0:T(8,128)(2,1)S(1)}, u32[]{:S(2)}, u32[]{:S(2)}) collective-permute-start(bf16[2,384,1024]{2,1,0:T(8,128)(2,1)S(1)} %get-tuple-element.191.refs_0_), channel_id=1, source_target_pairs={{0,16},{8,24},{16,0},{24,8},{1,17},{9,25},{17,1},{25,9},{2,18},{10... | collective-permute-start | bytes 4718600 | tf_op jit(solution)/shard_map/ppermute | solution.py:618
  160.1 243.2 %reduce-scatter.7.cloned.1.call-start = ((), (), s32[]{:S(2)}) async-start(), calls=%async_computation.9 | async-start | bytes 10027008 | tf_op jit(solution)/shard_map/reduce_scatter | solution.py:701
  160.5 79.6 %collective-permute-start.16 = (bf16[2,384,1024]{2,1,0:T(8,128)(2,1)}, bf16[2,384,1024]{2,1,0:T(8,128)(2,1)}, u32[]{:S(2)}, u32[]{:S(2)}) collective-permute-start(bf16[2,384,1024]{2,1,0:T(8,128)(2,1)} %get-tuple-element.198.refs_0_), channel_id=1, source_target_pairs={{0,8},{8,0},{16,24},{24,16},{1,9},{9,1},{17,25},{25,17},{2,10},{10... | collective-permute-start | bytes 4718600 | tf_op jit(solution)/shard_map/ppermute | solution.py:618
  161.2 79.0 %collective-permute-start.17 = (bf16[2,384,1024]{2,1,0:T(8,128)(2,1)}, bf16[2,384,1024]{2,1,0:T(8,128)(2,1)}, u32[]{:S(2)}, u32[]{:S(2)}) collective-permute-start(bf16[2,384,1024]{2,1,0:T(8,128)(2,1)} %get-tuple-element.198.refs_0_), channel_id=1, source_target_pairs={{0,16},{8,24},{16,0},{24,8},{1,17},{9,25},{17,1},{25,9},{2,18},{10... | collective-permute-start | bytes 4718600 | tf_op jit(solution)/shard_map/ppermute | solution.py:618
  165.5 46.7 %collective-permute-start.14 = (bf16[1,384,1024]{2,1,0:T(8,128)(2,1)}, bf16[1,384,1024]{2,1,0:T(8,128)(2,1)}, u32[]{:S(2)}, u32[]{:S(2)}) collective-permute-start(bf16[1,384,1024]{2,1,0:T(8,128)(2,1)} %slice.224), channel_id=1, source_target_pairs={{0,8},{8,0},{16,24},{24,16},{1,9},{9,1},{17,25},{25,17},{2,10},{10... | collective-permute-start | bytes 2359304 | tf_op jit(solution)/shard_map/ppermute | solution.py:618
  166.1 46.2 %collective-permute-start.15 = (bf16[1,384,1024]{2,1,0:T(8,128)(2,1)}, bf16[1,384,1024]{2,1,0:T(8,128)(2,1)}, u32[]{:S(2)}, u32[]{:S(2)}) collective-permute-start(bf16[1,384,1024]{2,1,0:T(8,128)(2,1)} %slice.225), channel_id=1, source_target_pairs={{0,16},{8,24},{16,0},{24,8},{1,17},{9,25},{17,1},{25,9},{2,18},{10... | collective-permute-start | bytes 2359304 | tf_op jit(solution)/shard_map/ppermute | solution.py:618
  302.5 163.3 %reduce-scatter.5.cloned.1.call-start = ((), (), s32[]{:S(2)}) async-start(), calls=%async_computation.8 | async-start | bytes 5308416 | tf_op jit(solution)/shard_map/reduce_scatter | solution.py:701
  347.7 32.5 %collective-permute-start.20 = (bf16[2,384,1024]{2,1,0:T(8,128)(2,1)}, bf16[2,384,1024]{2,1,0:T(8,128)(2,1)}, u32[]{:S(2)}, u32[]{:S(2)}) collective-permute-start(bf16[2,384,1024]{2,1,0:T(8,128)(2,1)} %get-tuple-element.221), channel_id=1, source_target_pairs={{0,8},{8,0},{16,24},{24,16},{1,9},{9,1},{17,25},{25,17},{2,10},{10... | collective-permute-start | bytes 4718600 | tf_op jit(solution)/shard_map/ppermute | solution.py:618
  348.3 32.4 %collective-permute-start.21 = (bf16[2,384,1024]{2,1,0:T(8,128)(2,1)}, bf16[2,384,1024]{2,1,0:T(8,128)(2,1)}, u32[]{:S(2)}, u32[]{:S(2)}) collective-permute-start(bf16[2,384,1024]{2,1,0:T(8,128)(2,1)} %get-tuple-element.222), channel_id=1, source_target_pairs={{0,16},{8,24},{16,0},{24,8},{1,17},{9,25},{17,1},{25,9},{2,18},{10... | collective-permute-start | bytes 4718600 | tf_op jit(solution)/shard_map/ppermute | solution.py:618
  389.9 141.9 %reduce-scatter.9.cloned.1.call-start = ((), (), s32[]{:S(2)}) async-start(), calls=%async_computation.10 | async-start | bytes 4718592 | tf_op jit(solution)/shard_map/reduce_scatter | solution.py:701
  398.7 192.9 %reduce-scatter.11.cloned.1.call-start = ((), (), s32[]{:S(2)}) async-start(), calls=%async_computation.11 | async-start | bytes 1880064 | tf_op jit(solution)/shard_map/reduce_scatter | solution.py:701
  430.8 35.1 %collective-permute-start.25 = (bf16[2,384,1024]{2,1,0:T(8,128)(2,1)}, bf16[2,384,1024]{2,1,0:T(8,128)(2,1)}, u32[]{:S(2)}, u32[]{:S(2)}) collective-permute-start(bf16[2,384,1024]{2,1,0:T(8,128)(2,1)} %get-tuple-element.243), channel_id=1, source_target_pairs={{0,8},{8,0},{16,24},{24,16},{1,9},{9,1},{17,25},{25,17},{2,10},{10... | collective-permute-start | bytes 4718600 | tf_op jit(solution)/shard_map/ppermute | solution.py:618
  432.6 33.3 %collective-permute-start.26 = (bf16[2,384,1024]{2,1,0:T(8,128)(2,1)}, bf16[2,384,1024]{2,1,0:T(8,128)(2,1)}, u32[]{:S(2)}, u32[]{:S(2)}) collective-permute-start(bf16[2,384,1024]{2,1,0:T(8,128)(2,1)} %get-tuple-element.244), channel_id=1, source_target_pairs={{0,16},{8,24},{16,0},{24,8},{1,17},{9,25},{17,1},{25,9},{2,18},{10... | collective-permute-start | bytes 4718600 | tf_op jit(solution)/shard_map/ppermute | solution.py:618
  493.8 37.9 %collective-permute-start.30 = (bf16[1,384,1024]{2,1,0:T(8,128)(2,1)}, bf16[1,384,1024]{2,1,0:T(8,128)(2,1)}, u32[]{:S(2)}, u32[]{:S(2)}) collective-permute-start(bf16[1,384,1024]{2,1,0:T(8,128)(2,1)} %add_convert_fusion.4), channel_id=1, source_target_pairs={{0,16},{8,24},{16,0},{24,8},{1,17},{9,25},{17,1},{25,9},{2,18},{10... | collective-permute-start | bytes 2359304 | tf_op jit(solution)/shard_map/ppermute | solution.py:618
  494.6 37.2 %collective-permute-start.31 = (bf16[1,384,1024]{2,1,0:T(8,128)(2,1)}, bf16[1,384,1024]{2,1,0:T(8,128)(2,1)}, u32[]{:S(2)}, u32[]{:S(2)}) collective-permute-start(bf16[1,384,1024]{2,1,0:T(8,128)(2,1)} %add_convert_fusion.3), channel_id=1, source_target_pairs={{0,8},{8,0},{16,24},{24,16},{1,9},{9,1},{17,25},{25,17},{2,10},{10... | collective-permute-start | bytes 2359304 | tf_op jit(solution)/shard_map/ppermute | solution.py:618
  506.4 39.7 %collective-permute-start.32 = (bf16[1,384,1024]{2,1,0:T(8,128)(2,1)}, bf16[1,384,1024]{2,1,0:T(8,128)(2,1)}, u32[]{:S(2)}, u32[]{:S(2)}) collective-permute-start(bf16[1,384,1024]{2,1,0:T(8,128)(2,1)} %add_convert_fusion.2), channel_id=1, source_target_pairs={{0,16},{8,24},{16,0},{24,8},{1,17},{9,25},{17,1},{25,9},{2,18},{10... | collective-permute-start | bytes 2359304 | tf_op jit(solution)/shard_map/ppermute | solution.py:618
  506.4 39.7 %collective-permute-start.33 = (bf16[1,384,1024]{2,1,0:T(8,128)(2,1)}, bf16[1,384,1024]{2,1,0:T(8,128)(2,1)}, u32[]{:S(2)}, u32[]{:S(2)}) collective-permute-start(bf16[1,384,1024]{2,1,0:T(8,128)(2,1)} %add_convert_fusion.1), channel_id=1, source_target_pairs={{0,8},{8,0},{16,24},{24,16},{1,9},{9,1},{17,25},{25,17},{2,10},{10... | collective-permute-start | bytes 2359304 | tf_op jit(solution)/shard_map/ppermute | solution.py:618
  559.8 27.6 %collective-permute-start.41 = (bf16[256,1024]{1,0:T(8,128)(2,1)S(1)}, bf16[256,1024]{1,0:T(8,128)(2,1)S(1)}, u32[]{:S(2)}, u32[]{:S(2)}) collective-permute-start(bf16[256,1024]{1,0:T(8,128)(2,1)S(1)} %copy-done.64), channel_id=1, source_target_pairs={{0,16},{8,24},{16,0},{24,8},{1,17},{9,25},{17,1},{25,9},{2,18},{10... | collective-permute-start | bytes 1572872 | tf_op jit(solution)/shard_map/ppermute | solution.py:618
  (86 other events, 988.4 us)
Sparse Core Ops, SparseCore 0:
  10.2 27.7 all-gather.4
  40.2 50.7 all-gather.8
  117.6 44.3 all-gather.10
  163.6 85.1 all-gather.6
  302.7 93.8 reduce-scatter.6
  398.7 53.3 reduce-scatter.4
  455.0 48.3 reduce-scatter.8
  546.2 35.3 reduce-scatter.10

commit v6 on v5

--- a/solution.py
+++ b/solution.py
@@ -470,7 +470,11 @@
         dh_sc[rows, FF:] = grad_up.astype(bf16)
         dx_ref[0, rows, :] = dot_nt(dh_sc[rows, :], wgu_ref[...]).astype(bf16)
 
-    for_blocks(total // chunk, chunk_step)
+    def loop_step(index, carry):
+        chunk_step(index)
+        return carry
+
+    lax.fori_loop(0, total // chunk, loop_step, 0)
 
     def put_grad(kind, lead, gate_up, down):
         ref = grad_refs[kind]
@@ -666,12 +670,27 @@
     return [lax.psum_scatter(grads[0], "tp", scatter_dimension=0)]
 
 
+def far_sums_body(came_x, kept_y, came_y, kept_x, first, second):
+    first[...] = (came_x[...].astype(f32) + kept_y[...].astype(f32)).astype(bf16)
+    second[...] = (came_y[...].astype(f32) + kept_x[...].astype(f32)).astype(bf16)
+
+
 def far_sums(near):
     if square():
         came_x, came_y, _, _, _, kept_y, kept_x = near
-        first = came_x[1:].astype(f32) + kept_y.astype(f32)
-        second = came_y[1:].astype(f32) + kept_x.astype(f32)
-        return [first.astype(bf16), second.astype(bf16)]
+        block = (1, LANES, MODEL_WIDTH)
+        second = pl.BlockSpec(block, lambda s: (1, s, 0))
+        only = pl.BlockSpec(block, lambda s: (0, s, 0))
+        return pl.pallas_call(
+            far_sums_body,
+            grid=(kept_y.shape[1] // LANES,),
+            in_specs=[second, only, second, only],
+            out_specs=[only, only],
+            out_shape=(jax.ShapeDtypeStruct(kept_y.shape, bf16),) * 2,
+            compiler_params=row_params,
+            cost_estimate=cost(0.1, 5.0),
+            name="far_sums",
+        )(came_x, kept_y, came_y, kept_x)
     return []
 
 
@@ -681,16 +700,39 @@
     return []
 
 
-def add_far(near, far):
+def weight_sums_body(*refs, gu_rows):
+    halves, (gate_up_ref, down_ref) = refs[:-2], refs[-2:]
+    cut = FF * gu_rows // MODEL_WIDTH
+    expert = 0
+    for at in range(0, len(halves), 5):
+        came_x, came_y, own, far_first, far_second = halves[at : at + 5]
+        for near, mine, far in ((came_x, 0, far_first), (came_y, 1, far_second)):
+            total = near[0].astype(f32) + own[mine].astype(f32) + far[0].astype(f32)
+            gate_up_ref[expert] = total[:gu_rows]
+            for k in range(MODEL_WIDTH // gu_rows):
+                down_ref[expert, k * cut : (k + 1) * cut, :] = total[
+                    gu_rows:, k * gu_rows : (k + 1) * gu_rows
+                ]
+            expert += 1
+
+
+def weight_sums(halves, gu_rows):
     if square():
-        came_x, came_y, own = [value.astype(f32) for value in near[:3]]
-        return jnp.concatenate(
-            [
-                came_x[:1] + own[:1] + far[0].astype(f32),
-                came_y[:1] + own[1:] + far[1].astype(f32),
-            ]
-        )
-    return near[0].astype(f32)
+        arrays = [array for near, far in halves for array in (*near[:3], *far)]
+        experts = 2 * len(halves)
+        return pl.pallas_call(
+            functools.partial(weight_sums_body, gu_rows=gu_rows),
+            out_shape=(
+                jax.ShapeDtypeStruct((experts, gu_rows, 2 * FF), f32),
+                jax.ShapeDtypeStruct((experts, FF, gu_rows), f32),
+            ),
+            compiler_params=params,
+            cost_estimate=cost(0.1, 5.0),
+            name="weight_sums",
+        )(*arrays)
+    return unpack_weights(
+        jnp.concatenate([near[0].astype(f32) for near, _ in halves]), gu_rows
+    )
 
 
 def ag_ep(value, axis=0):
@@ -817,7 +859,6 @@
             full.append([ag_ep(jnp.concatenate([normed_two, cotangent[m], masks[m]], axis=-1))])
 
     pieces = [gather_weights_far(near[0])]
-    near.append(gather_weights_near(after(packed_weights[1], near[0])))
     old = [(), ()]
     mixes = []
     grads = []
@@ -825,6 +866,8 @@
     for m in range(micro):
         sources = after(full[m], ready) if m else full[m]
         xd, gd, pt, pgt = dispatch(offset, sources, router, local)
+        if m == 0:
+            near.append(gather_weights_near(after(packed_weights[1], pieces[0], xd)))
         merged = (local, ep_size * CAP, MODEL_WIDTH)
         xd = xd.reshape(merged)
         gd = gd.reshape(merged)
@@ -950,8 +993,8 @@
     outputs = [
         (hiddens[m] + residual_scale * mixes[m].astype(f32)).astype(bf16) for m in range(micro)
     ]
-    grad_gate_up, grad_down = unpack_weights(
-        jnp.concatenate([add_far(near_first, far_first), add_far(near_second, far_second)]), w_gate_up.shape[1]
+    grad_gate_up, grad_down = weight_sums(
+        [(near_first, far_first), (near_second, far_second)], w_gate_up.shape[1]
     )
     split = local_heads * GROUP_COLS
     grad_qkv = summed[:own_rows, :split].reshape(own_rows, local_heads, GROUP_COLS)

time: 611 us -> 582 us (0.953)
  waiting for transfers between devices: 177 us -> 152 us
  other arithmetic: 65.3 us -> 43.6 us
  Pallas kernels: 254 us -> 274 us
    ppermute x43, waiting for transfers between devices: 177 us -> 151 us  [flip(): return lax.ppermute(value, 'tp', [(t, t ^ bits) for t in range(4)])]
    convert_element_type x6 -> x0, other arithmetic: 16.6 us -> none  [the longest x4 9.53 us: far_sums(): return [first.astype(bf16), second.astype(bf16)]]
    pallas_call x0 -> x3, Pallas kernels: none -> 16.1 us  [the longest x1 8.29 us: weight_sums(): pl.pallas_call(functools.partial(weight_sums_body, gu_rows=gu_rows), out_...]
    add x2 -> x0, other arithmetic: 6.57 us -> none  [add_far(): came_x[:1] + own[:1] + far[0].astype(f32)]
  transfers between devices with their start and end apart: 51 -> 51, of which waited for: 23 -> 24; matrix products, arithmetic and copies ran while one was open for 16% -> 13% of each run, Pallas kernels for 42% -> 47%
where the time goes in v6:
time: 582 us; the launch traced here: 578 us
  Pallas kernels  274 us (47%)
  waiting for transfers between devices  152 us (26%)
  starting transfers between devices  51.1 us (9%)
  other arithmetic  43.6 us (7%)
  local copies, waits for them, and re-layouts  33.2 us (6%)
  between operations  15.3 us (3%)
  matrix products  9.01 us (2%)
    ppermute x43, waiting for transfers between devices, flip(): return lax.ppermute(value, 'tp', [(t, t ^ bits) for t in range(4)])  151 us
    pallas_call x4, Pallas kernels, run_experts(): pl.pallas_call(functools.partial(experts_body, base=base, slices=slices,...  121 us
    ppermute x43, starting transfers between devices, flip(): return lax.ppermute(value, 'tp', [(t, t ^ bits) for t in range(4)])  50.1 us
    pallas_call x2, Pallas kernels, attention_backward(): pl.pallas_call(functools.partial(attention_backward_body, count=count), o...  47.3 us
    pallas_call x3, Pallas kernels, combine(): pl.pallas_call(functools.partial(body, count=count), grid=(blocks,), in_s...  31.1 us
    pallas_call x2, Pallas kernels, dispatch(): pl.pallas_call(functools.partial(dispatch_body, local=local, count=len(so...  29.6 us
    pallas_call x2, Pallas kernels, attention_forward(): pl.pallas_call(functools.partial(attention_forward_body, count=count), ou...  29.3 us
  transfers between devices with their start and end apart: 51, of which 24 were waited for; matrix products, arithmetic and copies ran while one was open for 13% of the time, Pallas kernels for 47%

profile of v6, /device:TPU:0, one launch (start us, length us, event | category | flops | bytes accessed | tf_op | source)
XLA Modules:
  0.0 577.6 jit_solution(8101887369638191480)
XLA Ops:
  25.6 5.5 fusion.16
  31.1 7.9 %collective-permute-done.1.refs_2_ = bf16[256,1024]{1,0:T(8,128)(2,1)} collective-permute-done((bf16[256,1024]{1,0:T(8,128)(2,1)S(1)}, bf16[256,1024]{1,0:T(8,128)(2,1)}, u32[]{:S(2)}, u32[]{:S(2)}) %collective-permute-start.1) | collective-permute-done | bytes 524320 | tf_op jit(solution)/shard_map/ppermute | solution.py:622
  45.1 14.7 %attn_fwd.2 = (bf16[256,1024]{1,0:T(8,128)(2,1)}, bf16[256,1024]{1,0:T(8,128)(2,1)}, bf16[256,1024]{1,0:T(8,128)(2,1)}, bf16[256,1024]{1,0:T(8,128)(2,1)}, bf16[...) custom-call(s32[4]{0:T(128)} %add_multiply_fusion.2.starts_ref, ...), custom_call_target="tpu_custom_call" | custom-call | flops 11000000 | bytes 40000 | tf_op jit(solution)/shard_map/attn_fwd/pallas_call | solution.py:182
  59.8 5.2 collective-permute-done.4.refs_2_
  69.6 14.5 %attn_fwd.3 = (bf16[256,1024]{1,0:T(8,128)(2,1)}, bf16[256,1024]{1,0:T(8,128)(2,1)}, bf16[256,1024]{1,0:T(8,128)(2,1)}, bf16[256,1024]{1,0:T(8,128)(2,1)}, bf16[...) custom-call(s32[4]{0:T(128)} %add_multiply_fusion.2.starts_ref, ...), custom_call_target="tpu_custom_call" | custom-call | flops 11000000 | bytes 40000 | tf_op jit(solution)/shard_map/attn_fwd/pallas_call | solution.py:182
  87.7 16.3 %collective-permute-done.7 = bf16[256,1024]{1,0:T(8,128)(2,1)S(1)} collective-permute-done((bf16[256,1024]{1,0:T(8,128)(2,1)}, bf16[256,1024]{1,0:T(8,128)(2,1)S(1)}, u32[]{:S(2)}, u32[]{:S(2)}) %collective-permute-start.7) | collective-permute-done | bytes 524320 | tf_op jit(solution)/shard_map/ppermute | solution.py:622
  104.0 10.1 %collective-permute-done.10 = bf16[256,1024]{1,0:T(8,128)(2,1)S(1)} collective-permute-done((bf16[256,1024]{1,0:T(8,128)(2,1)}, bf16[256,1024]{1,0:T(8,128)(2,1)S(1)}, u32[]{:S(2)}, u32[]{:S(2)}) %collective-permute-start.10) | collective-permute-done | bytes 524320 | tf_op jit(solution)/shard_map/ppermute | solution.py:622
  123.5 33.2 %collective-permute-done.12.refs_1_ = bf16[2,384,1024]{2,1,0:T(8,128)(2,1)S(1)} collective-permute-done((bf16[2,384,1024]{2,1,0:T(8,128)(2,1)S(1)}, bf16[2,384,1024]{2,1,0:T(8,128)(2,1)S(1)}, u32[]{:S(2)}, u32[]{:S(2)}) %collective-permute-start.12) | collective-permute-done | bytes 1572896 | tf_op jit(solution)/shard_map/ppermute | solution.py:622
  167.3 14.7 %dispatch.2 = (bf16[4,8,96,1024]{3,2,1,0:T(8,128)(2,1)}, bf16[4,8,96,1024]{3,2,1,0:T(8,128)(2,1)}, bf16[2048,384]{1,0:T(8,128)(2,1)}, bf16[2048,384]{1,0:T(8,128)(2,1)}) custom-call(s32[1]{0:T(128)} %bitcast.15.offset_ref, bf16[2048,1024]{1,0:T(8,128)(2,1)} %all-gather.11.cloned.1.call-done.refs_0_, bf16[2048,1152]{1,0:T(8,128)(2,1)} %all-gather.9.cloned.1.call-done.refs_1_, ...), custom_call_target="tpu_custom_call" | custom-call | flops 11000000 | bytes 40000 | tf_op jit(solution)/shard_map/dispatch/pallas_call | solution.py:363
  184.8 28.9 %experts.4 = (bf16[2,768,1024]{2,1,0:T(8,128)(2,1)}, bf16[2,768,1024]{2,1,0:T(8,128)(2,1)}, bf16[2,768,128]{2,1,0:T(8,128)(2,1)}, bf16[2,384,1024]{2,1,0:T(8,128...) custom-call(s32[5]{0:T(128)} %concatenate.27.place_ref, ...), custom_call_target="tpu_custom_call" | custom-call | flops 20000000 | bytes 60000 | tf_op jit(solution)/shard_map/experts/pallas_call | solution.py:537
  221.0 12.6 %collective-permute-done.18.refs_3_ = bf16[1,384,1024]{2,1,0:T(8,128)(2,1)S(1)} collective-permute-done((bf16[1,384,1024]{2,1,0:T(8,128)(2,1)S(1)}, bf16[1,384,1024]{2,1,0:T(8,128)(2,1)S(1)}, u32[]{:S(2)}, u32[]{:S(2)}) %collective-permute-start.18) | collective-permute-done | bytes 786464 | tf_op jit(solution)/shard_map/ppermute | solution.py:622
  237.0 29.2 %experts.5 = (bf16[2,768,1024]{2,1,0:T(8,128)(2,1)}, bf16[2,768,1024]{2,1,0:T(8,128)(2,1)}, bf16[2,768,128]{2,1,0:T(8,128)(2,1)}, bf16[2,384,1024]{2,1,0:T(8,128...) custom-call(s32[5]{0:T(128)} %concatenate.27.place_ref, ...), custom_call_target="tpu_custom_call" | custom-call | flops 20000000 | bytes 60000 | tf_op jit(solution)/shard_map/experts/pallas_call | solution.py:537
  266.1 13.3 %combine.1 = bf16[2048,2176]{1,0:T(8,128)(2,1)} custom-call(bf16[2,8,96,1024]{3,2,1,0:T(8,128)(2,1)} %bitcast.129, bf16[2,8,96,1024]{3,2,1,0:T(8,128)(2,1)} %bitcast.131, bf16[2,8,96,1024]{3,2,1,0:T(8,128)(2,1)} %bitcast.130, bf16[2,8,96,1024]{3,2,1,0:T(8,128)(2,1)} %bitcast.132, bf16[2,8,96,128]{3,2,1,0:T(8,128)(2,1)} %bitcast.142, ...), custom_call_target="tpu_custom_call" | custom-call | flops 5000000 | bytes 17000 | tf_op jit(solution)/shard_map/combine/pallas_call | solution.py:609
  279.5 14.9 %dispatch.3 = (bf16[4,8,96,1024]{3,2,1,0:T(8,128)(2,1)}, bf16[4,8,96,1024]{3,2,1,0:T(8,128)(2,1)}, bf16[2048,384]{1,0:T(8,128)(2,1)}, bf16[2048,384]{1,0:T(8,128)(2,1)}) custom-call(s32[1]{0:T(128)} %bitcast.15.offset_ref, bf16[2048,2176]{1,0:T(8,128)(2,1)} %all-gather.7.cloned.1.call-done.refs_0_, bf16[1024,128]{1,0:T(8,128)(2,1)} %pad.8.refs_2_.refs_1_), custom_call_target="tpu_custom_call" | custom-call | flops 11000000 | bytes 40000 | tf_op jit(solution)/shard_map/dispatch/pallas_call | solution.py:363
  294.4 31.2 %experts.6 = (bf16[2,768,1024]{2,1,0:T(8,128)(2,1)}, bf16[2,768,1024]{2,1,0:T(8,128)(2,1)}, bf16[2,768,128]{2,1,0:T(8,128)(2,1)}, bf16[2,384,1024]{2,1,0:T(8,128...) custom-call(s32[5]{0:T(128)} %concatenate.27.place_ref, ...), custom_call_target="tpu_custom_call" | custom-call | flops 20000000 | bytes 60000 | tf_op jit(solution)/shard_map/experts/pallas_call | solution.py:537
  328.0 31.3 %experts.7 = (bf16[2,768,1024]{2,1,0:T(8,128)(2,1)}, bf16[2,768,1024]{2,1,0:T(8,128)(2,1)}, bf16[2,768,128]{2,1,0:T(8,128)(2,1)}, bf16[2,384,1024]{2,1,0:T(8,128...) custom-call(s32[5]{0:T(128)} %concatenate.27.place_ref, ...), custom_call_target="tpu_custom_call" | custom-call | flops 20000000 | bytes 60000 | tf_op jit(solution)/shard_map/experts/pallas_call | solution.py:537
  359.3 9.1 %combine_grad.1 = bf16[2048,1152]{1,0:T(8,128)(2,1)} custom-call(bf16[2,8,96,1024]{3,2,1,0:T(8,128)(2,1)} %bitcast.134, bf16[2,8,96,1024]{3,2,1,0:T(8,128)(2,1)} %bitcast.136, bf16[2,8,96,128]{3,2,1,0:T(8,128)(2,1)} %bitcast.138, bf16[2,8,96,128]{3,2,1,0:T(8,128)(2,1)} %bitcast.139, bf16[2048,384]{1,0:T(8,128)(2,1)} %get-tuple-element.236.refs_4_), custom_call_target="tpu_custom_call" | custom-call | flops 5000000 | bytes 17000 | tf_op jit(solution)/shard_map/combine_grad/pallas_call | solution.py:609
  368.5 8.7 %combine_mix.1 = bf16[2048,1024]{1,0:T(8,128)(2,1)} custom-call(bf16[2,8,96,1024]{3,2,1,0:T(8,128)(2,1)} %bitcast.133, bf16[2,8,96,1024]{3,2,1,0:T(8,128)(2,1)} %bitcast.135, bf16[2048,384]{1,0:T(8,128)(2,1)} %get-tuple-element.247.refs_2_), custom_call_target="tpu_custom_call" | custom-call | flops 5000000 | bytes 17000 | tf_op jit(solution)/shard_map/combine_mix/pallas_call | solution.py:609
  390.7 10.9 %collective-permute-done.22.refs_16_ = bf16[256,1024]{1,0:T(8,128)(2,1)S(1)} collective-permute-done((bf16[256,1024]{1,0:T(8,128)(2,1)S(1)}, bf16[256,1024]{1,0:T(8,128)(2,1)S(1)}, u32[]{:S(2)}, u32[]{:S(2)}) %collective-permute-start.22) | collective-permute-done | bytes 524320 | tf_op jit(solution)/shard_map/ppermute | solution.py:622
  401.6 6.6 %collective-permute-done.23.refs_17_ = bf16[256,1024]{1,0:T(8,128)(2,1)S(1)} collective-permute-done((bf16[256,1024]{1,0:T(8,128)(2,1)S(1)}, bf16[256,1024]{1,0:T(8,128)(2,1)S(1)}, u32[]{:S(2)}, u32[]{:S(2)}) %collective-permute-start.23) | collective-permute-done | bytes 524320 | tf_op jit(solution)/shard_map/ppermute | solution.py:622
  412.8 23.8 %attn_bwd.2 = (bf16[256,1024]{1,0:T(8,128)(2,1)}, bf16[256,1024]{1,0:T(8,128)(2,1)}, bf16[256,1024]{1,0:T(8,128)(2,1)}, bf16[256,1024]{1,0:T(8,128)(2,1)}, bf16[1024,768]{1,0:T(8,128)(2,1)}, /*index=5*/f32[1,1024]{1,0:T(1,128)}) custom-call(s32[4]{0:T(128)} %add_multiply_fusion.2.starts_ref, bf16[256,1024]{1,0:T(8,128)(2,1)} %copy-done.9, ...), custom_call_target="tpu_custom_call" | custom-call | flops 18000000 | bytes 65000 | tf_op jit(solution)/shard_map/attn_bwd/pallas_call | solution.py:284
  436.7 4.4 collective-permute-done.25.came_x.refs_5_
  450.1 3.8 far_sums.2
  454.0 6.2 %collective-permute-done.27.refs_16_ = bf16[256,1024]{1,0:T(8,128)(2,1)} collective-permute-done((bf16[256,1024]{1,0:T(8,128)(2,1)}, bf16[256,1024]{1,0:T(8,128)(2,1)}, u32[]{:S(2)}, u32[]{:S(2)}) %collective-permute-start.27) | collective-permute-done | bytes 524320 | tf_op jit(solution)/shard_map/ppermute | solution.py:622
  460.2 4.1 collective-permute-done.28.refs_17_
  464.3 3.5 collective-permute-done.29.refs_18_
  473.3 4.0 far_sums.3
  481.6 23.5 %attn_bwd.3 = (bf16[256,1024]{1,0:T(8,128)(2,1)}, bf16[256,1024]{1,0:T(8,128)(2,1)}, bf16[256,1024]{1,0:T(8,128)(2,1)}, bf16[256,1024]{1,0:T(8,128)(2,1)}, bf16[1024,768]{1,0:T(8,128)(2,1)}, /*index=5*/f32[1,1024]{1,0:T(1,128)}) custom-call(s32[4]{0:T(128)} %add_multiply_fusion.2.starts_ref, bf16[256,1024]{1,0:T(8,128)(2,1)} %copy-done.8, ...), custom_call_target="tpu_custom_call" | custom-call | flops 18000000 | bytes 65000 | tf_op jit(solution)/shard_map/attn_bwd/pallas_call | solution.py:284
  524.4 9.7 %collective-permute-done.37 = bf16[256,1024]{1,0:T(8,128)(2,1)S(1)} collective-permute-done((bf16[256,1024]{1,0:T(8,128)(2,1)}, bf16[256,1024]{1,0:T(8,128)(2,1)S(1)}, u32[]{:S(2)}, u32[]{:S(2)}) %collective-permute-start.37) | collective-permute-done | bytes 524320 | tf_op jit(solution)/shard_map/ppermute | solution.py:622
  536.6 8.3 %weight_sums.1 = (f32[4,256,1024]{2,1,0:T(8,128)}, f32[4,512,256]{2,1,0:T(8,128)}) custom-call(bf16[2,384,1024]{2,1,0:T(8,128)(2,1)} %collective-permute-done.20.came_x.refs_0_, bf16[2,384,1024]{2,1,0:T(8,128)(2,1)} %collective-permute-done.21.came_y.refs_1_, bf16[2,384,1024]{2,1,0:T(8,128)(2,1)} %get-tuple-element.310.refs_2_, ...), custom_call_target="tpu_custom_call" | custom-call | flops 100000 | bytes 5000 | tf_op jit(solution)/shard_map/weight_sums/pallas_call | solution.py:723
  546.2 4.8 collective-permute-done.40
  551.1 4.9 collective-permute-done.41
  (307 shorter events, 142.5 us)
Async XLA Ops:
  7.2 31.8 %all-gather.5.cloned.1.call-start = ((), (), s32[]{:S(2)}) async-start(), calls=%async_computation.4 | async-start | bytes 1769472 | tf_op jit(solution)/shard_map/all_gather | solution.py:739
  9.8 107.6 %all-gather.9.cloned.1.call-start = ((), (), s32[]{:S(2)}) async-start(), calls=%async_computation.6 | async-start | bytes 5308416 | tf_op jit(solution)/shard_map/all_gather | solution.py:739
  14.3 24.7 %collective-permute-start.1 = (bf16[256,1024]{1,0:T(8,128)(2,1)S(1)}, bf16[256,1024]{1,0:T(8,128)(2,1)}, u32[]{:S(2)}, u32[]{:S(2)}) collective-permute-start(bf16[256,1024]{1,0:T(8,128)(2,1)S(1)} %get-tuple-element.375.refs_0_), channel_id=1, source_target_pairs={{0,16},{8,24},{16,0},{24,8},{1,17},{9,25},{17,1},{25,9},{2,18},{10... | collective-permute-start | bytes 1572872 | tf_op jit(solution)/shard_map/ppermute | solution.py:622
  39.0 128.2 %all-gather.11.cloned.1.call-start = ((), (), s32[]{:S(2)}) async-start(), calls=%async_computation.7 | async-start | bytes 4718592 | tf_op jit(solution)/shard_map/all_gather | solution.py:739
  40.6 24.4 %collective-permute-start.4 = (bf16[256,1024]{1,0:T(8,128)(2,1)S(1)}, bf16[256,1024]{1,0:T(8,128)(2,1)S(1)}, u32[]{:S(2)}, u32[]{:S(2)}) collective-permute-start(bf16[256,1024]{1,0:T(8,128)(2,1)S(1)} %get-tuple-element.174.refs_0_), channel_id=1, source_target_pairs={{0,16},{8,24},{16,0},{24,8},{1,17},{9,25},{17,1},{25,9},{2,18},{10... | collective-permute-start | bytes 1572872 | tf_op jit(solution)/shard_map/ppermute | solution.py:622
  67.1 36.8 %collective-permute-start.7 = (bf16[256,1024]{1,0:T(8,128)(2,1)}, bf16[256,1024]{1,0:T(8,128)(2,1)S(1)}, u32[]{:S(2)}, u32[]{:S(2)}) collective-permute-start(bf16[256,1024]{1,0:T(8,128)(2,1)} %get-tuple-element.171), channel_id=1, source_target_pairs={{0,16},{8,24},{16,0},{24,8},{1,17},{9,25},{17,1},{25,9},{2,18},{10... | collective-permute-start | bytes 1572872 | tf_op jit(solution)/shard_map/ppermute | solution.py:622
  68.1 35.9 %collective-permute-start.8 = (bf16[256,1024]{1,0:T(8,128)(2,1)}, bf16[256,1024]{1,0:T(8,128)(2,1)S(1)}, u32[]{:S(2)}, u32[]{:S(2)}) collective-permute-start(bf16[256,1024]{1,0:T(8,128)(2,1)} %get-tuple-element.172), channel_id=1, source_target_pairs={{0,24},{8,16},{16,8},{24,0},{1,25},{9,17},{17,9},{25,1},{2,26},{10... | collective-permute-start | bytes 1572872 | tf_op jit(solution)/shard_map/ppermute | solution.py:622
  84.2 29.9 %collective-permute-start.10 = (bf16[256,1024]{1,0:T(8,128)(2,1)}, bf16[256,1024]{1,0:T(8,128)(2,1)S(1)}, u32[]{:S(2)}, u32[]{:S(2)}) collective-permute-start(bf16[256,1024]{1,0:T(8,128)(2,1)} %get-tuple-element.180), channel_id=1, source_target_pairs={{0,16},{8,24},{16,0},{24,8},{1,17},{9,25},{17,1},{25,9},{2,18},{10... | collective-permute-start | bytes 1572872 | tf_op jit(solution)/shard_map/ppermute | solution.py:622
  85.6 28.5 %collective-permute-start.11 = (bf16[256,1024]{1,0:T(8,128)(2,1)}, bf16[256,1024]{1,0:T(8,128)(2,1)S(1)}, u32[]{:S(2)}, u32[]{:S(2)}) collective-permute-start(bf16[256,1024]{1,0:T(8,128)(2,1)} %get-tuple-element.181), channel_id=1, source_target_pairs={{0,24},{8,16},{16,8},{24,0},{1,25},{9,17},{17,9},{25,1},{2,26},{10... | collective-permute-start | bytes 1572872 | tf_op jit(solution)/shard_map/ppermute | solution.py:622
  86.7 27.4 %collective-permute-start.9 = (bf16[256,1024]{1,0:T(8,128)(2,1)}, bf16[256,1024]{1,0:T(8,128)(2,1)S(1)}, u32[]{:S(2)}, u32[]{:S(2)}) collective-permute-start(bf16[256,1024]{1,0:T(8,128)(2,1)} %get-tuple-element.179), channel_id=1, source_target_pairs={{0,8},{8,0},{16,24},{24,16},{1,9},{9,1},{17,25},{25,17},{2,10},{10... | collective-permute-start | bytes 1572872 | tf_op jit(solution)/shard_map/ppermute | solution.py:622
  117.5 162.0 %all-gather.7.cloned.1.call-start = ((), (), s32[]{:S(2)}) async-start(), calls=%async_computation.5 | async-start | bytes 10027008 | tf_op jit(solution)/shard_map/all_gather | solution.py:739
  121.4 35.3 %collective-permute-start.12 = (bf16[2,384,1024]{2,1,0:T(8,128)(2,1)S(1)}, bf16[2,384,1024]{2,1,0:T(8,128)(2,1)S(1)}, u32[]{:S(2)}, u32[]{:S(2)}) collective-permute-start(bf16[2,384,1024]{2,1,0:T(8,128)(2,1)S(1)} %get-tuple-element.197.refs_0_), channel_id=1, source_target_pairs={{0,8},{8,0},{16,24},{24,16},{1,9},{9,1},{17,25},{25,17},{2,10},{10... | collective-permute-start | bytes 4718600 | tf_op jit(solution)/shard_map/ppermute | solution.py:622
  122.5 35.3 %collective-permute-start.13 = (bf16[2,384,1024]{2,1,0:T(8,128)(2,1)S(1)}, bf16[2,384,1024]{2,1,0:T(8,128)(2,1)S(1)}, u32[]{:S(2)}, u32[]{:S(2)}) collective-permute-start(bf16[2,384,1024]{2,1,0:T(8,128)(2,1)S(1)} %get-tuple-element.197.refs_0_), channel_id=1, source_target_pairs={{0,16},{8,24},{16,0},{24,8},{1,17},{9,25},{17,1},{25,9},{2,18},{10... | collective-permute-start | bytes 4718600 | tf_op jit(solution)/shard_map/ppermute | solution.py:622
  160.1 221.9 %reduce-scatter.7.cloned.1.call-start = ((), (), s32[]{:S(2)}) async-start(), calls=%async_computation.9 | async-start | bytes 10027008 | tf_op jit(solution)/shard_map/reduce_scatter | solution.py:743
  182.0 34.2 %collective-permute-start.16 = (bf16[2,384,1024]{2,1,0:T(8,128)(2,1)}, bf16[2,384,1024]{2,1,0:T(8,128)(2,1)}, u32[]{:S(2)}, u32[]{:S(2)}) collective-permute-start(bf16[2,384,1024]{2,1,0:T(8,128)(2,1)} %get-tuple-element.204.refs_0_), channel_id=1, source_target_pairs={{0,8},{8,0},{16,24},{24,16},{1,9},{9,1},{17,25},{25,17},{2,10},{10... | collective-permute-start | bytes 4718600 | tf_op jit(solution)/shard_map/ppermute | solution.py:622
  183.3 33.4 %collective-permute-start.17 = (bf16[2,384,1024]{2,1,0:T(8,128)(2,1)}, bf16[2,384,1024]{2,1,0:T(8,128)(2,1)}, u32[]{:S(2)}, u32[]{:S(2)}) collective-permute-start(bf16[2,384,1024]{2,1,0:T(8,128)(2,1)} %get-tuple-element.204.refs_0_), channel_id=1, source_target_pairs={{0,16},{8,24},{16,0},{24,8},{1,17},{9,25},{17,1},{25,9},{2,18},{10... | collective-permute-start | bytes 4718600 | tf_op jit(solution)/shard_map/ppermute | solution.py:622
  279.4 157.3 %reduce-scatter.5.cloned.1.call-start = ((), (), s32[]{:S(2)}) async-start(), calls=%async_computation.8 | async-start | bytes 5308416 | tf_op jit(solution)/shard_map/reduce_scatter | solution.py:743
  325.6 33.7 %collective-permute-start.20 = (bf16[2,384,1024]{2,1,0:T(8,128)(2,1)}, bf16[2,384,1024]{2,1,0:T(8,128)(2,1)}, u32[]{:S(2)}, u32[]{:S(2)}) collective-permute-start(bf16[2,384,1024]{2,1,0:T(8,128)(2,1)} %get-tuple-element.227), channel_id=1, source_target_pairs={{0,8},{8,0},{16,24},{24,16},{1,9},{9,1},{17,25},{25,17},{2,10},{10... | collective-permute-start | bytes 4718600 | tf_op jit(solution)/shard_map/ppermute | solution.py:622
  326.2 33.1 %collective-permute-start.21 = (bf16[2,384,1024]{2,1,0:T(8,128)(2,1)}, bf16[2,384,1024]{2,1,0:T(8,128)(2,1)}, u32[]{:S(2)}, u32[]{:S(2)}) collective-permute-start(bf16[2,384,1024]{2,1,0:T(8,128)(2,1)} %get-tuple-element.228), channel_id=1, source_target_pairs={{0,16},{8,24},{16,0},{24,8},{1,17},{9,25},{17,1},{25,9},{2,18},{10... | collective-permute-start | bytes 4718600 | tf_op jit(solution)/shard_map/ppermute | solution.py:622
  368.5 136.6 %reduce-scatter.9.cloned.1.call-start = ((), (), s32[]{:S(2)}) async-start(), calls=%async_computation.10 | async-start | bytes 4718592 | tf_op jit(solution)/shard_map/reduce_scatter | solution.py:743
  377.3 187.7 %reduce-scatter.11.cloned.1.call-start = ((), (), s32[]{:S(2)}) async-start(), calls=%async_computation.11 | async-start | bytes 1880064 | tf_op jit(solution)/shard_map/reduce_scatter | solution.py:743
  408.9 32.2 %collective-permute-start.25 = (bf16[2,384,1024]{2,1,0:T(8,128)(2,1)}, bf16[2,384,1024]{2,1,0:T(8,128)(2,1)}, u32[]{:S(2)}, u32[]{:S(2)}) collective-permute-start(bf16[2,384,1024]{2,1,0:T(8,128)(2,1)} %get-tuple-element.249), channel_id=1, source_target_pairs={{0,8},{8,0},{16,24},{24,16},{1,9},{9,1},{17,25},{25,17},{2,10},{10... | collective-permute-start | bytes 4718600 | tf_op jit(solution)/shard_map/ppermute | solution.py:622
  410.3 31.2 %collective-permute-start.26 = (bf16[2,384,1024]{2,1,0:T(8,128)(2,1)}, bf16[2,384,1024]{2,1,0:T(8,128)(2,1)}, u32[]{:S(2)}, u32[]{:S(2)}) collective-permute-start(bf16[2,384,1024]{2,1,0:T(8,128)(2,1)} %get-tuple-element.250), channel_id=1, source_target_pairs={{0,16},{8,24},{16,0},{24,8},{1,17},{9,25},{17,1},{25,9},{2,18},{10... | collective-permute-start | bytes 4718600 | tf_op jit(solution)/shard_map/ppermute | solution.py:622
  467.8 37.2 %collective-permute-start.30 = (bf16[1,384,1024]{2,1,0:T(8,128)(2,1)}, bf16[1,384,1024]{2,1,0:T(8,128)(2,1)}, u32[]{:S(2)}, u32[]{:S(2)}) collective-permute-start(bf16[1,384,1024]{2,1,0:T(8,128)(2,1)} %get-tuple-element.276), channel_id=1, source_target_pairs={{0,16},{8,24},{16,0},{24,8},{1,17},{9,25},{17,1},{25,9},{2,18},{10... | collective-permute-start | bytes 2359304 | tf_op jit(solution)/shard_map/ppermute | solution.py:622
  469.7 35.4 %collective-permute-start.31 = (bf16[1,384,1024]{2,1,0:T(8,128)(2,1)}, bf16[1,384,1024]{2,1,0:T(8,128)(2,1)}, u32[]{:S(2)}, u32[]{:S(2)}) collective-permute-start(bf16[1,384,1024]{2,1,0:T(8,128)(2,1)} %get-tuple-element.277), channel_id=1, source_target_pairs={{0,8},{8,0},{16,24},{24,16},{1,9},{9,1},{17,25},{25,17},{2,10},{10... | collective-permute-start | bytes 2359304 | tf_op jit(solution)/shard_map/ppermute | solution.py:622
  479.8 41.0 %collective-permute-start.32 = (bf16[1,384,1024]{2,1,0:T(8,128)(2,1)}, bf16[1,384,1024]{2,1,0:T(8,128)(2,1)}, u32[]{:S(2)}, u32[]{:S(2)}) collective-permute-start(bf16[1,384,1024]{2,1,0:T(8,128)(2,1)} %get-tuple-element.288), channel_id=1, source_target_pairs={{0,16},{8,24},{16,0},{24,8},{1,17},{9,25},{17,1},{25,9},{2,18},{10... | collective-permute-start | bytes 2359304 | tf_op jit(solution)/shard_map/ppermute | solution.py:622
  481.0 39.7 %collective-permute-start.33 = (bf16[1,384,1024]{2,1,0:T(8,128)(2,1)}, bf16[1,384,1024]{2,1,0:T(8,128)(2,1)}, u32[]{:S(2)}, u32[]{:S(2)}) collective-permute-start(bf16[1,384,1024]{2,1,0:T(8,128)(2,1)} %get-tuple-element.289), channel_id=1, source_target_pairs={{0,8},{8,0},{16,24},{24,16},{1,9},{9,1},{17,25},{25,17},{2,10},{10... | collective-permute-start | bytes 2359304 | tf_op jit(solution)/shard_map/ppermute | solution.py:622
  520.8 25.4 %collective-permute-start.38 = (bf16[256,1024]{1,0:T(8,128)(2,1)}, bf16[256,1024]{1,0:T(8,128)(2,1)}, u32[]{:S(2)}, u32[]{:S(2)}) collective-permute-start(bf16[256,1024]{1,0:T(8,128)(2,1)} %get-tuple-element.300), channel_id=1, source_target_pairs={{0,16},{8,24},{16,0},{24,8},{1,17},{9,25},{17,1},{25,9},{2,18},{10... | collective-permute-start | bytes 1572872 | tf_op jit(solution)/shard_map/ppermute | solution.py:622
  520.9 25.3 %collective-permute-start.39 = (bf16[256,1024]{1,0:T(8,128)(2,1)}, bf16[256,1024]{1,0:T(8,128)(2,1)}, u32[]{:S(2)}, u32[]{:S(2)}) collective-permute-start(bf16[256,1024]{1,0:T(8,128)(2,1)} %get-tuple-element.301), channel_id=1, source_target_pairs={{0,24},{8,16},{16,8},{24,0},{1,25},{9,17},{17,9},{25,1},{2,26},{10... | collective-permute-start | bytes 1572872 | tf_op jit(solution)/shard_map/ppermute | solution.py:622
  522.6 28.5 %collective-permute-start.40 = (bf16[256,1024]{1,0:T(8,128)(2,1)}, bf16[256,1024]{1,0:T(8,128)(2,1)}, u32[]{:S(2)}, u32[]{:S(2)}) collective-permute-start(bf16[256,1024]{1,0:T(8,128)(2,1)} %get-tuple-element.307), channel_id=1, source_target_pairs={{0,8},{8,0},{16,24},{24,16},{1,9},{9,1},{17,25},{25,17},{2,10},{10... | collective-permute-start | bytes 1572872 | tf_op jit(solution)/shard_map/ppermute | solution.py:622
  524.2 31.8 %collective-permute-start.41 = (bf16[256,1024]{1,0:T(8,128)(2,1)}, bf16[256,1024]{1,0:T(8,128)(2,1)}, u32[]{:S(2)}, u32[]{:S(2)}) collective-permute-start(bf16[256,1024]{1,0:T(8,128)(2,1)} %get-tuple-element.308), channel_id=1, source_target_pairs={{0,16},{8,24},{16,0},{24,8},{1,17},{9,25},{17,1},{25,9},{2,18},{10... | collective-permute-start | bytes 1572872 | tf_op jit(solution)/shard_map/ppermute | solution.py:622
  534.1 23.8 %collective-permute-start.42 = (bf16[256,1024]{1,0:T(8,128)(2,1)}, bf16[256,1024]{1,0:T(8,128)(2,1)}, u32[]{:S(2)}, u32[]{:S(2)}) collective-permute-start(bf16[256,1024]{1,0:T(8,128)(2,1)} %get-tuple-element.309), channel_id=1, source_target_pairs={{0,24},{8,16},{16,8},{24,0},{1,25},{9,17},{17,9},{25,1},{2,26},{10... | collective-permute-start | bytes 1572872 | tf_op jit(solution)/shard_map/ppermute | solution.py:622
  (80 other events, 984.3 us)
Sparse Core Ops, SparseCore 0:
  10.2 27.7 all-gather.4
  40.2 50.7 all-gather.8
  117.6 44.4 all-gather.10
  163.6 85.1 all-gather.6
  279.5 93.8 reduce-scatter.6
  375.6 53.3 reduce-scatter.4
  431.9 48.3 reduce-scatter.8
  519.1 37.9 reduce-scatter.10
